TPU v7x, 32 devices: a whole 2x2x4 slice. The times are simulated.
32 devices in a mesh: gx: 4 (over y, core), gy: 8 (over z, x).
Axes of the slice: x: 2, y: 2, z: 4, core: 2. Of those that a mesh axis runs over, the one named last changes fastest.
Arguments:
- orbitals: bfloat16 [56, 56, 29, 256], P('gx', 'gy'), may hold values from -6 to 6
- cell_matrices: bfloat16 [4, 8, 8, 512, 512], P('gx', 'gy'), may hold values from -0.09375 to 0.09375
- cell_nodes: int32 [4, 8, 8, 512], P('gx', 'gy'), may hold values from 0 to 3479, as said below
- projectors: bfloat16 [4, 8, 8, 16, 32, 512], P('gx', 'gy'), may hold values from -0.125 to 0.125
- entry_atom: int32 [4, 8, 8, 16], P('gx', 'gy'), may hold values from 0 to 1023, as said below
- coupling: float32 [1024, 32, 32], P(('gx', 'gy')), may hold values from -0.75 to 0.75
- proj_counts: int32 [1024], P(('gx', 'gy')), may hold values from 8 to 32
Outputs:
- filtered: bfloat16 [56, 56, 29, 256], P('gx', 'gy')
Inputs may be any that keep to these rules, and one draw needn't show every extreme that they name: `cell_nodes`: values index the device's extended node grid of (15) x (8) x (29) nodes, first index slowest; local cell c = i * 4 + l (with j = 0, since each device has one cell along the second direction) names each node of its block of (8) cubed nodes starting at (7 * i, 7 * j, 7 * l) once, in a drawn order. `entry_atom`: atom a is homed on device a // 32, devices numbered over gx and gy with gx slowest. The entries of one device name atoms of any one home device at most 8 times, and exactly 8 times for some home device.
All inputs are finite; a program needn't handle non-finite values.
Results may differ from a plain program's by a relative error of at most 0.0095.
Values may be sent and summed in bfloat16 or wider, within the bound.
No kernel may reach another device: no remote copies, remote signals or barrier semaphores. Data moves between devices by JAX's collectives and lax.ppermute only.
A program may use at most 128 MiB of HBM per device.

v0:
```python
import jax
import jax.numpy as jnp
from jax import lax
from jax.sharding import PartitionSpec as P

FILTER_DEGREE = 3


def passed_along(x, axis, by):
    count = lax.axis_size(axis)
    return lax.ppermute(x, axis, [(i, (i + by) % count) for i in range(count)])


def ghosts_in(owned):
    row_next = passed_along(owned[0:1], "gx", -1)
    widened = jnp.concatenate([owned, row_next], axis=0)
    column_next = passed_along(widened[:, 0:1], "gy", -1)
    return jnp.concatenate([widened, column_next], axis=1)


def settle(total):
    span_x = total.shape[0] - 1
    span_y = total.shape[1] - 1
    carried = passed_along(total[:, span_y:], "gy", 1)
    narrowed = total[:, :span_y].at[:, 0:1].add(carried)
    carried_row = passed_along(narrowed[span_x:], "gx", 1)
    return narrowed[:span_x].at[0:1].add(carried_row)


def send_out(outgoing):
    arrived = lax.all_to_all(outgoing, ("gx", "gy"), split_axis=0, concat_axis=0, tiled=True)
    return arrived


def send_back(replies):
    arrived = lax.all_to_all(replies, ("gx", "gy"), split_axis=0, concat_axis=0, tiled=True)
    return arrived


def on_device(orbitals, cell_matrices, cell_nodes, projectors, entry_atom, coupling, proj_counts):
    span_x, span_y, layers, breadth = orbitals.shape
    matrices = cell_matrices[0, 0]
    node_map = cell_nodes[0, 0]
    shapes = projectors[0, 0]
    atom_names = entry_atom[0, 0]
    cells, per_cell = atom_names.shape
    per_atom = shapes.shape[2]
    entries = cells * per_cell
    devices = lax.axis_size("gx") * lax.axis_size("gy")
    slots = max(2, 2 * entries // devices)
    home_atoms = coupling.shape[0]
    buffer_rows = devices * slots
    flat_atoms = atom_names.reshape(entries)
    homes = flat_atoms // home_atoms
    entry_order = jnp.arange(entries, dtype=jnp.int32)
    earlier = (homes[:, None] == homes[None, :]) & (entry_order[None, :] < entry_order[:, None])
    placed = homes * slots + jnp.sum(earlier.astype(jnp.int32), axis=1)
    sent_ids = jnp.full((buffer_rows,), -1, jnp.int32).at[placed].set(flat_atoms % home_atoms)
    got_ids = lax.all_to_all(sent_ids, ("gx", "gy"), split_axis=0, concat_axis=0, tiled=True)
    members = (got_ids[None, :] == jnp.arange(home_atoms, dtype=jnp.int32)[:, None]).astype(
        jnp.bfloat16
    )
    active = (jnp.arange(per_atom, dtype=jnp.int32)[None, :] < proj_counts[:, None]).astype(
        jnp.float32
    )
    flat_nodes = node_map.reshape(-1)
    extended_rows = (span_x + 1) * (span_y + 1) * layers

    def operate(extended):
        table = extended.reshape(extended_rows, breadth)
        local = table[node_map]
        projected = jnp.einsum(
            "ckpn,cno->ckpo", shapes, local, preferred_element_type=jnp.float32
        ).astype(jnp.bfloat16)
        outgoing = (
            jnp.zeros((buffer_rows, per_atom, breadth), jnp.bfloat16)
            .at[placed]
            .set(projected.reshape(entries, per_atom, breadth))
        )
        incoming = send_out(outgoing)
        summed = jnp.dot(
            members,
            incoming.reshape(buffer_rows, per_atom * breadth),
            preferred_element_type=jnp.float32,
        )
        summed = summed.reshape(home_atoms, per_atom, breadth)
        mixed = jnp.einsum(
            "apq,aqo->apo", coupling, active[:, :, None] * summed, precision=lax.Precision.HIGHEST
        )
        weighted = (active[:, :, None] * mixed).astype(jnp.bfloat16)
        replies = jnp.dot(
            members.T,
            weighted.reshape(home_atoms, per_atom * breadth),
            preferred_element_type=jnp.float32,
        )
        replies = replies.astype(jnp.bfloat16).reshape(buffer_rows, per_atom, breadth)
        answers = send_back(replies)
        returned = answers[placed].reshape(cells, per_cell, per_atom, breadth)
        result = jnp.einsum("cmn,cno->cmo", matrices, local, preferred_element_type=jnp.float32)
        result = result + jnp.einsum(
            "ckpn,ckpo->cno", shapes, returned, preferred_element_type=jnp.float32
        )
        total = (
            jnp.zeros((extended_rows, breadth), jnp.float32)
            .at[flat_nodes]
            .add(result.reshape(-1, breadth))
        )
        return total.reshape(span_x + 1, span_y + 1, layers, breadth)

    previous = orbitals.astype(jnp.float32)
    current = settle(operate(ghosts_in(orbitals)))
    for _ in range(FILTER_DEGREE - 1):
        following = 2.0 * settle(operate(ghosts_in(current.astype(jnp.bfloat16)))) - previous
        previous, current = (current, following)
    filtered = current.astype(jnp.bfloat16)
    return filtered


def solution(mesh):
    in_specs = (
        P("gx", "gy", None, None),
        P("gx", "gy", None, None, None),
        P("gx", "gy", None, None),
        P("gx", "gy", None, None, None, None),
        P("gx", "gy", None, None),
        P(("gx", "gy"), None, None),
        P(("gx", "gy")),
    )
    out_specs = P("gx", "gy", None, None)
    return jax.shard_map(
        on_device, mesh=mesh, in_specs=in_specs, out_specs=out_specs, check_vma=False
    )
```

profile of v0, /device:TPU:0, one launch (start us, length us, event | category | flops | bytes accessed | tf_op | source)
XLA Modules:
  0.0 1027.0 jit_solution(12321182024736901083)
XLA Ops:
  3.5 7.3 all-to-all-start
  30.2 16.9 %gather_fusion = bf16[4096,256]{1,0:T(8,128)(2,1)} fusion(bf16[3480,256]{1,0:T(8,128)(2,1)S(1)} %reshape.489, s32[4096]{0:T(1024)S(1)} %broadcast_clamp_fusion), kind=kCustom, calls=%fused_computation | custom fusion | bytes 4210688 | tf_op jit(solution)/shard_map/gather | solution.py:71
  53.7 15.7 %scatter_fusion = bf16[256,32,256]{2,1,0:T(8,128)(2,1)} fusion(bf16[256,32,256]{2,1,0:T(8,128)(2,1)} %broadcast.297.clone, s32[128]{0:T(128)S(1)} %fusion.82, bf16[128,32,256]{2,1,0:T(8,128)(2,1)S(1)} %bitcast.184), kind=kCustom, calls=%fused_computation.7 | custom fusion | bytes 6291968 | tf_op jit(solution)/shard_map/scatter | solution.py:78
  76.5 93.6 %all-to-all-done.1 = bf16[256,32,256]{2,1,0:T(8,128)(2,1)} async-done(((bf16[256,32,256]{2,1,0:T(8,128)(2,1)}), bf16[256,32,256]{2,1,0:T(8,128)(2,1)}, u32[]{:S(2)}, u32[]{:S(2)}) %all-to-all-start.1) | async-done | bytes 4194336 | tf_op jit(solution)/shard_map/all_to_all | solution.py:31
  170.1 7.6 copy.65
  192.1 94.9 %all-to-all-done.2 = bf16[256,32,256]{2,1,0:T(8,128)(2,1)} async-done(((bf16[256,32,256]{2,1,0:T(8,128)(2,1)}), bf16[256,32,256]{2,1,0:T(8,128)(2,1)}, u32[]{:S(2)}, u32[]{:S(2)}) %all-to-all-start.2) | async-done | bytes 4194336 | tf_op jit(solution)/shard_map/all_to_all | solution.py:36
  302.8 24.8 %scatter_custom_fusion.2 = f32[3480,256]{1,0:T(8,128)} fusion(s32[4096]{0:T(1024)S(1)} %bitcast.197, f32[4096,256]{1,0:T(8,128)} %bitcast.181, f32[]{:T(128)} %constant.165.clone.1), kind=kCustom, calls=%fused_computation.58 | custom fusion | flops 1048576 | bytes 3564032 | tf_op jit(solution)/shard_map/scatter-add | solution.py:106
  333.7 15.6 %collective-permute-done.2 = f32[15,1,29,256]{3,2,1,0:T(8,128)S(1)} collective-permute-done((f32[15,1,29,256]{3,2,1,0:T(8,128)S(1)}, f32[15,1,29,256]{3,2,1,0:T(8,128)S(1)}, u32[]{:S(2)}, u32[]{:S(2)}) %collective-permute-start.2) | collective-permute-done | bytes 445472 | tf_op jit(solution)/shard_map/ppermute | solution.py:11
  357.7 8.4 collective-permute-done.5
  370.2 17.0 %gather_fusion.2 = bf16[4096,256]{1,0:T(8,128)(2,1)} fusion(bf16[3480,256]{1,0:T(8,128)(2,1)S(1)} %reshape.497, s32[4096]{0:T(1024)S(1)} %broadcast_clamp_fusion), kind=kCustom, calls=%fused_computation.2 | custom fusion | bytes 4210688 | tf_op jit(solution)/shard_map/gather | solution.py:71
  393.8 15.7 %scatter_fusion.1 = bf16[256,32,256]{2,1,0:T(8,128)(2,1)} fusion(bf16[256,32,256]{2,1,0:T(8,128)(2,1)} %broadcast.297.clone.1, s32[128]{0:T(128)S(1)} %fusion.82, bf16[128,32,256]{2,1,0:T(8,128)(2,1)S(1)} %bitcast.185), kind=kCustom, calls=%fused_computation.9 | custom fusion | bytes 6291968 | tf_op jit(solution)/shard_map/scatter | solution.py:78
  409.5 98.9 %all_to_all.39 = bf16[256,32,256]{2,1,0:T(8,128)(2,1)} all-to-all(bf16[256,32,256]{2,1,0:T(8,128)(2,1)} %scatter_fusion.1), channel_id=1, replica_groups=mesh['gx'=4,'gy'=8] {'gx','gy'}, dimensions={0} | all-to-all | bytes 8388608 | tf_op jit(solution)/shard_map/all_to_all | solution.py:31
  508.4 7.6 copy.66
  524.2 97.3 %all_to_all.40 = bf16[256,32,256]{2,1,0:T(8,128)(2,1)} all-to-all(bf16[256,32,256]{2,1,0:T(8,128)(2,1)S(1)} %bitcast.172), channel_id=1, replica_groups=mesh['gx'=4,'gy'=8] {'gx','gy'}, dimensions={0} | all-to-all | bytes 8388608 | tf_op jit(solution)/shard_map/all_to_all | solution.py:36
  637.2 24.8 %scatter_custom_fusion.4 = f32[3480,256]{1,0:T(8,128)} fusion(s32[4096]{0:T(1024)S(1)} %bitcast.198, f32[4096,256]{1,0:T(8,128)} %bitcast.182, f32[]{:T(128)} %constant.165.clone.1), kind=kCustom, calls=%fused_computation.56 | custom fusion | flops 1048576 | bytes 3564032 | tf_op jit(solution)/shard_map/scatter-add | solution.py:106
  669.1 14.8 %collective-permute-done.6 = f32[15,1,29,256]{3,2,1,0:T(8,128)S(1)} collective-permute-done((f32[15,1,29,256]{3,2,1,0:T(8,128)S(1)}, f32[15,1,29,256]{3,2,1,0:T(8,128)S(1)}, u32[]{:S(2)}, u32[]{:S(2)}) %collective-permute-start.6) | collective-permute-done | bytes 445472 | tf_op jit(solution)/shard_map/ppermute | solution.py:11
  692.8 8.4 collective-permute-done.9
  705.3 17.0 %gather_fusion.4 = bf16[4096,256]{1,0:T(8,128)(2,1)} fusion(bf16[3480,256]{1,0:T(8,128)(2,1)S(1)} %reshape.505, s32[4096]{0:T(1024)S(1)} %broadcast_clamp_fusion), kind=kCustom, calls=%fused_computation.4 | custom fusion | bytes 4210688 | tf_op jit(solution)/shard_map/gather | solution.py:71
  728.8 15.7 %scatter_fusion.2 = bf16[256,32,256]{2,1,0:T(8,128)(2,1)} fusion(bf16[256,32,256]{2,1,0:T(8,128)(2,1)} %broadcast.297, s32[128]{0:T(128)S(1)} %fusion.82, bf16[128,32,256]{2,1,0:T(8,128)(2,1)S(1)} %bitcast.183), kind=kCustom, calls=%fused_computation.11 | custom fusion | bytes 6291968 | tf_op jit(solution)/shard_map/scatter | solution.py:78
  744.6 98.8 %all_to_all.41 = bf16[256,32,256]{2,1,0:T(8,128)(2,1)} all-to-all(bf16[256,32,256]{2,1,0:T(8,128)(2,1)} %scatter_fusion.2), channel_id=1, replica_groups=mesh['gx'=4,'gy'=8] {'gx','gy'}, dimensions={0} | all-to-all | bytes 8388608 | tf_op jit(solution)/shard_map/all_to_all | solution.py:31
  843.3 7.6 copy.67
  859.1 97.6 %all_to_all.42 = bf16[256,32,256]{2,1,0:T(8,128)(2,1)} all-to-all(bf16[256,32,256]{2,1,0:T(8,128)(2,1)S(1)} %bitcast.173), channel_id=1, replica_groups=mesh['gx'=4,'gy'=8] {'gx','gy'}, dimensions={0} | all-to-all | bytes 8388608 | tf_op jit(solution)/shard_map/all_to_all | solution.py:36
  972.4 24.8 %scatter_custom_fusion.6 = f32[3480,256]{1,0:T(8,128)} fusion(s32[4096]{0:T(1024)S(1)} %bitcast.199, f32[4096,256]{1,0:T(8,128)} %bitcast.180, f32[]{:T(128)} %constant.165.clone.1), kind=kCustom, calls=%fused_computation.54 | custom fusion | flops 1048576 | bytes 3564032 | tf_op jit(solution)/shard_map/scatter-add | solution.py:106
  1004.1 14.8 %collective-permute-done.10 = f32[15,1,29,256]{3,2,1,0:T(8,128)S(1)} collective-permute-done((f32[15,1,29,256]{3,2,1,0:T(8,128)S(1)}, f32[15,1,29,256]{3,2,1,0:T(8,128)S(1)}, u32[]{:S(2)}, u32[]{:S(2)}) %collective-permute-start.10) | collective-permute-done | bytes 445472 | tf_op jit(solution)/shard_map/ppermute | solution.py:11
  (144 shorter events, 180.3 us)
Async XLA Ops:
  0.0 181.2 %copy-start = (f32[32,32,32]{2,1,0:T(8,128)S(1)}, f32[32,32,32]{2,1,0:T(8,128)}, u32[]{:S(2)}) copy-start(f32[32,32,32]{2,1,0:T(8,128)} %param.24) | copy-start | bytes 393220
  3.5 65.9 %all-to-all-start = ((s32[32,8,1]{1,2,0:T(1,128)}), s32[32,8,1]{1,2,0:T(1,128)S(1)}, u32[]{:S(2)}, u32[]{:S(2)}) async-start(s32[32,8,1]{1,2,0:T(1,128)} %bitcast.6), calls=%async_computation | async-start | bytes 32768 | tf_op jit(solution)/shard_map/all_to_all | solution.py:59
  11.7 3.9 collective-permute-start
  15.7 10.4 %collective-permute-start.1 = (bf16[15,1,29,256]{3,2,1,0:T(8,128)(2,1)S(1)}, bf16[15,1,29,256]{3,2,1,0:T(8,128)(2,1)S(1)}, u32[]{:S(2)}, u32[]{:S(2)}) collective-permute-start(bf16[15,1,29,256]{3,2,1,0:T(8,128)(2,1)S(1)} %slice.270), channel_id=1, source_target_pairs={{0,7},{1,0},{2,1},{3,2},{4,3},{5,4},{6,5},{7,6},{8,15},{9,8},{10,9... | collective-permute-start | bytes 668168 | tf_op jit(solution)/shard_map/ppermute | solution.py:11
  69.4 5.7 copy-start.14
  69.4 100.7 %all-to-all-start.1 = ((bf16[256,32,256]{2,1,0:T(8,128)(2,1)}), bf16[256,32,256]{2,1,0:T(8,128)(2,1)}, u32[]{:S(2)}, u32[]{:S(2)}) async-start(bf16[256,32,256]{2,1,0:T(8,128)(2,1)} %scatter_fusion), calls=%async_computation.1 | async-start | bytes 8388608 | tf_op jit(solution)/shard_map/all_to_all | solution.py:31
  187.8 99.2 %all-to-all-start.2 = ((bf16[256,32,256]{2,1,0:T(8,128)(2,1)}), bf16[256,32,256]{2,1,0:T(8,128)(2,1)}, u32[]{:S(2)}, u32[]{:S(2)}) async-start(bf16[256,32,256]{2,1,0:T(8,128)(2,1)} %bitcast.168), calls=%async_computation.2 | async-start | bytes 8388608 | tf_op jit(solution)/shard_map/all_to_all | solution.py:36
  332.4 16.9 %copy-start.6 = (f32[15,8,29,256]{3,2,1,0:T(8,128)S(1)}, f32[15,8,29,256]{3,2,1,0:T(8,128)}, u32[]{:S(2)}) copy-start(f32[15,8,29,256]{3,2,1,0:T(8,128)} %reshape.496) | copy-start | bytes 10690564
  333.6 15.6 %slice-start = ((f32[15,8,29,256]{3,2,1,0:T(8,128)}), f32[15,7,29,256]{3,2,1,0:T(8,128)S(1)}, s32[]{:S(2)}) async-start(f32[15,8,29,256]{3,2,1,0:T(8,128)} %reshape.496), calls=%async_computation.7 | async-start | bytes 6881280 | tf_op jit(solution)/shard_map/slice | solution.py:25
  333.6 15.6 %collective-permute-start.2 = (f32[15,1,29,256]{3,2,1,0:T(8,128)S(1)}, f32[15,1,29,256]{3,2,1,0:T(8,128)S(1)}, u32[]{:S(2)}, u32[]{:S(2)}) collective-permute-start(f32[15,1,29,256]{3,2,1,0:T(8,128)S(1)} %slice.273), channel_id=1, source_target_pairs={{0,1},{1,2},{2,3},{3,4},{4,5},{5,6},{6,7},{7,0},{8,9},{9,10},{10,1... | collective-permute-start | bytes 1336328 | tf_op jit(solution)/shard_map/ppermute | solution.py:11
  349.4 5.5 collective-permute-start.3
  355.2 2.4 collective-permute-start.4
  357.6 8.4 collective-permute-start.5
  666.9 17.1 %copy-start.7 = (f32[15,8,29,256]{3,2,1,0:T(8,128)S(1)}, f32[15,8,29,256]{3,2,1,0:T(8,128)}, u32[]{:S(2)}) copy-start(f32[15,8,29,256]{3,2,1,0:T(8,128)} %reshape.504) | copy-start | bytes 10690564
  668.1 15.9 %slice-start.1 = ((f32[15,8,29,256]{3,2,1,0:T(8,128)}), f32[15,7,29,256]{3,2,1,0:T(8,128)S(1)}, s32[]{:S(2)}) async-start(f32[15,8,29,256]{3,2,1,0:T(8,128)} %reshape.504), calls=%async_computation.8 | async-start | bytes 6881280 | tf_op jit(solution)/shard_map/slice | solution.py:25
  668.1 15.8 %collective-permute-start.6 = (f32[15,1,29,256]{3,2,1,0:T(8,128)S(1)}, f32[15,1,29,256]{3,2,1,0:T(8,128)S(1)}, u32[]{:S(2)}, u32[]{:S(2)}) collective-permute-start(f32[15,1,29,256]{3,2,1,0:T(8,128)S(1)} %slice.280), channel_id=1, source_target_pairs={{0,1},{1,2},{2,3},{3,4},{4,5},{5,6},{6,7},{7,0},{8,9},{9,10},{10,1... | collective-permute-start | bytes 1336328 | tf_op jit(solution)/shard_map/ppermute | solution.py:11
  684.0 5.5 copy-start.12
  684.1 5.5 collective-permute-start.7
  690.2 2.4 collective-permute-start.8
  692.7 8.4 collective-permute-start.9
  1002.0 16.9 %copy-start.8 = (f32[15,8,29,256]{3,2,1,0:T(8,128)S(1)}, f32[15,8,29,256]{3,2,1,0:T(8,128)}, u32[]{:S(2)}) copy-start(f32[15,8,29,256]{3,2,1,0:T(8,128)} %reshape.512) | copy-start | bytes 10690564
  1003.2 15.6 %slice-start.2 = ((f32[15,8,29,256]{3,2,1,0:T(8,128)}), f32[15,7,29,256]{3,2,1,0:T(8,128)S(1)}, s32[]{:S(2)}) async-start(f32[15,8,29,256]{3,2,1,0:T(8,128)} %reshape.512), calls=%async_computation.9 | async-start | bytes 6881280 | tf_op jit(solution)/shard_map/slice | solution.py:25
  1003.2 15.6 %collective-permute-start.10 = (f32[15,1,29,256]{3,2,1,0:T(8,128)S(1)}, f32[15,1,29,256]{3,2,1,0:T(8,128)S(1)}, u32[]{:S(2)}, u32[]{:S(2)}) collective-permute-start(f32[15,1,29,256]{3,2,1,0:T(8,128)S(1)} %slice.287), channel_id=1, source_target_pairs={{0,1},{1,2},{2,3},{3,4},{4,5},{5,6},{6,7},{7,0},{8,9},{9,10},{10,1... | collective-permute-start | bytes 1336328 | tf_op jit(solution)/shard_map/ppermute | solution.py:11
  1019.0 5.5 collective-permute-start.11
  (9 other events, 35.8 us)
where the time goes:
time: 1040 us; the launch traced here: 1030 us
  blocking collectives  393 us (38%)
  waiting for transfers between devices  277 us (27%)
  local copies, waits for them, and re-layouts  195 us (19%)
  other arithmetic  83.9 us (8%)
  matrix products  52.5 us (5%)
  starting transfers between devices  25.2 us (2%)
    all_to_all x2, blocking collectives, send_out(): lax.all_to_all(outgoing, ('gx', 'gy'), split_axis=0, concat_axis=0, tiled...  198 us
    all_to_all x2, blocking collectives, send_back(): lax.all_to_all(replies, ('gx', 'gy'), split_axis=0, concat_axis=0, tiled=...  195 us
    all_to_all x1, waiting for transfers between devices, send_back(): lax.all_to_all(replies, ('gx', 'gy'), split_axis=0, concat_axis=0, tiled=...  94.9 us
    all_to_all x1, waiting for transfers between devices, send_out(): lax.all_to_all(outgoing, ('gx', 'gy'), split_axis=0, concat_axis=0, tiled...  93.6 us
    ppermute x12, waiting for transfers between devices, passed_along(): return lax.ppermute(x, axis, [(i, (i + by) % count) for i in range(count)])  88.1 us
    scatter-add x3, other arithmetic, operate(): total = jnp.zeros((extended_rows, breadth), jnp.float32).at[flat_nodes].a...  74.4 us
    gather x3, local copies, waits for them, and re-layouts, operate(): local = table[node_map]  50.8 us
    scatter x3, local copies, waits for them, and re-layouts, operate(): outgoing = jnp.zeros((buffer_rows, per_atom, breadth), jnp.bfloat16).at[p...  47.2 us
  transfers between devices with their start and end apart: 15, of which 14 were waited for; matrix products, arithmetic and copies ran while one was open for 5% of the time, Pallas kernels for 0%

commit v1 on v0

v1 whole, which is shorter than its diff:
```python
import itertools

import jax
import jax.numpy as jnp
from jax import lax
from jax.experimental import pallas as pl
from jax.experimental.pallas import tpu as pltpu
from jax.sharding import PartitionSpec as P

FILTER_DEGREE = 3
STREAMS = 1
GROUP = 8
BF16 = jnp.bfloat16
F32 = jnp.float32


def shifted(x, axes, by):
    sizes = [lax.axis_size(a) for a in axes]
    pairs = []
    for place in itertools.product(*[range(s) for s in sizes]):
        source = 0
        target = 0
        for at, step, size in zip(place, by, sizes):
            source = source * size + at
            target = target * size + (at + step) % size
        pairs.append((source, target))
    return lax.ppermute(x, axes if len(axes) > 1 else axes[0], pairs)


def whole(shape):
    return pl.BlockSpec(shape, lambda c: (0,) * len(shape), pipeline_mode=pl.Buffered(1))


def smem():
    return pl.BlockSpec(memory_space=pltpu.SMEM)


def canonical(places, matrices, shapes):
    cells, nodes = places.shape
    rows = shapes.shape[1]

    def body(place_ref, matrix_ref, shape_ref, joint_ref, straight_ref):
        spots = lax.broadcasted_iota(jnp.int32, (nodes, nodes), 0)
        pick = (spots == place_ref[0]).astype(BF16)
        last = (((1,), (1,)), ((), ()))
        half = jnp.dot(pick, matrix_ref[0], preferred_element_type=F32).astype(BF16)
        joint_ref[0, :, :nodes] = lax.dot_general(
            half, pick, last, preferred_element_type=F32
        ).astype(BF16)
        joint_ref[0, :, nodes:] = lax.dot_general(
            pick, shape_ref[0], last, preferred_element_type=F32
        ).astype(BF16)
        straight_ref[0] = lax.dot_general(
            shape_ref[0], pick, last, preferred_element_type=F32
        ).astype(BF16)

    return pl.pallas_call(
        body,
        grid=(cells,),
        in_specs=[
            pl.BlockSpec((1, 1, nodes), lambda c: (c, 0, 0)),
            pl.BlockSpec((1, nodes, nodes), lambda c: (c, 0, 0)),
            pl.BlockSpec((1, rows, nodes), lambda c: (c, 0, 0)),
        ],
        out_specs=[
            pl.BlockSpec((1, nodes, nodes + rows), lambda c: (c, 0, 0)),
            pl.BlockSpec((1, rows, nodes), lambda c: (c, 0, 0)),
        ],
        out_shape=[
            jax.ShapeDtypeStruct((cells, nodes, nodes + rows), BF16),
            jax.ShapeDtypeStruct((cells, rows, nodes), BF16),
        ],
        name="canonical",
    )(places.reshape(cells, 1, nodes), matrices, shapes)


def project(field, straight, placed, slots, cz, per_atom):
    cells, rows, nodes = straight.shape
    side = field.shape[2]
    deg = side - 1
    breadth = field.shape[3]
    per_cell = rows // per_atom

    def body(placed_ref, field_ref, straight_ref, local_ref, out_ref):
        c = pl.program_id(0)
        u = c // cz * deg
        w = c % cz * deg
        block = field_ref[pl.ds(u, side), pl.ds(w, side)]
        local = block.reshape(nodes, breadth).astype(BF16)
        local_ref[0] = local
        values = jnp.dot(straight_ref[0], local, preferred_element_type=F32).astype(BF16)
        for k in range(per_cell):
            out_ref[placed_ref[c * per_cell + k]] = values[k * per_atom : (k + 1) * per_atom]

    return pl.pallas_call(
        body,
        grid=(cells,),
        in_specs=[
            smem(),
            whole(field.shape),
            pl.BlockSpec((1, rows, nodes), lambda c: (c, 0, 0)),
        ],
        out_specs=[
            pl.BlockSpec((1, nodes, breadth), lambda c: (c, 0, 0)),
            whole((slots, per_atom, breadth)),
        ],
        out_shape=[
            jax.ShapeDtypeStruct((cells, nodes, breadth), BF16),
            jax.ShapeDtypeStruct((slots, per_atom, breadth), BF16),
        ],
        name="project",
    )(placed, field, straight)


def merge(incoming, ids, filled, atoms):
    slots, per_atom, breadth = incoming.shape
    senders = filled.shape[0]
    each = slots // senders

    def body(ids_ref, filled_ref, incoming_ref, sums_ref, sent_ref):
        sums_ref[...] = jnp.zeros_like(sums_ref)
        for g in range(senders):

            def add(j, carry):
                slot = g * each + j
                atom = ids_ref[slot]
                sums_ref[atom] = sums_ref[atom] + incoming_ref[slot].astype(F32)
                return carry

            lax.fori_loop(0, filled_ref[g], add, 0)
        sent_ref[...] = sums_ref[...].astype(BF16)

    return pl.pallas_call(
        body,
        in_specs=[smem(), smem(), pl.BlockSpec(memory_space=pltpu.VMEM)],
        out_specs=[pl.BlockSpec(memory_space=pltpu.VMEM)] * 2,
        out_shape=[
            jax.ShapeDtypeStruct((atoms, per_atom, breadth), F32),
            jax.ShapeDtypeStruct((atoms, per_atom, breadth), BF16),
        ],
        name="merge",
    )(ids, filled, incoming)


def couple(sums, others, high, low, ids, filled, slots):
    atoms, per_atom, breadth = sums.shape
    groups, edge, _ = high.shape
    members = atoms // groups
    senders = filled.shape[0]
    each = slots // senders

    def body(ids_ref, filled_ref, sums_ref, others_ref, high_ref, low_ref, out_ref, kept_ref):
        for g in range(groups):
            part = pl.ds(g * members, members)
            total = sums_ref[part] + others_ref[part].astype(F32)
            total = total.reshape(edge, breadth)
            upper = total.astype(BF16)
            lower = (total - upper.astype(F32)).astype(BF16)
            mixed = jnp.dot(high_ref[g], upper, preferred_element_type=F32)
            mixed = mixed + jnp.dot(low_ref[g], upper, preferred_element_type=F32)
            mixed = mixed + jnp.dot(high_ref[g], lower, preferred_element_type=F32)
            kept_ref[part] = mixed.astype(BF16).reshape(members, per_atom, breadth)
        for g in range(senders):

            def copy(j, carry):
                slot = g * each + j
                out_ref[slot] = kept_ref[ids_ref[slot]]
                return carry

            lax.fori_loop(0, filled_ref[g], copy, 0)

    vmem = pl.BlockSpec(memory_space=pltpu.VMEM)
    return pl.pallas_call(
        body,
        in_specs=[smem(), smem(), vmem, vmem, vmem, vmem],
        out_specs=vmem,
        out_shape=jax.ShapeDtypeStruct((slots, per_atom, breadth), BF16),
        scratch_shapes=[pltpu.VMEM((atoms, per_atom, breadth), BF16)],
        name="couple",
    )(ids, filled, sums, others, high, low)


def apply(joint, local, answers, placed, extended, cz):
    cells, nodes, columns = joint.shape
    slots, per_atom, breadth = answers.shape
    rows = columns - nodes
    per_cell = rows // per_atom
    side = extended[2]
    deg = side - 1

    def body(placed_ref, joint_ref, local_ref, answers_ref, total_ref, stack_ref):
        c = pl.program_id(0)

        @pl.when(c == 0)
        def _():
            total_ref[...] = jnp.zeros_like(total_ref)

        stack_ref[:nodes] = local_ref[0]
        for k in range(per_cell):
            at = nodes + k * per_atom
            stack_ref[at : at + per_atom] = answers_ref[placed_ref[c * per_cell + k]]
        result = jnp.dot(joint_ref[0], stack_ref[...], preferred_element_type=F32)
        u = pl.ds(c // cz * deg, side)
        w = pl.ds(c % cz * deg, side)
        total_ref[u, w] = total_ref[u, w] + result.reshape(side, side, side, breadth)

    shape = extended + (breadth,)
    return pl.pallas_call(
        body,
        grid=(cells,),
        in_specs=[
            smem(),
            pl.BlockSpec((1, nodes, columns), lambda c: (c, 0, 0)),
            pl.BlockSpec((1, nodes, breadth), lambda c: (c, 0, 0)),
            whole(answers.shape),
        ],
        out_specs=whole(shape),
        out_shape=jax.ShapeDtypeStruct(shape, F32),
        scratch_shapes=[pltpu.VMEM((columns, breadth), BF16)],
        name="apply",
    )(placed, joint, local, answers)


def completed(total):
    low_u, high_u = total[:1], total[-1:]
    low_v, high_v = total[:, :, :1], total[:, :, -1:]

    def moved(x, axes, by):
        return shifted(x.astype(BF16), axes, by).astype(F32)

    both = ("gx", "gy")
    from_next_u = moved(low_u, ("gx",), (-1,))
    from_prev_u = moved(high_u, ("gx",), (1,))
    from_next_v = moved(low_v, ("gy",), (-1,))
    from_prev_v = moved(high_v, ("gy",), (1,))
    corner_nn = moved(low_u[:, :, :1], both, (-1, -1))
    corner_np = moved(low_u[:, :, -1:], both, (-1, 1))
    corner_pn = moved(high_u[:, :, :1], both, (1, -1))
    corner_pp = moved(high_u[:, :, -1:], both, (1, 1))
    span_u, _, span_v, _ = total.shape
    rest_v = ((0, 0), (0, 0), (1, span_v - 2), (0, 0))

    def at_ends(first, last, axis):
        shape = list(total.shape)
        shape[axis] = total.shape[axis] - 2
        for other in range(4):
            if other != axis:
                shape[other] = first.shape[other]
        return jnp.concatenate([first, jnp.zeros(shape, F32), last], axis=axis)

    first_row = from_prev_u + at_ends(corner_pp, corner_pn, 2)
    last_row = from_next_u + at_ends(corner_np, corner_nn, 2)
    return total + at_ends(first_row, last_row, 0) + at_ends(from_prev_v, from_next_v, 2)


def on_device(orbitals, cell_matrices, cell_nodes, projectors, entry_atom, coupling, proj_counts):
    span_x, span_y, layers, _ = orbitals.shape
    matrices = cell_matrices[0, 0]
    node_map = cell_nodes[0, 0]
    cells, per_cell, per_atom, nodes = projectors.shape[2:]
    shapes = projectors[0, 0].reshape(cells, per_cell * per_atom, nodes)
    atom_names = entry_atom[0, 0]
    side = round(nodes ** (1 / 3))
    deg = side - 1
    cz = (layers - 1) // deg
    assert span_y == deg and side**3 == nodes and cells * deg == span_x * cz
    entries = cells * per_cell
    n_gx, n_gy = lax.axis_size("gx"), lax.axis_size("gy")
    devices = n_gx * n_gy
    half = n_gy // 2
    senders = devices // 2
    home_atoms = coupling.shape[0]
    atoms = 2 * home_atoms
    each = 2 * max(2, 2 * entries // devices)
    slots = senders * each
    both = ("gx", "gy")
    teams = [
        [p * n_gy + h * half + r for p in range(n_gx) for r in range(half)] for h in range(2)
    ]

    def exchange(x):
        return lax.all_to_all(
            x, both, split_axis=0, concat_axis=0, axis_index_groups=teams, tiled=True
        )

    flat = atom_names.reshape(entries)
    homes = flat // home_atoms
    homes_y = homes % n_gy
    collectors = homes // n_gy * half + homes_y % half
    inner = homes_y // half * home_atoms + flat % home_atoms
    order = jnp.arange(entries, dtype=jnp.int32)
    earlier = (collectors[:, None] == collectors[None, :]) & (order[None, :] < order[:, None])
    placed = collectors * each + jnp.sum(earlier.astype(jnp.int32), axis=1)
    named = placed[None, :] == jnp.arange(slots, dtype=jnp.int32)[:, None]
    sent_ids = jnp.sum(jnp.where(named, inner[None, :] + 1, 0), axis=1) - 1
    ids = exchange(sent_ids.reshape(senders, each))
    filled = jnp.sum((ids >= 0).astype(jnp.int32), axis=1)
    ids = ids.reshape(slots)

    active = (jnp.arange(per_atom, dtype=jnp.int32)[None, :] < proj_counts[:, None]).astype(F32)
    masked = coupling * active[:, :, None] * active[:, None, :]
    partner = shifted(masked, ("gy",), (half,))
    upper_half = lax.axis_index("gy") >= half
    mixers = jnp.where(
        upper_half,
        jnp.concatenate([partner, masked], axis=0),
        jnp.concatenate([masked, partner], axis=0),
    )
    mixers = mixers.reshape(atoms // GROUP, GROUP, per_atom, 1, per_atom)
    own = jnp.eye(GROUP, dtype=F32)[None, :, None, :, None]
    mixers = (mixers * own).reshape(atoms // GROUP, GROUP * per_atom, GROUP * per_atom)
    mix_high = mixers.astype(BF16)
    mix_low = (mixers - mix_high.astype(F32)).astype(BF16)

    cell_ids = jnp.arange(cells, dtype=jnp.int32)[:, None]
    node_w = node_map % layers - cell_ids % cz * deg
    node_v = node_map // layers % (span_y + 1)
    node_u = node_map // (layers * (span_y + 1)) - cell_ids // cz * deg
    places = (node_u * side + node_w) * side + node_v
    joint, straight = canonical(places, matrices, shapes)

    row_next = shifted(orbitals[:1], ("gx",), (-1,))
    column_next = shifted(orbitals[:, :1], ("gy",), (-1,))
    corner_next = shifted(orbitals[:1, :1], both, (-1, -1))
    widened = jnp.concatenate(
        [
            jnp.concatenate([orbitals, column_next], axis=1),
            jnp.concatenate([row_next, corner_next], axis=1),
        ],
        axis=0,
    )
    grid = jnp.transpose(widened, (0, 2, 1, 3)).astype(F32)
    extended = grid.shape[:3]

    def operate(field):
        local, outgoing = project(field, straight, placed, slots, cz, per_atom)
        incoming = exchange(outgoing)
        sums, sent = merge(incoming, ids, filled, atoms)
        others = shifted(sent, ("gy",), (half,))
        replies = couple(sums, others, mix_high, mix_low, ids, filled, slots)
        answers = exchange(replies)
        return completed(apply(joint, local, answers, placed, extended, cz))

    width = grid.shape[3] // STREAMS
    results = []
    for s in range(STREAMS):
        previous = grid[..., s * width : (s + 1) * width]
        current = operate(previous)
        for _ in range(FILTER_DEGREE - 1):
            previous, current = (current, 2.0 * operate(current) - previous)
        results.append(current[:span_x, :, :span_y].astype(BF16))
    filtered = jnp.concatenate(results, axis=-1) if STREAMS > 1 else results[0]
    return jnp.transpose(filtered, (0, 2, 1, 3))


def solution(mesh):
    in_specs = (
        P("gx", "gy", None, None),
        P("gx", "gy", None, None, None),
        P("gx", "gy", None, None),
        P("gx", "gy", None, None, None, None),
        P("gx", "gy", None, None),
        P(("gx", "gy"), None, None),
        P(("gx", "gy")),
    )
    out_specs = P("gx", "gy", None, None)
    return jax.shard_map(
        on_device, mesh=mesh, in_specs=in_specs, out_specs=out_specs, check_vma=False
    )
```

time: 1040 us -> 770 us (0.74); the launches traced: 1030 us -> 768 us
  blocking collectives: 393 us -> 160 us
  local copies, waits for them, and re-layouts: 195 us -> 22.6 us
  Pallas kernels: 0 us -> 109 us
  waiting for transfers between devices: 277 us -> 367 us
  other arithmetic: 83.9 us -> 28.7 us
  starting transfers between devices: 25.2 us -> 79.4 us
  matrix products: 52.5 us -> 0 us
    all_to_all x4 -> x3, blocking collectives: 393 us -> 160 us  [exchange(): lax.all_to_all(x, both, split_axis=0, concat_axis=0, axis_index_groups=te...]
    ppermute x12 -> x31, waiting for transfers between devices: 88.1 us -> 213 us  [shifted(): return lax.ppermute(x, axes if len(axes) > 1 else axes[0], pairs)]
    pallas_call x0 -> x13, Pallas kernels: none -> 109 us  [the longest x3 33 us: apply(): pl.pallas_call(body, grid=(cells,), in_specs=[smem(), pl.BlockSpec((1, no...]
    scatter-add x9 -> x0, other arithmetic: 74.7 us -> none  [the longest x3 74.4 us: operate(): total = jnp.zeros((extended_rows, breadth), jnp.float32).at[flat_nodes].a...]
    gather x6 -> x0, local copies, waits for them, and re-layouts: 59.4 us -> none  [the longest x3 50.8 us: operate(): local = table[node_map]]
    dot_general x18 -> x0, matrix products: 52.5 us -> none  [the longest x3 12.2 us: operate(): jnp.einsum('ckpn,cno->ckpo', shapes, local, preferred_element_type=jnp.fl...]
    ppermute x12 -> x31, starting transfers between devices: 8.1 us -> 59.3 us  [shifted(): return lax.ppermute(x, axes if len(axes) > 1 else axes[0], pairs)]
    scatter x4 -> x0, local copies, waits for them, and re-layouts: 48.2 us -> none  [the longest x3 47.2 us: operate(): outgoing = jnp.zeros((buffer_rows, per_atom, breadth), jnp.bfloat16).at[p...]
  transfers between devices with their start and end apart: 15 -> 35, of which waited for: 14 -> 12; matrix products, arithmetic and copies ran while one was open for 5% -> 4% of each run, Pallas kernels for 0% -> 3%
where the time goes in v1:
time: 770 us; the launch traced here: 768 us
  waiting for transfers between devices  367 us (48%)
  blocking collectives  160 us (21%)
  Pallas kernels  109 us (14%)
  starting transfers between devices  79.4 us (10%)
  other arithmetic  28.7 us (4%)
  local copies, waits for them, and re-layouts  22.6 us (3%)
    ppermute x31, waiting for transfers between devices, shifted(): return lax.ppermute(x, axes if len(axes) > 1 else axes[0], pairs)  213 us
    all_to_all x3, blocking collectives, exchange(): lax.all_to_all(x, both, split_axis=0, concat_axis=0, axis_index_groups=te...  160 us
    all_to_all x4, waiting for transfers between devices, exchange(): lax.all_to_all(x, both, split_axis=0, concat_axis=0, axis_index_groups=te...  155 us
    ppermute x31, starting transfers between devices, shifted(): return lax.ppermute(x, axes if len(axes) > 1 else axes[0], pairs)  59.3 us
    pallas_call x3, Pallas kernels, apply(): pl.pallas_call(body, grid=(cells,), in_specs=[smem(), pl.BlockSpec((1, no...  33 us
    pallas_call x3, Pallas kernels, project(): pl.pallas_call(body, grid=(cells,), in_specs=[smem(), whole(field.shape),...  28.3 us
    all_to_all x4, starting transfers between devices, exchange(): lax.all_to_all(x, both, split_axis=0, concat_axis=0, axis_index_groups=te...  20.2 us
    pallas_call x3, Pallas kernels, couple(): pl.pallas_call(body, in_specs=[smem(), smem(), vmem, vmem, vmem, vmem], o...  19.2 us
  transfers between devices with their start and end apart: 35, of which 12 were waited for; matrix products, arithmetic and copies ran while one was open for 4% of the time, Pallas kernels for 3%

profile of v1, /device:TPU:0, one launch (start us, length us, event | category | flops | bytes accessed | tf_op | source)
XLA Modules:
  0.0 768.2 jit_solution(13110437844892080133)
XLA Ops:
  1.8 6.3 all-to-all-start
  18.5 13.2 %canonical.1 = (bf16[8,512,1024]{2,1,0:T(8,128)(2,1)}, bf16[8,512,512]{2,1,0:T(8,128)(2,1)}) custom-call(s32[8,1,512]{2,1,0:T(1,128)} %fusion.10.place_ref, bf16[8,512,512]{2,1,0:T(8,128)(2,1)} %bitcast.37, bf16[8,512,512]{2,1,0:T(8,128)(2,1)} %bitcast.38), custom_call_target="tpu_custom_call" | custom-call | tf_op jit(solution)/shard_map/canonical/pallas_call | solution.py:57
  34.3 9.4 %project.3 = (bf16[8,512,256]{2,1,0:T(8,128)(2,1)}, bf16[256,32,256]{2,1,0:T(8,128)(2,1)}) custom-call(s32[128]{0:T(128)} %copy-done.12, f32[15,29,8,256]{3,2,1,0:T(8,128)} %convert_bitcast_fusion.field_ref, bf16[8,512,512]{2,1,0:T(8,128)(2,1)} %get-tuple-element.20.straight_ref), custom_call_target="tpu_custom_call" | custom-call | tf_op jit(solution)/shard_map/project/pallas_call | solution.py:95
  50.8 50.0 %all-to-all-done.1.incoming_ref = bf16[256,32,256]{2,1,0:T(8,128)(2,1)} async-done(((bf16[256,32,256]{2,1,0:T(8,128)(2,1)}), bf16[256,32,256]{2,1,0:T(8,128)(2,1)}, u32[]{:S(2)}, u32[]{:S(2)}) %all-to-all-start.1) | async-done | bytes 4194336 | tf_op jit(solution)/shard_map/all_to_all | solution.py:282
  109.8 67.0 %collective-permute-done.4 = f32[32,32,32]{2,1,0:T(8,128)} collective-permute-done((f32[32,32,32]{2,1,0:T(8,128)S(1)}, f32[32,32,32]{2,1,0:T(8,128)}, u32[]{:S(2)}, u32[]{:S(2)}) %collective-permute-start.4) | collective-permute-done | bytes 131104 | tf_op jit(solution)/shard_map/ppermute | solution.py:27
  182.1 7.0 mul.127
  192.5 6.3 couple.3
  203.6 52.4 %all-to-all-done.2.answers_ref = bf16[256,32,256]{2,1,0:T(8,128)(2,1)} async-done(((bf16[256,32,256]{2,1,0:T(8,128)(2,1)}), bf16[256,32,256]{2,1,0:T(8,128)(2,1)}, u32[]{:S(2)}, u32[]{:S(2)}) %all-to-all-start.2) | async-done | bytes 4194336 | tf_op jit(solution)/shard_map/all_to_all | solution.py:282
  256.0 11.0 %apply.3 = f32[15,29,8,256]{3,2,1,0:T(8,128)} custom-call(s32[128]{0:T(128)} %copy-done.12, bf16[8,512,1024]{2,1,0:T(8,128)(2,1)} %get-tuple-element.19.joint_ref, bf16[8,512,256]{2,1,0:T(8,128)(2,1)} %get-tuple-element.21.local_ref, bf16[256,32,256]{2,1,0:T(8,128)(2,1)} %all-to-all-done.2.answers_ref), custom_call_target="tpu_custom_call" | custom-call | tf_op jit(solution)/shard_map/apply/pallas_call | solution.py:208
  286.9 13.7 %collective-permute-done.11 = bf16[15,29,1,256]{3,2,1,0:T(2,128)(2,1)S(1)} collective-permute-done((bf16[15,29,1,256]{3,2,1,0:T(2,128)(2,1)S(1)}, bf16[15,29,1,256]{3,2,1,0:T(2,128)(2,1)S(1)}, u32[]{:S(2)}, u32[]{:S(2)}) %collective-permute-start.11) | collective-permute-done | bytes 222752 | tf_op jit(solution)/shard_map/ppermute | solution.py:27
  306.8 9.4 %project.4 = (bf16[8,512,256]{2,1,0:T(8,128)(2,1)}, bf16[256,32,256]{2,1,0:T(8,128)(2,1)}) custom-call(s32[128]{0:T(128)} %copy-done.12, f32[15,29,8,256]{3,2,1,0:T(8,128)} %fusion.field_ref, bf16[8,512,512]{2,1,0:T(8,128)(2,1)} %get-tuple-element.20.straight_ref), custom_call_target="tpu_custom_call" | custom-call | tf_op jit(solution)/shard_map/project/pallas_call | solution.py:95
  316.3 53.4 %all_to_all.36.incoming_ref = bf16[256,32,256]{2,1,0:T(8,128)(2,1)} all-to-all(bf16[256,32,256]{2,1,0:T(8,128)(2,1)} %get-tuple-element.26), channel_id=1, replica_groups={{0,1,2,3,8,9,10,11,16,17,18,19,24,25,26,27},{4,5,6,7,12,13,14,15,20,21,..., dimensions={0} | all-to-all | bytes 8388608 | tf_op jit(solution)/shard_map/all_to_all | solution.py:282
  374.8 48.8 %collective-permute-done.13.others_ref = bf16[64,32,256]{2,1,0:T(8,128)(2,1)S(1)} collective-permute-done((bf16[64,32,256]{2,1,0:T(8,128)(2,1)}, bf16[64,32,256]{2,1,0:T(8,128)(2,1)S(1)}, u32[]{:S(2)}, u32[]{:S(2)}) %collective-permute-start.13) | collective-permute-done | bytes 1048608 | tf_op jit(solution)/shard_map/ppermute | solution.py:27
  424.6 6.3 couple.4
  431.0 53.4 %all_to_all.37.answers_ref = bf16[256,32,256]{2,1,0:T(8,128)(2,1)} all-to-all(bf16[256,32,256]{2,1,0:T(8,128)(2,1)} %couple.4), channel_id=1, replica_groups={{0,1,2,3,8,9,10,11,16,17,18,19,24,25,26,27},{4,5,6,7,12,13,14,15,20,21,..., dimensions={0} | all-to-all | bytes 8388608 | tf_op jit(solution)/shard_map/all_to_all | solution.py:282
  484.4 11.0 %apply.4 = f32[15,29,8,256]{3,2,1,0:T(8,128)} custom-call(s32[128]{0:T(128)} %copy-done.12, bf16[8,512,1024]{2,1,0:T(8,128)(2,1)} %get-tuple-element.19.joint_ref, bf16[8,512,256]{2,1,0:T(8,128)(2,1)} %get-tuple-element.25.local_ref, bf16[256,32,256]{2,1,0:T(8,128)(2,1)} %all_to_all.37.answers_ref), custom_call_target="tpu_custom_call" | custom-call | tf_op jit(solution)/shard_map/apply/pallas_call | solution.py:208
  515.1 13.2 %collective-permute-done.20 = bf16[15,29,1,256]{3,2,1,0:T(2,128)(2,1)S(1)} collective-permute-done((bf16[15,29,1,256]{3,2,1,0:T(2,128)(2,1)S(1)}, bf16[15,29,1,256]{3,2,1,0:T(2,128)(2,1)S(1)}, u32[]{:S(2)}, u32[]{:S(2)}) %collective-permute-start.20) | collective-permute-done | bytes 222752 | tf_op jit(solution)/shard_map/ppermute | solution.py:27
  535.7 9.4 %project.5 = (bf16[8,512,256]{2,1,0:T(8,128)(2,1)}, bf16[256,32,256]{2,1,0:T(8,128)(2,1)}) custom-call(s32[128]{0:T(128)} %copy-done.12, f32[15,29,8,256]{3,2,1,0:T(8,128)} %fusion.3.field_ref, bf16[8,512,512]{2,1,0:T(8,128)(2,1)} %get-tuple-element.20.straight_ref), custom_call_target="tpu_custom_call" | custom-call | tf_op jit(solution)/shard_map/project/pallas_call | solution.py:95
  545.1 53.4 %all_to_all.38.incoming_ref = bf16[256,32,256]{2,1,0:T(8,128)(2,1)} all-to-all(bf16[256,32,256]{2,1,0:T(8,128)(2,1)} %get-tuple-element.30), channel_id=1, replica_groups={{0,1,2,3,8,9,10,11,16,17,18,19,24,25,26,27},{4,5,6,7,12,13,14,15,20,21,..., dimensions={0} | all-to-all | bytes 8388608 | tf_op jit(solution)/shard_map/all_to_all | solution.py:282
  603.6 48.8 %collective-permute-done.22.others_ref = bf16[64,32,256]{2,1,0:T(8,128)(2,1)S(1)} collective-permute-done((bf16[64,32,256]{2,1,0:T(8,128)(2,1)}, bf16[64,32,256]{2,1,0:T(8,128)(2,1)S(1)}, u32[]{:S(2)}, u32[]{:S(2)}) %collective-permute-start.22) | collective-permute-done | bytes 1048608 | tf_op jit(solution)/shard_map/ppermute | solution.py:27
  653.5 6.5 couple.5
  664.8 52.2 %all-to-all-done.6.answers_ref = bf16[256,32,256]{2,1,0:T(8,128)(2,1)} async-done(((bf16[256,32,256]{2,1,0:T(8,128)(2,1)}), bf16[256,32,256]{2,1,0:T(8,128)(2,1)}, u32[]{:S(2)}, u32[]{:S(2)}) %all-to-all-start.6) | async-done | bytes 4194336 | tf_op jit(solution)/shard_map/all_to_all | solution.py:282
  717.0 11.0 %apply.5 = f32[15,29,8,256]{3,2,1,0:T(8,128)} custom-call(s32[128]{0:T(128)} %copy-done.12, bf16[8,512,1024]{2,1,0:T(8,128)(2,1)} %get-tuple-element.19.joint_ref, bf16[8,512,256]{2,1,0:T(8,128)(2,1)} %get-tuple-element.29.local_ref, bf16[256,32,256]{2,1,0:T(8,128)(2,1)} %all-to-all-done.6.answers_ref), custom_call_target="tpu_custom_call" | custom-call | tf_op jit(solution)/shard_map/apply/pallas_call | solution.py:208
  748.1 13.4 %collective-permute-done.29 = bf16[15,29,1,256]{3,2,1,0:T(2,128)(2,1)S(1)} collective-permute-done((bf16[15,29,1,256]{3,2,1,0:T(2,128)(2,1)S(1)}, bf16[15,29,1,256]{3,2,1,0:T(2,128)(2,1)S(1)}, u32[]{:S(2)}, u32[]{:S(2)}) %collective-permute-start.29) | collective-permute-done | bytes 222752 | tf_op jit(solution)/shard_map/ppermute | solution.py:27
  (163 shorter events, 140.7 us)
Async XLA Ops:
  1.8 41.9 %all-to-all-start = ((s32[16,1,16]{2,1,0:T(1,128)}), s32[16,1,16]{2,1,0:T(1,128)S(1)}, u32[]{:S(2)}, u32[]{:S(2)}) async-start(s32[16,1,16]{2,1,0:T(1,128)} %sub.84), calls=%async_computation | async-start | bytes 16384 | tf_op jit(solution)/shard_map/all_to_all | solution.py:282
  10.6 21.1 %collective-permute-start.2 = (bf16[1,1,29,256]{3,1,2,0:T(2,128)(2,1)S(1)}, bf16[1,1,29,256]{3,1,2,0:T(2,128)(2,1)S(1)}, u32[]{:S(2)}, u32[]{:S(2)}) collective-permute-start(bf16[1,1,29,256]{3,1,2,0:T(2,128)(2,1)S(1)} %slice.151), channel_id=1, source_target_pairs={{0,31},{1,24},{2,25},{3,26},{4,27},{5,28},{6,29},{7,30},{8,7},{9,0... | collective-permute-start | bytes 44552 | tf_op jit(solution)/shard_map/ppermute | solution.py:27
  16.2 15.6 %collective-permute-start.1 = (bf16[1,7,29,256]{3,1,2,0:T(8,128)(2,1)S(1)}, bf16[1,7,29,256]{3,1,2,0:T(8,128)(2,1)S(1)}, u32[]{:S(2)}, u32[]{:S(2)}) collective-permute-start(bf16[1,7,29,256]{3,1,2,0:T(8,128)(2,1)S(1)} %slice.150), channel_id=1, source_target_pairs={{0,24},{8,0},{16,8},{24,16},{1,25},{9,1},{17,9},{25,17},{2,26},{10... | collective-permute-start | bytes 311816 | tf_op jit(solution)/shard_map/ppermute | solution.py:27
  17.0 14.7 %collective-permute-start = (bf16[14,1,29,256]{3,1,2,0:T(2,128)(2,1)S(1)}, bf16[14,1,29,256]{3,1,2,0:T(2,128)(2,1)S(1)}, u32[]{:S(2)}, u32[]{:S(2)}) collective-permute-start(bf16[14,1,29,256]{3,1,2,0:T(2,128)(2,1)S(1)} %slice.149), channel_id=1, source_target_pairs={{0,7},{1,0},{2,1},{3,2},{4,3},{5,4},{6,5},{7,6},{8,15},{9,8},{10,9... | collective-permute-start | bytes 623624 | tf_op jit(solution)/shard_map/ppermute | solution.py:27
  43.8 57.1 %all-to-all-start.1 = ((bf16[256,32,256]{2,1,0:T(8,128)(2,1)}), bf16[256,32,256]{2,1,0:T(8,128)(2,1)}, u32[]{:S(2)}, u32[]{:S(2)}) async-start(bf16[256,32,256]{2,1,0:T(8,128)(2,1)} %get-tuple-element.22), calls=%async_computation.1 | async-start | bytes 8388608 | tf_op jit(solution)/shard_map/all_to_all | solution.py:282
  106.0 86.5 %collective-permute-start.3 = (bf16[64,32,256]{2,1,0:T(8,128)(2,1)}, bf16[64,32,256]{2,1,0:T(8,128)(2,1)}, u32[]{:S(2)}, u32[]{:S(2)}) collective-permute-start(bf16[64,32,256]{2,1,0:T(8,128)(2,1)} %get-tuple-element.24), channel_id=1, source_target_pairs={{0,4},{1,5},{2,6},{3,7},{4,0},{5,1},{6,2},{7,3},{8,12},{9,13},{10,... | collective-permute-start | bytes 3145736 | tf_op jit(solution)/shard_map/ppermute | solution.py:27
  106.3 70.4 %collective-permute-start.4 = (f32[32,32,32]{2,1,0:T(8,128)S(1)}, f32[32,32,32]{2,1,0:T(8,128)}, u32[]{:S(2)}, u32[]{:S(2)}) collective-permute-start(f32[32,32,32]{2,1,0:T(8,128)S(1)} %multiply_multiply_fusion), channel_id=1, source_target_pairs={{0,4},{1,5},{2,6},{3,7},{4,0},{5,1},{6,2},{7,3},{8,12},{9,13},{10,... | collective-permute-start | bytes 393224 | tf_op jit(solution)/shard_map/ppermute | solution.py:27
  198.9 57.1 %all-to-all-start.2 = ((bf16[256,32,256]{2,1,0:T(8,128)(2,1)}), bf16[256,32,256]{2,1,0:T(8,128)(2,1)}, u32[]{:S(2)}, u32[]{:S(2)}) async-start(bf16[256,32,256]{2,1,0:T(8,128)(2,1)} %couple.3), calls=%async_computation.2 | async-start | bytes 8388608 | tf_op jit(solution)/shard_map/all_to_all | solution.py:282
  269.3 12.2 %collective-permute-start.10 = (bf16[1,29,1,256]{3,2,1,0:T(2,128)(2,1)S(1)}, bf16[1,29,1,256]{3,2,1,0:T(2,128)(2,1)S(1)}, u32[]{:S(2)}, u32[]{:S(2)}) collective-permute-start(bf16[1,29,1,256]{3,2,1,0:T(2,128)(2,1)S(1)} %get-tuple-element.62), channel_id=1, source_target_pairs={{0,31},{1,24},{2,25},{3,26},{4,27},{5,28},{6,29},{7,30},{8,7},{9,0... | collective-permute-start | bytes 44552 | tf_op jit(solution)/shard_map/ppermute | solution.py:27
  274.7 11.9 %collective-permute-start.7 = (bf16[1,29,1,256]{3,2,1,0:T(2,128)(2,1)S(1)}, bf16[1,29,1,256]{3,2,1,0:T(2,128)(2,1)S(1)}, u32[]{:S(2)}, u32[]{:S(2)}) collective-permute-start(bf16[1,29,1,256]{3,2,1,0:T(2,128)(2,1)S(1)} %get-tuple-element.64), channel_id=1, source_target_pairs={{0,15},{1,8},{2,9},{3,10},{4,11},{5,12},{6,13},{7,14},{8,23},{9,16... | collective-permute-start | bytes 44552 | tf_op jit(solution)/shard_map/ppermute | solution.py:27
  281.5 19.0 %collective-permute-start.11 = (bf16[15,29,1,256]{3,2,1,0:T(2,128)(2,1)S(1)}, bf16[15,29,1,256]{3,2,1,0:T(2,128)(2,1)S(1)}, u32[]{:S(2)}, u32[]{:S(2)}) collective-permute-start(bf16[15,29,1,256]{3,2,1,0:T(2,128)(2,1)S(1)} %get-tuple-element.57), channel_id=1, source_target_pairs={{0,1},{1,2},{2,3},{3,4},{4,5},{5,6},{6,7},{7,0},{8,9},{9,10},{10,1... | collective-permute-start | bytes 668168 | tf_op jit(solution)/shard_map/ppermute | solution.py:27
  281.6 21.8 %collective-permute-start.12 = (bf16[15,29,1,256]{3,2,1,0:T(2,128)(2,1)S(1)}, bf16[15,29,1,256]{3,2,1,0:T(2,128)(2,1)S(1)}, u32[]{:S(2)}, u32[]{:S(2)}) collective-permute-start(bf16[15,29,1,256]{3,2,1,0:T(2,128)(2,1)S(1)} %get-tuple-element.58), channel_id=1, source_target_pairs={{0,7},{1,0},{2,1},{3,2},{4,3},{5,4},{6,5},{7,6},{8,15},{9,8},{10,9... | collective-permute-start | bytes 668168 | tf_op jit(solution)/shard_map/ppermute | solution.py:27
  374.8 48.9 %collective-permute-start.13 = (bf16[64,32,256]{2,1,0:T(8,128)(2,1)}, bf16[64,32,256]{2,1,0:T(8,128)(2,1)S(1)}, u32[]{:S(2)}, u32[]{:S(2)}) collective-permute-start(bf16[64,32,256]{2,1,0:T(8,128)(2,1)} %get-tuple-element.28), channel_id=1, source_target_pairs={{0,4},{1,5},{2,6},{3,7},{4,0},{5,1},{6,2},{7,3},{8,12},{9,13},{10,... | collective-permute-start | bytes 3145736 | tf_op jit(solution)/shard_map/ppermute | solution.py:27
  497.7 10.2 %collective-permute-start.15 = (bf16[1,29,1,256]{3,2,1,0:T(2,128)(2,1)S(1)}, bf16[1,29,1,256]{3,2,1,0:T(2,128)(2,1)S(1)}, u32[]{:S(2)}, u32[]{:S(2)}) collective-permute-start(bf16[1,29,1,256]{3,2,1,0:T(2,128)(2,1)S(1)} %get-tuple-element.53), channel_id=1, source_target_pairs={{0,9},{1,10},{2,11},{3,12},{4,13},{5,14},{6,15},{7,8},{8,17},{9,18... | collective-permute-start | bytes 44552 | tf_op jit(solution)/shard_map/ppermute | solution.py:27
  498.4 11.6 %collective-permute-start.19 = (bf16[1,29,1,256]{3,2,1,0:T(2,128)(2,1)S(1)}, bf16[1,29,1,256]{3,2,1,0:T(2,128)(2,1)S(1)}, u32[]{:S(2)}, u32[]{:S(2)}) collective-permute-start(bf16[1,29,1,256]{3,2,1,0:T(2,128)(2,1)S(1)} %get-tuple-element.54), channel_id=1, source_target_pairs={{0,31},{1,24},{2,25},{3,26},{4,27},{5,28},{6,29},{7,30},{8,7},{9,0... | collective-permute-start | bytes 44552 | tf_op jit(solution)/shard_map/ppermute | solution.py:27
  503.1 11.7 %collective-permute-start.16 = (bf16[1,29,1,256]{3,2,1,0:T(2,128)(2,1)S(1)}, bf16[1,29,1,256]{3,2,1,0:T(2,128)(2,1)S(1)}, u32[]{:S(2)}, u32[]{:S(2)}) collective-permute-start(bf16[1,29,1,256]{3,2,1,0:T(2,128)(2,1)S(1)} %get-tuple-element.56), channel_id=1, source_target_pairs={{0,15},{1,8},{2,9},{3,10},{4,11},{5,12},{6,13},{7,14},{8,23},{9,16... | collective-permute-start | bytes 44552 | tf_op jit(solution)/shard_map/ppermute | solution.py:27
  510.0 18.4 %collective-permute-start.20 = (bf16[15,29,1,256]{3,2,1,0:T(2,128)(2,1)S(1)}, bf16[15,29,1,256]{3,2,1,0:T(2,128)(2,1)S(1)}, u32[]{:S(2)}, u32[]{:S(2)}) collective-permute-start(bf16[15,29,1,256]{3,2,1,0:T(2,128)(2,1)S(1)} %get-tuple-element.49), channel_id=1, source_target_pairs={{0,1},{1,2},{2,3},{3,4},{4,5},{5,6},{6,7},{7,0},{8,9},{9,10},{10,1... | collective-permute-start | bytes 668168 | tf_op jit(solution)/shard_map/ppermute | solution.py:27
  510.1 21.6 %collective-permute-start.21 = (bf16[15,29,1,256]{3,2,1,0:T(2,128)(2,1)S(1)}, bf16[15,29,1,256]{3,2,1,0:T(2,128)(2,1)S(1)}, u32[]{:S(2)}, u32[]{:S(2)}) collective-permute-start(bf16[15,29,1,256]{3,2,1,0:T(2,128)(2,1)S(1)} %get-tuple-element.50), channel_id=1, source_target_pairs={{0,7},{1,0},{2,1},{3,2},{4,3},{5,4},{6,5},{7,6},{8,15},{9,8},{10,9... | collective-permute-start | bytes 668168 | tf_op jit(solution)/shard_map/ppermute | solution.py:27
  603.6 48.9 %collective-permute-start.22 = (bf16[64,32,256]{2,1,0:T(8,128)(2,1)}, bf16[64,32,256]{2,1,0:T(8,128)(2,1)S(1)}, u32[]{:S(2)}, u32[]{:S(2)}) collective-permute-start(bf16[64,32,256]{2,1,0:T(8,128)(2,1)} %get-tuple-element.32), channel_id=1, source_target_pairs={{0,4},{1,5},{2,6},{3,7},{4,0},{5,1},{6,2},{7,3},{8,12},{9,13},{10,... | collective-permute-start | bytes 3145736 | tf_op jit(solution)/shard_map/ppermute | solution.py:27
  659.9 57.1 %all-to-all-start.6 = ((bf16[256,32,256]{2,1,0:T(8,128)(2,1)}), bf16[256,32,256]{2,1,0:T(8,128)(2,1)}, u32[]{:S(2)}, u32[]{:S(2)}) async-start(bf16[256,32,256]{2,1,0:T(8,128)(2,1)} %couple.5), calls=%async_computation.6 | async-start | bytes 8388608 | tf_op jit(solution)/shard_map/all_to_all | solution.py:282
  730.4 12.2 %collective-permute-start.28 = (bf16[1,29,1,256]{3,2,1,0:T(2,128)(2,1)S(1)}, bf16[1,29,1,256]{3,2,1,0:T(2,128)(2,1)S(1)}, u32[]{:S(2)}, u32[]{:S(2)}) collective-permute-start(bf16[1,29,1,256]{3,2,1,0:T(2,128)(2,1)S(1)} %get-tuple-element.44), channel_id=1, source_target_pairs={{0,31},{1,24},{2,25},{3,26},{4,27},{5,28},{6,29},{7,30},{8,7},{9,0... | collective-permute-start | bytes 44552 | tf_op jit(solution)/shard_map/ppermute | solution.py:27
  735.8 11.7 %collective-permute-start.25 = (bf16[1,29,1,256]{3,2,1,0:T(2,128)(2,1)S(1)}, bf16[1,29,1,256]{3,2,1,0:T(2,128)(2,1)S(1)}, u32[]{:S(2)}, u32[]{:S(2)}) collective-permute-start(bf16[1,29,1,256]{3,2,1,0:T(2,128)(2,1)S(1)} %get-tuple-element.46), channel_id=1, source_target_pairs={{0,15},{1,8},{2,9},{3,10},{4,11},{5,12},{6,13},{7,14},{8,23},{9,16... | collective-permute-start | bytes 44552 | tf_op jit(solution)/shard_map/ppermute | solution.py:27
  742.6 18.9 %collective-permute-start.29 = (bf16[15,29,1,256]{3,2,1,0:T(2,128)(2,1)S(1)}, bf16[15,29,1,256]{3,2,1,0:T(2,128)(2,1)S(1)}, u32[]{:S(2)}, u32[]{:S(2)}) collective-permute-start(bf16[15,29,1,256]{3,2,1,0:T(2,128)(2,1)S(1)} %get-tuple-element.47), channel_id=1, source_target_pairs={{0,1},{1,2},{2,3},{3,4},{4,5},{5,6},{6,7},{7,0},{8,9},{9,10},{10,1... | collective-permute-start | bytes 668168 | tf_op jit(solution)/shard_map/ppermute | solution.py:27
  742.7 21.7 %collective-permute-start.30 = (bf16[15,29,1,256]{3,2,1,0:T(2,128)(2,1)S(1)}, bf16[15,29,1,256]{3,2,1,0:T(2,128)(2,1)S(1)}, u32[]{:S(2)}, u32[]{:S(2)}) collective-permute-start(bf16[15,29,1,256]{3,2,1,0:T(2,128)(2,1)S(1)} %get-tuple-element.48), channel_id=1, source_target_pairs={{0,7},{1,0},{2,1},{3,2},{4,3},{5,4},{6,5},{7,6},{8,15},{9,8},{10,9... | collective-permute-start | bytes 668168 | tf_op jit(solution)/shard_map/ppermute | solution.py:27
  (25 other events, 458.5 us)

commit v2 on v1

v2 whole, which is shorter than its diff:
```python
import itertools

import jax
import jax.numpy as jnp
from jax import lax
from jax.experimental import pallas as pl
from jax.experimental.pallas import tpu as pltpu
from jax.sharding import PartitionSpec as P


FILTER_DEGREE = 3
PARTS = 2
GRANT = 20 * 1024 * 1024
GROUP = 8
BF16 = jnp.bfloat16
F32 = jnp.float32


def shifted(x, axes, by):
    sizes = [lax.axis_size(a) for a in axes]
    pairs = []
    for place in itertools.product(*[range(s) for s in sizes]):
        source = 0
        target = 0
        for at, step, size in zip(place, by, sizes):
            source = source * size + at
            target = target * size + (at + step) % size
        pairs.append((source, target))
    return lax.ppermute(x, axes if len(axes) > 1 else axes[0], pairs)


def whole(shape):
    return pl.BlockSpec(shape, lambda c: (0,) * len(shape), pipeline_mode=pl.Buffered(1))


def smem():
    return pl.BlockSpec(memory_space=pltpu.SMEM)


def unread(after):
    return [pl.BlockSpec(memory_space=pl.ANY)] * len(after)


def canonical(places, matrices, shapes):
    cells, nodes = places.shape
    rows = shapes.shape[1]

    def body(place_ref, matrix_ref, shape_ref, stiff_ref, turned_ref, straight_ref):
        spots = lax.broadcasted_iota(jnp.int32, (nodes, nodes), 0)
        pick = (spots == place_ref[0]).astype(BF16)
        last = (((1,), (1,)), ((), ()))
        half = jnp.dot(pick, matrix_ref[0], preferred_element_type=F32).astype(BF16)
        stiff_ref[0] = lax.dot_general(
            half, pick, last, preferred_element_type=F32
        ).astype(BF16)
        turned_ref[0] = lax.dot_general(
            pick, shape_ref[0], last, preferred_element_type=F32
        ).astype(BF16)
        straight_ref[0] = lax.dot_general(
            shape_ref[0], pick, last, preferred_element_type=F32
        ).astype(BF16)

    return pl.pallas_call(
        body,
        grid=(cells,),
        in_specs=[
            pl.BlockSpec((1, 1, nodes), lambda c: (c, 0, 0)),
            pl.BlockSpec((1, nodes, nodes), lambda c: (c, 0, 0)),
            pl.BlockSpec((1, rows, nodes), lambda c: (c, 0, 0)),
        ],
        out_specs=[
            pl.BlockSpec((1, nodes, nodes), lambda c: (c, 0, 0)),
            pl.BlockSpec((1, nodes, rows), lambda c: (c, 0, 0)),
            pl.BlockSpec((1, rows, nodes), lambda c: (c, 0, 0)),
        ],
        out_shape=[
            jax.ShapeDtypeStruct((cells, nodes, nodes), BF16),
            jax.ShapeDtypeStruct((cells, nodes, rows), BF16),
            jax.ShapeDtypeStruct((cells, rows, nodes), BF16),
        ],
        compiler_params=pltpu.CompilerParams(vmem_limit_bytes=GRANT),
        name="canonical",
    )(places.reshape(cells, 1, nodes), matrices, shapes)


def spread(mixers):
    atoms, per_atom, _ = mixers.shape
    groups = atoms // GROUP
    edge = GROUP * per_atom

    def body(mixers_ref, high_ref, low_ref):
        rows = lax.broadcasted_iota(jnp.int32, (edge, edge), 0) // per_atom
        columns = lax.broadcasted_iota(jnp.int32, (edge, edge), 1) // per_atom
        for g in range(groups):
            block = mixers_ref[g * GROUP : (g + 1) * GROUP].reshape(edge, per_atom)
            block = jnp.concatenate([block] * GROUP, axis=1)
            block = jnp.where(rows == columns, block, 0.0)
            high = block.astype(BF16)
            high_ref[g] = high
            low_ref[g] = (block - high.astype(F32)).astype(BF16)

    vmem = pl.BlockSpec(memory_space=pltpu.VMEM)
    return pl.pallas_call(
        body,
        in_specs=[vmem],
        out_specs=[vmem, vmem],
        out_shape=[jax.ShapeDtypeStruct((groups, edge, edge), BF16)] * 2,
        compiler_params=pltpu.CompilerParams(vmem_limit_bytes=GRANT),
        name="spread",
    )(mixers)


def project(field, straight, placed, slots, cz, per_atom):
    cells, rows, nodes = straight.shape
    side = field.shape[2]
    deg = side - 1
    breadth = field.shape[3]
    per_cell = rows // per_atom
    width = breadth // PARTS

    def body(placed_ref, field_ref, straight_ref, local_ref, *out_refs):
        c = pl.program_id(0)
        u = c // cz * deg
        w = c % cz * deg
        block = field_ref[pl.ds(u, side), pl.ds(w, side)]
        local = block.reshape(nodes, breadth).astype(BF16)
        local_ref[0] = local
        values = jnp.dot(straight_ref[0], local, preferred_element_type=F32).astype(BF16)
        for k in range(per_cell):
            slot = placed_ref[c * per_cell + k]
            for s, out_ref in enumerate(out_refs):
                out_ref[slot] = values[
                    k * per_atom : (k + 1) * per_atom, s * width : (s + 1) * width
                ]

    return pl.pallas_call(
        body,
        grid=(cells,),
        in_specs=[
            smem(),
            whole(field.shape),
            pl.BlockSpec((1, rows, nodes), lambda c: (c, 0, 0)),
        ],
        out_specs=[
            pl.BlockSpec((1, nodes, breadth), lambda c: (c, 0, 0)),
        ]
        + [whole((slots, per_atom, width))] * PARTS,
        out_shape=[
            jax.ShapeDtypeStruct((cells, nodes, breadth), BF16),
        ]
        + [jax.ShapeDtypeStruct((slots, per_atom, width), BF16)] * PARTS,
        compiler_params=pltpu.CompilerParams(vmem_limit_bytes=GRANT),
        name="project",
    )(placed, field, straight)


def stiffen(stiff, local, extended, cz):
    cells, nodes, _ = stiff.shape
    breadth = local.shape[2]
    side = extended[2]
    deg = side - 1

    def body(stiff_ref, local_ref, total_ref):
        c = pl.program_id(0)

        @pl.when(c == 0)
        def _():
            total_ref[...] = jnp.zeros_like(total_ref)

        result = jnp.dot(stiff_ref[0], local_ref[0], preferred_element_type=F32)
        u = pl.ds(c // cz * deg, side)
        w = pl.ds(c % cz * deg, side)
        total_ref[u, w] = total_ref[u, w] + result.reshape(side, side, side, breadth)

    shape = extended + (breadth,)
    return pl.pallas_call(
        body,
        grid=(cells,),
        in_specs=[
            pl.BlockSpec((1, nodes, nodes), lambda c: (c, 0, 0)),
            pl.BlockSpec((1, nodes, breadth), lambda c: (c, 0, 0)),
        ],
        out_specs=whole(shape),
        out_shape=jax.ShapeDtypeStruct(shape, F32),
        compiler_params=pltpu.CompilerParams(vmem_limit_bytes=GRANT),
        name="stiffen",
    )(stiff, local)


def merge(incoming, ids, filled, atoms, after):
    slots, per_atom, breadth = incoming.shape
    senders = filled.shape[0]
    each = slots // senders

    def body(ids_ref, filled_ref, incoming_ref, *refs):
        sums_ref, sent_ref = refs[len(after) :]
        sums_ref[...] = jnp.zeros_like(sums_ref)
        for g in range(senders):

            def add(j, carry):
                slot = g * each + j
                atom = ids_ref[slot]
                sums_ref[atom] = sums_ref[atom] + incoming_ref[slot].astype(F32)
                return carry

            lax.fori_loop(0, filled_ref[g], add, 0)
        sent_ref[...] = sums_ref[...].astype(BF16)

    return pl.pallas_call(
        body,
        in_specs=[smem(), smem(), pl.BlockSpec(memory_space=pltpu.VMEM)] + unread(after),
        out_specs=[pl.BlockSpec(memory_space=pltpu.VMEM)] * 2,
        out_shape=[
            jax.ShapeDtypeStruct((atoms, per_atom, breadth), F32),
            jax.ShapeDtypeStruct((atoms, per_atom, breadth), BF16),
        ],
        compiler_params=pltpu.CompilerParams(vmem_limit_bytes=GRANT),
        name="merge",
    )(ids, filled, incoming, *after)


def couple(sums, others, high, low, ids, filled, slots, after):
    atoms, per_atom, breadth = sums.shape
    groups, edge, _ = high.shape
    members = atoms // groups
    senders = filled.shape[0]
    each = slots // senders

    def body(ids_ref, filled_ref, sums_ref, others_ref, high_ref, low_ref, *refs):
        out_ref, kept_ref = refs[len(after) :]
        for g in range(groups):
            part = pl.ds(g * members, members)
            total = sums_ref[part] + others_ref[part].astype(F32)
            total = total.reshape(edge, breadth)
            upper = total.astype(BF16)
            lower = (total - upper.astype(F32)).astype(BF16)
            mixed = jnp.dot(high_ref[g], upper, preferred_element_type=F32)
            mixed = mixed + jnp.dot(low_ref[g], upper, preferred_element_type=F32)
            mixed = mixed + jnp.dot(high_ref[g], lower, preferred_element_type=F32)
            kept_ref[part] = mixed.astype(BF16).reshape(members, per_atom, breadth)
        for g in range(senders):

            def copy(j, carry):
                slot = g * each + j
                out_ref[slot] = kept_ref[ids_ref[slot]]
                return carry

            lax.fori_loop(0, filled_ref[g], copy, 0)

    vmem = pl.BlockSpec(memory_space=pltpu.VMEM)
    return pl.pallas_call(
        body,
        in_specs=[smem(), smem(), vmem, vmem, vmem, vmem] + unread(after),
        out_specs=vmem,
        out_shape=jax.ShapeDtypeStruct((slots, per_atom, breadth), BF16),
        scratch_shapes=[pltpu.VMEM((atoms, per_atom, breadth), BF16)],
        compiler_params=pltpu.CompilerParams(vmem_limit_bytes=GRANT),
        name="couple",
    )(ids, filled, sums, others, high, low, *after)


def apply(turned, answers, begun, placed, part, cz, after):
    cells, nodes, rows = turned.shape
    _, per_atom, breadth = answers.shape
    per_cell = rows // per_atom
    side = begun.shape[2]
    deg = side - 1

    def body(placed_ref, turned_ref, answers_ref, begun_ref, *refs):
        total_ref, stack_ref = refs[len(after) :]
        c = pl.program_id(0)

        @pl.when(c == 0)
        def _():
            total_ref[...] = begun_ref[...]

        for k in range(per_cell):
            at = k * per_atom
            stack_ref[at : at + per_atom] = answers_ref[placed_ref[c * per_cell + k]]
        result = jnp.dot(turned_ref[0], stack_ref[...], preferred_element_type=F32)
        u = pl.ds(c // cz * deg, side)
        w = pl.ds(c % cz * deg, side)
        total_ref[u, w] = total_ref[u, w] + result.reshape(side, side, side, breadth)

    shape = begun.shape[:3] + (breadth,)
    return pl.pallas_call(
        body,
        grid=(cells,),
        in_specs=[
            smem(),
            pl.BlockSpec((1, nodes, rows), lambda c: (c, 0, 0)),
            whole(answers.shape),
            pl.BlockSpec(shape, lambda c: (0, 0, 0, part), pipeline_mode=pl.Buffered(1)),
        ]
        + unread(after),
        out_specs=whole(shape),
        out_shape=jax.ShapeDtypeStruct(shape, F32),
        scratch_shapes=[pltpu.VMEM((rows, breadth), BF16)],
        compiler_params=pltpu.CompilerParams(vmem_limit_bytes=GRANT),
        name="apply",
    )(placed, turned, answers, begun, *after)


def completed(total):
    span_u, span_w, span_v, breadth = total.shape
    low_v = total[:, :, 0].astype(BF16)
    high_v = total[:, :, -1].astype(BF16)
    from_next = shifted(low_v, ("gy",), (-1,)).astype(F32)[:, :, None]
    from_prev = shifted(high_v, ("gy",), (1,)).astype(F32)[:, :, None]
    gap = jnp.zeros((span_u, span_w, span_v - 2, breadth), F32)
    total = total + jnp.concatenate([from_prev, gap, from_next], axis=2)
    low_u = total[0].astype(BF16)
    high_u = total[-1].astype(BF16)
    from_next = shifted(low_u, ("gx",), (-1,)).astype(F32)[None]
    from_prev = shifted(high_u, ("gx",), (1,)).astype(F32)[None]
    gap = jnp.zeros((span_u - 2, span_w, span_v, breadth), F32)
    return total + jnp.concatenate([from_prev, gap, from_next], axis=0)


def on_device(orbitals, cell_matrices, cell_nodes, projectors, entry_atom, coupling, proj_counts):
    span_x, span_y, layers, _ = orbitals.shape
    matrices = cell_matrices[0, 0]
    node_map = cell_nodes[0, 0]
    cells, per_cell, per_atom, nodes = projectors.shape[2:]
    shapes = projectors[0, 0].reshape(cells, per_cell * per_atom, nodes)
    atom_names = entry_atom[0, 0]
    side = round(nodes ** (1 / 3))
    deg = side - 1
    cz = (layers - 1) // deg
    assert span_y == deg and side**3 == nodes and cells * deg == span_x * cz
    entries = cells * per_cell
    n_gx, n_gy = lax.axis_size("gx"), lax.axis_size("gy")
    devices = n_gx * n_gy
    half = n_gy // 2
    senders = devices // 2
    home_atoms = coupling.shape[0]
    atoms = 2 * home_atoms
    each = 2 * max(2, 2 * entries // devices)
    slots = senders * each
    both = ("gx", "gy")
    teams = [
        [p * n_gy + h * half + r for p in range(n_gx) for r in range(half)] for h in range(2)
    ]

    def exchange(x):
        return lax.all_to_all(
            x, both, split_axis=0, concat_axis=0, axis_index_groups=teams, tiled=True
        )

    flat = atom_names.reshape(entries)
    homes = flat // home_atoms
    homes_y = homes % n_gy
    collectors = homes // n_gy * half + homes_y % half
    inner = homes_y // half * home_atoms + flat % home_atoms
    order = jnp.arange(entries, dtype=jnp.int32)
    earlier = (collectors[:, None] == collectors[None, :]) & (order[None, :] < order[:, None])
    placed = collectors * each + jnp.sum(earlier.astype(jnp.int32), axis=1)
    named = placed[None, :] == jnp.arange(slots, dtype=jnp.int32)[:, None]
    sent_ids = jnp.sum(jnp.where(named, inner[None, :] + 1, 0), axis=1) - 1
    ids = exchange(sent_ids.reshape(senders, each))
    filled = jnp.sum((ids >= 0).astype(jnp.int32), axis=1)
    ids = ids.reshape(slots)

    active = (jnp.arange(per_atom, dtype=jnp.int32)[None, :] < proj_counts[:, None]).astype(F32)
    masked = coupling * active[:, :, None] * active[:, None, :]
    partner = shifted(masked.reshape(-1, 128), ("gy",), (half,)).reshape(coupling.shape)
    upper_half = lax.axis_index("gy") >= half
    mixers = jnp.where(
        upper_half,
        jnp.concatenate([partner, masked], axis=0),
        jnp.concatenate([masked, partner], axis=0),
    )
    mix_high, mix_low = spread(mixers)

    cell_ids = jnp.arange(cells, dtype=jnp.int32)[:, None]
    node_w = node_map % layers - cell_ids % cz * deg
    node_v = node_map // layers % (span_y + 1)
    node_u = node_map // (layers * (span_y + 1)) - cell_ids // cz * deg
    places = (node_u * side + node_w) * side + node_v
    stiff, turned, straight = canonical(places, matrices, shapes)

    row_next = shifted(orbitals[:1], ("gx",), (-1,))
    column_next = shifted(orbitals[:, :1], ("gy",), (-1,))
    corner_next = shifted(orbitals[:1, :1], both, (-1, -1))
    widened = jnp.concatenate(
        [
            jnp.concatenate([orbitals, column_next], axis=1),
            jnp.concatenate([row_next, corner_next], axis=1),
        ],
        axis=0,
    )
    grid = jnp.transpose(widened, (0, 2, 1, 3)).astype(F32)
    extended = grid.shape[:3]

    def advance(field, older):
        local, *outgoing = project(field, straight, placed, slots, cz, per_atom)
        image = stiffen(stiff, local, extended, cz)
        after = (image,)
        gathered = []
        for packet in outgoing:
            incoming = exchange(packet)
            gathered.append(merge(incoming, ids, filled, atoms, after))
            after = (gathered[-1][0],)
        answers = []
        for sums, sent in gathered:
            others = shifted(sent, ("gy",), (half,))
            replies = couple(sums, others, mix_high, mix_low, ids, filled, slots, after)
            answers.append(exchange(replies))
            after = (replies,)
        totals = []
        for part in range(PARTS):
            totals.append(apply(turned, answers[part], image, placed, part, cz, after))
            after = (totals[-1],)
        image = completed(jnp.concatenate(totals, axis=-1))
        return image if older is None else 2.0 * image - older

    older, field = None, grid
    for _ in range(FILTER_DEGREE):
        older, field = field, advance(field, older)
    filtered = field[:span_x, :, :span_y].astype(BF16)
    return jnp.transpose(filtered, (0, 2, 1, 3))


def solution(mesh):
    in_specs = (
        P("gx", "gy", None, None),
        P("gx", "gy", None, None, None),
        P("gx", "gy", None, None),
        P("gx", "gy", None, None, None, None),
        P("gx", "gy", None, None),
        P(("gx", "gy"), None, None),
        P(("gx", "gy")),
    )
    out_specs = P("gx", "gy", None, None)
    return jax.shard_map(
        on_device, mesh=mesh, in_specs=in_specs, out_specs=out_specs, check_vma=False
    )
```

time: 770 us -> 649 us (0.84); the launches traced: 768 us -> 639 us
  waiting for transfers between devices: 367 us -> 276 us
  blocking collectives: 160 us -> 91.1 us
  local copies, waits for them, and re-layouts: 22.6 us -> 90.5 us
  Pallas kernels: 109 us -> 90.1 us
  other arithmetic: 28.7 us -> 12 us
    unnamed x29 -> x131, local copies, waits for them, and re-layouts: 4.42 us -> 81.9 us
    all_to_all x3, blocking collectives: 160 us -> 91.1 us  [exchange(): lax.all_to_all(x, both, split_axis=0, concat_axis=0, axis_index_groups=te...]
    all_to_all x4 -> x10, waiting for transfers between devices: 155 us -> 102 us  [exchange(): lax.all_to_all(x, both, split_axis=0, concat_axis=0, axis_index_groups=te...]
    ppermute x31 -> x22, waiting for transfers between devices: 213 us -> 173 us  [shifted(): return lax.ppermute(x, axes if len(axes) > 1 else axes[0], pairs)]
    ppermute x31 -> x22, starting transfers between devices: 59.3 us -> 33.6 us  [shifted(): return lax.ppermute(x, axes if len(axes) > 1 else axes[0], pairs)]
    all_to_all x4 -> x10, starting transfers between devices: 20.2 us -> 44.9 us  [exchange(): lax.all_to_all(x, both, split_axis=0, concat_axis=0, axis_index_groups=te...]
    pallas_call x3, Pallas kernels: 28.3 us -> 12.1 us  [project(): pl.pallas_call(body, grid=(cells,), in_specs=[smem(), whole(field.shape),...]
    mul x4 -> x0, local copies, waits for them, and re-layouts: 11.4 us -> none  [on_device(): mixers * own]
  transfers between devices with their start and end apart: 35 -> 32, of which waited for: 12 -> 21; matrix products, arithmetic and copies ran while one was open for 4% -> 1% of each run, Pallas kernels for 3% -> 9%
where the time goes in v2:
time: 649 us; the launch traced here: 639 us
  waiting for transfers between devices  276 us (43%)
  blocking collectives  91.1 us (14%)
  local copies, waits for them, and re-layouts  90.5 us (14%)
  Pallas kernels  90.1 us (14%)
  starting transfers between devices  78.6 us (12%)
  other arithmetic  12 us (2%)
    ppermute x22, waiting for transfers between devices, shifted(): return lax.ppermute(x, axes if len(axes) > 1 else axes[0], pairs)  173 us
    all_to_all x10, waiting for transfers between devices, exchange(): lax.all_to_all(x, both, split_axis=0, concat_axis=0, axis_index_groups=te...  102 us
    all_to_all x3, blocking collectives, exchange(): lax.all_to_all(x, both, split_axis=0, concat_axis=0, axis_index_groups=te...  91.1 us
    unnamed x131, local copies, waits for them, and re-layouts  81.9 us
    all_to_all x10, starting transfers between devices, exchange(): lax.all_to_all(x, both, split_axis=0, concat_axis=0, axis_index_groups=te...  44.9 us
    ppermute x22, starting transfers between devices, shifted(): return lax.ppermute(x, axes if len(axes) > 1 else axes[0], pairs)  33.6 us
    pallas_call x6, Pallas kernels, apply(): pl.pallas_call(body, grid=(cells,), in_specs=[smem(), pl.BlockSpec((1, no...  26.3 us
    pallas_call x6, Pallas kernels, couple(): pl.pallas_call(body, in_specs=[smem(), smem(), vmem, vmem, vmem, vmem] +...  16.3 us
  transfers between devices with their start and end apart: 32, of which 21 were waited for; matrix products, arithmetic and copies ran while one was open for 1% of the time, Pallas kernels for 9%

profile of v2, /device:TPU:0, one launch (start us, length us, event | category | flops | bytes accessed | tf_op | source)
XLA Modules:
  0.0 639.1 jit_solution(17644742833804463515)
XLA Ops:
  2.7 6.1 collective-permute-start
  19.8 10.0 %canonical.1 = (bf16[8,512,512]{2,1,0:T(8,128)(2,1)S(1)}, bf16[8,512,512]{2,1,0:T(8,128)(2,1)S(1)}, bf16[8,512,512]{2,1,0:T(8,128)(2,1)S(1)}) custom-call(s32[8,1,512]{2,1,0:T(1,128)S(1)} %fusion.12.place_ref, bf16[8,512,512]{2,1,0:T(8,128)(2,1)S(1)} %bitcast.97, bf16[8,512,512]{2,1,0:T(8,128)(2,1)S(1)} %bitcast.98), custom_call_target="tpu_custom_call" | custom-call | tf_op jit(solution)/shard_map/canonical/pallas_call | solution.py:63
  43.2 31.3 %all_to_all.66.incoming_ref = bf16[256,32,128]{2,1,0:T(8,128)(2,1)S(1)} all-to-all(bf16[256,32,128]{2,1,0:T(8,128)(2,1)} %copy-done.51), channel_id=1, replica_groups={{0,1,2,3,8,9,10,11,16,17,18,19,24,25,26,27},{4,5,6,7,12,13,14,15,20,21,..., dimensions={0} | all-to-all | bytes 4194304 | tf_op jit(solution)/shard_map/all_to_all | solution.py:346
  94.6 28.6 %collective-permute-done.4 = f32[256,128]{1,0:T(8,128)S(1)} collective-permute-done((f32[256,128]{1,0:T(8,128)S(1)}, f32[256,128]{1,0:T(8,128)S(1)}, u32[]{:S(2)}, u32[]{:S(2)}) %collective-permute-start.4) | collective-permute-done | bytes 131104 | tf_op jit(solution)/shard_map/ppermute | solution.py:29
  139.4 35.3 %collective-permute-done.5.others_ref = bf16[64,32,128]{2,1,0:T(8,128)(2,1)S(1)} collective-permute-done((bf16[64,32,128]{2,1,0:T(8,128)(2,1)}, bf16[64,32,128]{2,1,0:T(8,128)(2,1)S(1)}, u32[]{:S(2)}, u32[]{:S(2)}) %collective-permute-start.5) | collective-permute-done | bytes 524320 | tf_op jit(solution)/shard_map/ppermute | solution.py:29
  180.1 5.4 all-to-all-start.4
  195.7 17.1 %all-to-all-done.4.answers_ref = bf16[256,32,128]{2,1,0:T(8,128)(2,1)} async-done(((bf16[256,32,128]{2,1,0:T(8,128)(2,1)}), bf16[256,32,128]{2,1,0:T(8,128)(2,1)}, u32[]{:S(2)}, u32[]{:S(2)}) %all-to-all-start.4) | async-done | bytes 2097184 | tf_op jit(solution)/shard_map/all_to_all | solution.py:346
  222.6 4.7 collective-permute-start.7
  227.2 5.9 collective-permute-done.6
  244.9 4.5 project.4
  249.5 29.9 %all_to_all.67.incoming_ref = bf16[256,32,128]{2,1,0:T(8,128)(2,1)} all-to-all(bf16[256,32,128]{2,1,0:T(8,128)(2,1)S(1)} %get-tuple-element.43), channel_id=1, replica_groups={{0,1,2,3,8,9,10,11,16,17,18,19,24,25,26,27},{4,5,6,7,12,13,14,15,20,21,..., dimensions={0} | all-to-all | bytes 4194304 | tf_op jit(solution)/shard_map/all_to_all | solution.py:346
  296.6 25.6 %all-to-all-done.6.incoming_ref = bf16[256,32,128]{2,1,0:T(8,128)(2,1)} async-done(((bf16[256,32,128]{2,1,0:T(8,128)(2,1)}), bf16[256,32,128]{2,1,0:T(8,128)(2,1)}, u32[]{:S(2)}, u32[]{:S(2)}) %all-to-all-start.6) | async-done | bytes 2097184 | tf_op jit(solution)/shard_map/all_to_all | solution.py:346
  336.2 35.7 %collective-permute-done.11.others_ref = bf16[64,32,128]{2,1,0:T(8,128)(2,1)S(1)} collective-permute-done((bf16[64,32,128]{2,1,0:T(8,128)(2,1)}, bf16[64,32,128]{2,1,0:T(8,128)(2,1)S(1)}, u32[]{:S(2)}, u32[]{:S(2)}) %collective-permute-start.11) | collective-permute-done | bytes 524320 | tf_op jit(solution)/shard_map/ppermute | solution.py:29
  377.3 4.6 all-to-all-start.8
  392.2 17.1 %all-to-all-done.8.answers_ref = bf16[256,32,128]{2,1,0:T(8,128)(2,1)} async-done(((bf16[256,32,128]{2,1,0:T(8,128)(2,1)}), bf16[256,32,128]{2,1,0:T(8,128)(2,1)}, u32[]{:S(2)}, u32[]{:S(2)}) %all-to-all-start.8) | async-done | bytes 2097184 | tf_op jit(solution)/shard_map/all_to_all | solution.py:346
  418.9 4.7 collective-permute-start.13
  423.6 6.0 collective-permute-done.12
  447.0 30.0 %all_to_all.68.incoming_ref = bf16[256,32,128]{2,1,0:T(8,128)(2,1)} all-to-all(bf16[256,32,128]{2,1,0:T(8,128)(2,1)S(1)} %get-tuple-element.50), channel_id=1, replica_groups={{0,1,2,3,8,9,10,11,16,17,18,19,24,25,26,27},{4,5,6,7,12,13,14,15,20,21,..., dimensions={0} | all-to-all | bytes 4194304 | tf_op jit(solution)/shard_map/all_to_all | solution.py:346
  494.6 25.2 %all-to-all-done.10.incoming_ref = bf16[256,32,128]{2,1,0:T(8,128)(2,1)} async-done(((bf16[256,32,128]{2,1,0:T(8,128)(2,1)}), bf16[256,32,128]{2,1,0:T(8,128)(2,1)}, u32[]{:S(2)}, u32[]{:S(2)}) %all-to-all-start.10) | async-done | bytes 2097184 | tf_op jit(solution)/shard_map/all_to_all | solution.py:346
  533.8 35.7 %collective-permute-done.17.others_ref = bf16[64,32,128]{2,1,0:T(8,128)(2,1)S(1)} collective-permute-done((bf16[64,32,128]{2,1,0:T(8,128)(2,1)}, bf16[64,32,128]{2,1,0:T(8,128)(2,1)S(1)}, u32[]{:S(2)}, u32[]{:S(2)}) %collective-permute-start.17) | collective-permute-done | bytes 524320 | tf_op jit(solution)/shard_map/ppermute | solution.py:29
  574.9 4.7 all-to-all-start.12
  589.8 17.1 %all-to-all-done.12.answers_ref = bf16[256,32,128]{2,1,0:T(8,128)(2,1)} async-done(((bf16[256,32,128]{2,1,0:T(8,128)(2,1)}), bf16[256,32,128]{2,1,0:T(8,128)(2,1)}, u32[]{:S(2)}, u32[]{:S(2)}) %all-to-all-start.12) | async-done | bytes 2097184 | tf_op jit(solution)/shard_map/all_to_all | solution.py:346
  616.6 4.6 collective-permute-start.19
  621.2 6.0 collective-permute-done.18
  (270 shorter events, 241.9 us)
Async XLA Ops:
  2.7 31.3 %collective-permute-start = (bf16[14,1,29,256]{3,1,2,0:T(2,128)(2,1)S(1)}, bf16[14,1,29,256]{3,1,2,0:T(2,128)(2,1)S(1)}, u32[]{:S(2)}, u32[]{:S(2)}) collective-permute-start(bf16[14,1,29,256]{3,1,2,0:T(2,128)(2,1)S(1)} %slice.77), channel_id=1, source_target_pairs={{0,7},{1,0},{2,1},{3,2},{4,3},{5,4},{6,5},{7,6},{8,15},{9,8},{10,9... | collective-permute-start | bytes 623624 | tf_op jit(solution)/shard_map/ppermute | solution.py:29
  8.8 25.2 %collective-permute-start.1 = (bf16[1,7,29,256]{3,1,2,0:T(8,128)(2,1)S(1)}, bf16[1,7,29,256]{3,1,2,0:T(8,128)(2,1)S(1)}, u32[]{:S(2)}, u32[]{:S(2)}) collective-permute-start(bf16[1,7,29,256]{3,1,2,0:T(8,128)(2,1)S(1)} %slice.78), channel_id=1, source_target_pairs={{0,24},{8,0},{16,8},{24,16},{1,25},{9,1},{17,9},{25,17},{2,26},{10... | collective-permute-start | bytes 311816 | tf_op jit(solution)/shard_map/ppermute | solution.py:29
  9.5 24.4 %collective-permute-start.2 = (bf16[1,1,29,256]{3,1,2,0:T(2,128)(2,1)S(1)}, bf16[1,1,29,256]{3,1,2,0:T(2,128)(2,1)S(1)}, u32[]{:S(2)}, u32[]{:S(2)}) collective-permute-start(bf16[1,1,29,256]{3,1,2,0:T(2,128)(2,1)S(1)} %slice.79), channel_id=1, source_target_pairs={{0,31},{1,24},{2,25},{3,26},{4,27},{5,28},{6,29},{7,30},{8,7},{9,0... | collective-permute-start | bytes 44552 | tf_op jit(solution)/shard_map/ppermute | solution.py:29
  11.6 31.5 %all-to-all-start = ((s32[16,1,16]{2,1,0:T(1,128)}), s32[16,1,16]{2,1,0:T(1,128)S(1)}, u32[]{:S(2)}, u32[]{:S(2)}) async-start(s32[16,1,16]{2,1,0:T(1,128)} %sub.81), calls=%async_computation | async-start | bytes 16384 | tf_op jit(solution)/shard_map/all_to_all | solution.py:346
  74.5 50.1 %all-to-all-start.2 = ((bf16[256,32,128]{2,1,0:T(8,128)(2,1)}), bf16[256,32,128]{2,1,0:T(8,128)(2,1)}, u32[]{:S(2)}, u32[]{:S(2)}) async-start(bf16[256,32,128]{2,1,0:T(8,128)(2,1)} %copy-done.50), calls=%async_computation.2 | async-start | bytes 4194304 | tf_op jit(solution)/shard_map/all_to_all | solution.py:346
  91.2 38.7 %collective-permute-start.3 = (bf16[64,32,128]{2,1,0:T(8,128)(2,1)}, bf16[64,32,128]{2,1,0:T(8,128)(2,1)}, u32[]{:S(2)}, u32[]{:S(2)}) collective-permute-start(bf16[64,32,128]{2,1,0:T(8,128)(2,1)} %get-tuple-element.37), channel_id=1, source_target_pairs={{0,4},{1,5},{2,6},{3,7},{4,0},{5,1},{6,2},{7,3},{8,12},{9,13},{10,... | collective-permute-start | bytes 1572872 | tf_op jit(solution)/shard_map/ppermute | solution.py:29
  91.6 31.6 %collective-permute-start.4 = (f32[256,128]{1,0:T(8,128)S(1)}, f32[256,128]{1,0:T(8,128)S(1)}, u32[]{:S(2)}, u32[]{:S(2)}) collective-permute-start(f32[256,128]{1,0:T(8,128)S(1)} %reshape.517), channel_id=1, source_target_pairs={{0,4},{1,5},{2,6},{3,7},{4,0},{5,1},{6,2},{7,3},{8,12},{9,13},{10,... | collective-permute-start | bytes 393224 | tf_op jit(solution)/shard_map/ppermute | solution.py:29
  134.2 45.9 %all-to-all-start.3 = ((bf16[256,32,128]{2,1,0:T(8,128)(2,1)}), bf16[256,32,128]{2,1,0:T(8,128)(2,1)}, u32[]{:S(2)}, u32[]{:S(2)}) async-start(bf16[256,32,128]{2,1,0:T(8,128)(2,1)} %copy-done.36), calls=%async_computation.3 | async-start | bytes 4194304 | tf_op jit(solution)/shard_map/all_to_all | solution.py:346
  138.6 36.0 %collective-permute-start.5 = (bf16[64,32,128]{2,1,0:T(8,128)(2,1)}, bf16[64,32,128]{2,1,0:T(8,128)(2,1)S(1)}, u32[]{:S(2)}, u32[]{:S(2)}) collective-permute-start(bf16[64,32,128]{2,1,0:T(8,128)(2,1)} %copy-done.54), channel_id=1, source_target_pairs={{0,4},{1,5},{2,6},{3,7},{4,0},{5,1},{6,2},{7,3},{8,12},{9,13},{10,... | collective-permute-start | bytes 1572872 | tf_op jit(solution)/shard_map/ppermute | solution.py:29
  180.1 32.8 %all-to-all-start.4 = ((bf16[256,32,128]{2,1,0:T(8,128)(2,1)}), bf16[256,32,128]{2,1,0:T(8,128)(2,1)}, u32[]{:S(2)}, u32[]{:S(2)}) async-start(bf16[256,32,128]{2,1,0:T(8,128)(2,1)} %copy-done.30), calls=%async_computation.4 | async-start | bytes 4194304 | tf_op jit(solution)/shard_map/all_to_all | solution.py:346
  222.6 13.0 %collective-permute-start.7 = (bf16[15,29,256]{2,0,1:T(8,128)(2,1)S(1)}, bf16[15,29,256]{2,0,1:T(8,128)(2,1)S(1)}, u32[]{:S(2)}, u32[]{:S(2)}) collective-permute-start(bf16[15,29,256]{2,0,1:T(8,128)(2,1)S(1)} %bitcast.100), channel_id=1, source_target_pairs={{0,7},{1,0},{2,1},{3,2},{4,3},{5,4},{6,5},{7,6},{8,15},{9,8},{10,9... | collective-permute-start | bytes 668168 | tf_op jit(solution)/shard_map/ppermute | solution.py:29
  279.3 42.8 %all-to-all-start.6 = ((bf16[256,32,128]{2,1,0:T(8,128)(2,1)}), bf16[256,32,128]{2,1,0:T(8,128)(2,1)}, u32[]{:S(2)}, u32[]{:S(2)}) async-start(bf16[256,32,128]{2,1,0:T(8,128)(2,1)} %get-tuple-element.47), calls=%async_computation.6 | async-start | bytes 4194304 | tf_op jit(solution)/shard_map/all_to_all | solution.py:346
  294.1 32.9 %collective-permute-start.10 = (bf16[64,32,128]{2,1,0:T(8,128)(2,1)}, bf16[64,32,128]{2,1,0:T(8,128)(2,1)}, u32[]{:S(2)}, u32[]{:S(2)}) collective-permute-start(bf16[64,32,128]{2,1,0:T(8,128)(2,1)} %get-tuple-element.46), channel_id=1, source_target_pairs={{0,4},{1,5},{2,6},{3,7},{4,0},{5,1},{6,2},{7,3},{8,12},{9,13},{10,... | collective-permute-start | bytes 1572872 | tf_op jit(solution)/shard_map/ppermute | solution.py:29
  331.4 45.9 %all-to-all-start.7 = ((bf16[256,32,128]{2,1,0:T(8,128)(2,1)}), bf16[256,32,128]{2,1,0:T(8,128)(2,1)}, u32[]{:S(2)}, u32[]{:S(2)}) async-start(bf16[256,32,128]{2,1,0:T(8,128)(2,1)} %copy-done.38), calls=%async_computation.7 | async-start | bytes 4194304 | tf_op jit(solution)/shard_map/all_to_all | solution.py:346
  335.9 36.0 %collective-permute-start.11 = (bf16[64,32,128]{2,1,0:T(8,128)(2,1)}, bf16[64,32,128]{2,1,0:T(8,128)(2,1)S(1)}, u32[]{:S(2)}, u32[]{:S(2)}) collective-permute-start(bf16[64,32,128]{2,1,0:T(8,128)(2,1)} %copy-done.55), channel_id=1, source_target_pairs={{0,4},{1,5},{2,6},{3,7},{4,0},{5,1},{6,2},{7,3},{8,12},{9,13},{10,... | collective-permute-start | bytes 1572872 | tf_op jit(solution)/shard_map/ppermute | solution.py:29
  377.3 32.0 %all-to-all-start.8 = ((bf16[256,32,128]{2,1,0:T(8,128)(2,1)}), bf16[256,32,128]{2,1,0:T(8,128)(2,1)}, u32[]{:S(2)}, u32[]{:S(2)}) async-start(bf16[256,32,128]{2,1,0:T(8,128)(2,1)} %copy-done.32), calls=%async_computation.8 | async-start | bytes 4194304 | tf_op jit(solution)/shard_map/all_to_all | solution.py:346
  418.9 13.0 %collective-permute-start.13 = (bf16[15,29,256]{2,0,1:T(8,128)(2,1)S(1)}, bf16[15,29,256]{2,0,1:T(8,128)(2,1)S(1)}, u32[]{:S(2)}, u32[]{:S(2)}) collective-permute-start(bf16[15,29,256]{2,0,1:T(8,128)(2,1)S(1)} %bitcast.101), channel_id=1, source_target_pairs={{0,7},{1,0},{2,1},{3,2},{4,3},{5,4},{6,5},{7,6},{8,15},{9,8},{10,9... | collective-permute-start | bytes 668168 | tf_op jit(solution)/shard_map/ppermute | solution.py:29
  477.0 42.8 %all-to-all-start.10 = ((bf16[256,32,128]{2,1,0:T(8,128)(2,1)}), bf16[256,32,128]{2,1,0:T(8,128)(2,1)}, u32[]{:S(2)}, u32[]{:S(2)}) async-start(bf16[256,32,128]{2,1,0:T(8,128)(2,1)} %get-tuple-element.54), calls=%async_computation.10 | async-start | bytes 4194304 | tf_op jit(solution)/shard_map/all_to_all | solution.py:346
  491.8 32.9 %collective-permute-start.16 = (bf16[64,32,128]{2,1,0:T(8,128)(2,1)}, bf16[64,32,128]{2,1,0:T(8,128)(2,1)}, u32[]{:S(2)}, u32[]{:S(2)}) collective-permute-start(bf16[64,32,128]{2,1,0:T(8,128)(2,1)} %get-tuple-element.53), channel_id=1, source_target_pairs={{0,4},{1,5},{2,6},{3,7},{4,0},{5,1},{6,2},{7,3},{8,12},{9,13},{10,... | collective-permute-start | bytes 1572872 | tf_op jit(solution)/shard_map/ppermute | solution.py:29
  529.0 45.9 %all-to-all-start.11 = ((bf16[256,32,128]{2,1,0:T(8,128)(2,1)}), bf16[256,32,128]{2,1,0:T(8,128)(2,1)}, u32[]{:S(2)}, u32[]{:S(2)}) async-start(bf16[256,32,128]{2,1,0:T(8,128)(2,1)} %copy-done.34), calls=%async_computation.11 | async-start | bytes 4194304 | tf_op jit(solution)/shard_map/all_to_all | solution.py:346
  533.5 36.0 %collective-permute-start.17 = (bf16[64,32,128]{2,1,0:T(8,128)(2,1)}, bf16[64,32,128]{2,1,0:T(8,128)(2,1)S(1)}, u32[]{:S(2)}, u32[]{:S(2)}) collective-permute-start(bf16[64,32,128]{2,1,0:T(8,128)(2,1)} %copy-done.56), channel_id=1, source_target_pairs={{0,4},{1,5},{2,6},{3,7},{4,0},{5,1},{6,2},{7,3},{8,12},{9,13},{10,... | collective-permute-start | bytes 1572872 | tf_op jit(solution)/shard_map/ppermute | solution.py:29
  574.9 32.0 %all-to-all-start.12 = ((bf16[256,32,128]{2,1,0:T(8,128)(2,1)}), bf16[256,32,128]{2,1,0:T(8,128)(2,1)}, u32[]{:S(2)}, u32[]{:S(2)}) async-start(bf16[256,32,128]{2,1,0:T(8,128)(2,1)} %copy-done.28), calls=%async_computation.12 | async-start | bytes 4194304 | tf_op jit(solution)/shard_map/all_to_all | solution.py:346
  616.3 10.9 %collective-permute-start.18 = (bf16[15,29,256]{2,0,1:T(8,128)(2,1)S(1)}, bf16[15,29,256]{2,0,1:T(8,128)(2,1)S(1)}, u32[]{:S(2)}, u32[]{:S(2)}) collective-permute-start(bf16[15,29,256]{2,0,1:T(8,128)(2,1)S(1)} %bitcast.104), channel_id=1, source_target_pairs={{0,1},{1,2},{2,3},{3,4},{4,5},{5,6},{6,7},{7,0},{8,9},{9,10},{10,1... | collective-permute-start | bytes 668168 | tf_op jit(solution)/shard_map/ppermute | solution.py:29
  616.6 12.9 %collective-permute-start.19 = (bf16[15,29,256]{2,0,1:T(8,128)(2,1)S(1)}, bf16[15,29,256]{2,0,1:T(8,128)(2,1)S(1)}, u32[]{:S(2)}, u32[]{:S(2)}) collective-permute-start(bf16[15,29,256]{2,0,1:T(8,128)(2,1)S(1)} %bitcast.102), channel_id=1, source_target_pairs={{0,7},{1,0},{2,1},{3,2},{4,3},{5,4},{6,5},{7,6},{8,15},{9,8},{10,9... | collective-permute-start | bytes 668168 | tf_op jit(solution)/shard_map/ppermute | solution.py:29
  (73 other events, 391.4 us)

commit v3 on v2

--- a/solution.py
+++ b/solution.py
@@ -9,7 +9,11 @@
 
 
 FILTER_DEGREE = 3
-PARTS = 2
+PARTS = 1
+UNIT = 8
+TIGHT = 54
+NARROW = 188
+MODE = "cond"
 GRANT = 20 * 1024 * 1024
 GROUP = 8
 BF16 = jnp.bfloat16
@@ -110,28 +114,28 @@
     )(mixers)
 
 
-def project(field, straight, placed, slots, cz, per_atom):
+def project(field, straight, starts, room, cz, per_atom):
     cells, rows, nodes = straight.shape
     side = field.shape[2]
     deg = side - 1
     breadth = field.shape[3]
     per_cell = rows // per_atom
     width = breadth // PARTS
-
-    def body(placed_ref, field_ref, straight_ref, local_ref, *out_refs):
+    units = per_atom // UNIT
+
+    def body(starts_ref, field_ref, straight_ref, local_ref, *out_refs):
         c = pl.program_id(0)
         u = c // cz * deg
         w = c % cz * deg
         block = field_ref[pl.ds(u, side), pl.ds(w, side)]
         local = block.reshape(nodes, breadth).astype(BF16)
         local_ref[0] = local
-        values = jnp.dot(straight_ref[0], local, preferred_element_type=F32).astype(BF16)
+        values = jnp.dot(straight_ref[0], local, preferred_element_type=F32)
         for k in range(per_cell):
-            slot = placed_ref[c * per_cell + k]
+            start = starts_ref[c * per_cell + k]
             for s, out_ref in enumerate(out_refs):
-                out_ref[slot] = values[
-                    k * per_atom : (k + 1) * per_atom, s * width : (s + 1) * width
-                ]
+                piece = values[k * per_atom : (k + 1) * per_atom, s * width : (s + 1) * width]
+                out_ref[pl.ds(start, units)] = piece.reshape(units, UNIT, width).astype(BF16)
 
     return pl.pallas_call(
         body,
@@ -144,14 +148,14 @@
         out_specs=[
             pl.BlockSpec((1, nodes, breadth), lambda c: (c, 0, 0)),
         ]
-        + [whole((slots, per_atom, width))] * PARTS,
+        + [whole((room, UNIT, width))] * PARTS,
         out_shape=[
             jax.ShapeDtypeStruct((cells, nodes, breadth), BF16),
         ]
-        + [jax.ShapeDtypeStruct((slots, per_atom, width), BF16)] * PARTS,
+        + [jax.ShapeDtypeStruct((room, UNIT, width), BF16)] * PARTS,
         compiler_params=pltpu.CompilerParams(vmem_limit_bytes=GRANT),
         name="project",
-    )(placed, field, straight)
+    )(starts, field, straight)
 
 
 def stiffen(stiff, local, extended, cz):
@@ -187,86 +191,114 @@
     )(stiff, local)
 
 
-def merge(incoming, ids, filled, atoms, after):
-    slots, per_atom, breadth = incoming.shape
+def merge(incoming, tables, atoms, units, span, after):
+    breadth = incoming.shape[2]
+    ids, begins, filled, spots, _ = tables
     senders = filled.shape[0]
-    each = slots // senders
-
-    def body(ids_ref, filled_ref, incoming_ref, *refs):
+    each = ids.shape[0] // senders
+
+    def body(ids_ref, begins_ref, filled_ref, spots_ref, incoming_ref, *refs):
         sums_ref, sent_ref = refs[len(after) :]
         sums_ref[...] = jnp.zeros_like(sums_ref)
-        for g in range(senders):
-
+
+        def sender(g, carry):
             def add(j, carry):
                 slot = g * each + j
-                atom = ids_ref[slot]
-                sums_ref[atom] = sums_ref[atom] + incoming_ref[slot].astype(F32)
+                into = pl.ds(ids_ref[slot] * units, units)
+                piece = incoming_ref[pl.ds(begins_ref[slot], units)].astype(F32)
+                sums_ref[into] = sums_ref[into] + piece
                 return carry
 
-            lax.fori_loop(0, filled_ref[g], add, 0)
-        sent_ref[...] = sums_ref[...].astype(BF16)
-
-    return pl.pallas_call(
-        body,
-        in_specs=[smem(), smem(), pl.BlockSpec(memory_space=pltpu.VMEM)] + unread(after),
+            return lax.fori_loop(0, filled_ref[g], add, carry)
+
+        lax.fori_loop(0, senders, sender, 0)
+
+        def pack(a, carry):
+            piece = sums_ref[pl.ds(a * units, units)]
+            sent_ref[pl.ds(spots_ref[a], units)] = piece.astype(BF16)
+            return carry
+
+        lax.fori_loop(0, atoms, pack, 0, unroll=4)
+
+    return pl.pallas_call(
+        body,
+        in_specs=[smem()] * 4 + [pl.BlockSpec(memory_space=pltpu.VMEM)] + unread(after),
         out_specs=[pl.BlockSpec(memory_space=pltpu.VMEM)] * 2,
         out_shape=[
-            jax.ShapeDtypeStruct((atoms, per_atom, breadth), F32),
-            jax.ShapeDtypeStruct((atoms, per_atom, breadth), BF16),
+            jax.ShapeDtypeStruct((atoms * units, UNIT, breadth), F32),
+            jax.ShapeDtypeStruct((span, UNIT, breadth), BF16),
         ],
         compiler_params=pltpu.CompilerParams(vmem_limit_bytes=GRANT),
         name="merge",
-    )(ids, filled, incoming, *after)
-
-
-def couple(sums, others, high, low, ids, filled, slots, after):
-    atoms, per_atom, breadth = sums.shape
+    )(ids, begins, filled, spots, incoming, *after)
+
+
+def couple(sums, others, high, low, tables, units, room, after):
+    breadth = sums.shape[2]
     groups, edge, _ = high.shape
-    members = atoms // groups
+    ids, begins, filled, spots, shared = tables
     senders = filled.shape[0]
-    each = slots // senders
-
-    def body(ids_ref, filled_ref, sums_ref, others_ref, high_ref, low_ref, *refs):
-        out_ref, kept_ref = refs[len(after) :]
-        for g in range(groups):
-            part = pl.ds(g * members, members)
-            total = sums_ref[part] + others_ref[part].astype(F32)
-            total = total.reshape(edge, breadth)
+    each = ids.shape[0] // senders
+    rows = units * UNIT
+
+    def body(ids_ref, begins_ref, filled_ref, spots_ref, shared_ref, sums_ref, others_ref, *refs):
+        high_ref, low_ref = refs[:2]
+        out_ref, total_ref, kept_ref = refs[2 + len(after) :]
+
+        def mix(g, carry):
+            for m in range(GROUP):
+                a = g * GROUP + m
+                piece = others_ref[pl.ds(spots_ref[a], units)].astype(F32)
+                piece = jnp.where(shared_ref[a] > 0, piece, 0.0)
+                piece = sums_ref[pl.ds(a * units, units)] + piece
+                total_ref[m * rows : (m + 1) * rows] = piece.reshape(rows, breadth)
+            total = total_ref[...]
             upper = total.astype(BF16)
             lower = (total - upper.astype(F32)).astype(BF16)
             mixed = jnp.dot(high_ref[g], upper, preferred_element_type=F32)
             mixed = mixed + jnp.dot(low_ref[g], upper, preferred_element_type=F32)
             mixed = mixed + jnp.dot(high_ref[g], lower, preferred_element_type=F32)
-            kept_ref[part] = mixed.astype(BF16).reshape(members, per_atom, breadth)
-        for g in range(senders):
-
+            mixed = mixed.reshape(GROUP * units, UNIT, breadth).astype(BF16)
+            kept_ref[pl.ds(g * GROUP * units, GROUP * units)] = mixed
+            return carry
+
+        lax.fori_loop(0, groups, mix, 0, unroll=2)
+
+        def sender(g, carry):
             def copy(j, carry):
                 slot = g * each + j
-                out_ref[slot] = kept_ref[ids_ref[slot]]
+                piece = kept_ref[pl.ds(ids_ref[slot] * units, units)]
+                out_ref[pl.ds(begins_ref[slot], units)] = piece
                 return carry
 
-            lax.fori_loop(0, filled_ref[g], copy, 0)
+            return lax.fori_loop(0, filled_ref[g], copy, carry)
+
+        lax.fori_loop(0, senders, sender, 0)
 
     vmem = pl.BlockSpec(memory_space=pltpu.VMEM)
     return pl.pallas_call(
         body,
-        in_specs=[smem(), smem(), vmem, vmem, vmem, vmem] + unread(after),
+        in_specs=[smem()] * 5 + [vmem] * 4 + unread(after),
         out_specs=vmem,
-        out_shape=jax.ShapeDtypeStruct((slots, per_atom, breadth), BF16),
-        scratch_shapes=[pltpu.VMEM((atoms, per_atom, breadth), BF16)],
+        out_shape=jax.ShapeDtypeStruct((room, UNIT, breadth), BF16),
+        scratch_shapes=[
+            pltpu.VMEM((edge, breadth), F32),
+            pltpu.VMEM((sums.shape[0], UNIT, breadth), BF16),
+        ],
         compiler_params=pltpu.CompilerParams(vmem_limit_bytes=GRANT),
         name="couple",
-    )(ids, filled, sums, others, high, low, *after)
-
-
-def apply(turned, answers, begun, placed, part, cz, after):
+    )(ids, begins, filled, spots, shared, sums, others, high, low, *after)
+
+
+def apply(turned, answers, begun, starts, used, part, cz, per_atom, after):
     cells, nodes, rows = turned.shape
-    _, per_atom, breadth = answers.shape
+    breadth = answers.shape[2]
     per_cell = rows // per_atom
+    units = per_atom // UNIT
     side = begun.shape[2]
     deg = side - 1
 
-    def body(placed_ref, turned_ref, answers_ref, begun_ref, *refs):
+    def body(starts_ref, used_ref, turned_ref, answers_ref, begun_ref, *refs):
         total_ref, stack_ref = refs[len(after) :]
         c = pl.program_id(0)
 
@@ -274,9 +306,13 @@
         def _():
             total_ref[...] = begun_ref[...]
 
+        row = lax.broadcasted_iota(jnp.int32, (per_atom, breadth), 0)
         for k in range(per_cell):
-            at = k * per_atom
-            stack_ref[at : at + per_atom] = answers_ref[placed_ref[c * per_cell + k]]
+            entry = c * per_cell + k
+            piece = answers_ref[pl.ds(starts_ref[entry], units)].astype(F32)
+            piece = piece.reshape(per_atom, breadth)
+            piece = jnp.where(row < used_ref[entry] * UNIT, piece, 0.0)
+            stack_ref[k * per_atom : (k + 1) * per_atom] = piece.astype(BF16)
         result = jnp.dot(turned_ref[0], stack_ref[...], preferred_element_type=F32)
         u = pl.ds(c // cz * deg, side)
         w = pl.ds(c % cz * deg, side)
@@ -287,6 +323,7 @@
         body,
         grid=(cells,),
         in_specs=[
+            smem(),
             smem(),
             pl.BlockSpec((1, nodes, rows), lambda c: (c, 0, 0)),
             whole(answers.shape),
@@ -298,7 +335,7 @@
         scratch_shapes=[pltpu.VMEM((rows, breadth), BF16)],
         compiler_params=pltpu.CompilerParams(vmem_limit_bytes=GRANT),
         name="apply",
-    )(placed, turned, answers, begun, *after)
+    )(starts, used, turned, answers, begun, *after)
 
 
 def completed(total):
@@ -347,29 +384,83 @@
             x, both, split_axis=0, concat_axis=0, axis_index_groups=teams, tiled=True
         )
 
-    flat = atom_names.reshape(entries)
-    homes = flat // home_atoms
+    units = per_atom // UNIT
+    my_x, my_y = lax.axis_index("gx"), lax.axis_index("gy")
+    my_half, my_place = my_y // half, my_y % half
+    me = my_x * n_gy + my_y
+    mine = my_x * half + my_place
+
+    notes = jnp.concatenate([atom_names.reshape(entries), proj_counts])
+    notes = jnp.broadcast_to(notes, (devices, entries + home_atoms))
+    notes = lax.all_to_all(notes, both, split_axis=0, concat_axis=0, tiled=True)
+    names, counts = notes[:, :entries], notes[:, entries:]
+    needs = (counts + UNIT - 1) // UNIT
+    homes, inner = names // home_atoms, names % home_atoms
     homes_y = homes % n_gy
+    at_home = (homes[:, :, None] == jnp.arange(devices)).astype(BF16)
+    at_inner = (inner[:, :, None] == jnp.arange(home_atoms)).astype(BF16)
+    picked = jnp.einsum("seh,hi->sei", at_home, needs.astype(BF16), preferred_element_type=F32)
+    sizes = jnp.sum(picked * at_inner.astype(F32), axis=2).astype(jnp.int32)
     collectors = homes // n_gy * half + homes_y % half
-    inner = homes_y // half * home_atoms + flat % home_atoms
-    order = jnp.arange(entries, dtype=jnp.int32)
-    earlier = (collectors[:, None] == collectors[None, :]) & (order[None, :] < order[:, None])
-    placed = collectors * each + jnp.sum(earlier.astype(jnp.int32), axis=1)
-    named = placed[None, :] == jnp.arange(slots, dtype=jnp.int32)[:, None]
-    sent_ids = jnp.sum(jnp.where(named, inner[None, :] + 1, 0), axis=1) - 1
-    ids = exchange(sent_ids.reshape(senders, each))
-    filled = jnp.sum((ids >= 0).astype(jnp.int32), axis=1)
-    ids = ids.reshape(slots)
-
-    active = (jnp.arange(per_atom, dtype=jnp.int32)[None, :] < proj_counts[:, None]).astype(F32)
-    masked = coupling * active[:, :, None] * active[:, None, :]
-    partner = shifted(masked.reshape(-1, 128), ("gy",), (half,)).reshape(coupling.shape)
-    upper_half = lax.axis_index("gy") >= half
+    held = homes_y // half * home_atoms + inner
+
+    def by_half(x):
+        return x.reshape((n_gx, 2, half) + x.shape[1:])
+
+    split = [
+        jnp.einsum(
+            "seh,sei->hi",
+            by_half(at_home)[:, h].reshape((senders,) + at_home.shape[1:]),
+            by_half(at_inner)[:, h].reshape((senders,) + at_inner.shape[1:]),
+            preferred_element_type=F32,
+        )
+        for h in range(2)
+    ]
+    common = ((split[0] > 0) & (split[1] > 0)).astype(jnp.int32)
+    at_collector = collectors[:, :, None] == jnp.arange(senders)
+    loads = jnp.sum(jnp.where(at_collector, sizes[:, :, None], 0), axis=1)
+    crossing = jnp.sum(by_half(common * needs), axis=(1, 3))
+    fits = (jnp.max(loads) + units - 1 <= TIGHT * each * units // 64) & (
+        jnp.max(crossing) + units <= NARROW * atoms * units // 256
+    )
+
+    def of_me(x):
+        return lax.dynamic_index_in_dim(x, me, 0, keepdims=False)
+
+    def of_my_half(x):
+        x = lax.dynamic_index_in_dim(by_half(x), my_half, 1, keepdims=False)
+        return x.reshape((senders,) + x.shape[2:])
+
+    def hosted(x):
+        x = lax.dynamic_index_in_dim(by_half(x), my_x, 0, keepdims=False)
+        return lax.dynamic_index_in_dim(x, my_place, 1, keepdims=False).reshape(atoms)
+
+    before = jnp.arange(entries)[:, None] < jnp.arange(entries)[None, :]
+    own, used = of_me(collectors), of_me(sizes)
+    ahead = before & (own[:, None] == own[None, :])
+    offsets = jnp.sum(jnp.where(ahead, used[:, None], 0), axis=0)
+    theirs = (of_my_half(collectors) == mine).astype(BF16)
+    earlier = before.astype(BF16)
+    ranks = jnp.dot(theirs, earlier, preferred_element_type=F32).astype(jnp.int32)
+    lengths = theirs * of_my_half(sizes).astype(BF16)
+    shifts = jnp.dot(lengths, earlier, preferred_element_type=F32).astype(jnp.int32)
+    chosen = (ranks[:, None, :] == jnp.arange(each)[:, None]) & (theirs[:, None, :] > 0)
+    ids = jnp.sum(jnp.where(chosen, of_my_half(held)[:, None, :], 0), axis=2).reshape(slots)
+    places_in = jnp.sum(jnp.where(chosen, shifts[:, None, :], 0), axis=2)
+    filled = jnp.sum(theirs.astype(F32), axis=1).astype(jnp.int32)
+    shared = hosted(common)
+    moved = shared * hosted(needs)
+    upto = jnp.arange(atoms)[:, None] < jnp.arange(atoms)[None, :]
+    spots = jnp.sum(jnp.where(upto, moved[:, None], 0), axis=0)
+
+    partner = shifted(coupling.reshape(-1, 128), ("gy",), (half,)).reshape(coupling.shape)
     mixers = jnp.where(
-        upper_half,
-        jnp.concatenate([partner, masked], axis=0),
-        jnp.concatenate([masked, partner], axis=0),
+        my_half > 0,
+        jnp.concatenate([partner, coupling], axis=0),
+        jnp.concatenate([coupling, partner], axis=0),
     )
+    active = (jnp.arange(per_atom)[None, :] < hosted(counts)[:, None]).astype(F32)
+    mixers = mixers * active[:, :, None] * active[:, None, :]
     mix_high, mix_low = spread(mixers)
 
     cell_ids = jnp.arange(cells, dtype=jnp.int32)[:, None]
@@ -392,32 +483,61 @@
     grid = jnp.transpose(widened, (0, 2, 1, 3)).astype(F32)
     extended = grid.shape[:3]
 
-    def advance(field, older):
-        local, *outgoing = project(field, straight, placed, slots, cz, per_atom)
+    def advance(field, older, cap, span):
+        room = senders * cap
+        starts = own * cap + offsets
+        begins = (places_in + jnp.arange(senders)[:, None] * cap).reshape(slots)
+        tables = (ids, begins, filled, spots, shared)
+        local, *outgoing = project(field, straight, starts, room, cz, per_atom)
         image = stiffen(stiff, local, extended, cz)
         after = (image,)
         gathered = []
         for packet in outgoing:
             incoming = exchange(packet)
-            gathered.append(merge(incoming, ids, filled, atoms, after))
+            gathered.append(merge(incoming, tables, atoms, units, span, after))
             after = (gathered[-1][0],)
         answers = []
         for sums, sent in gathered:
             others = shifted(sent, ("gy",), (half,))
-            replies = couple(sums, others, mix_high, mix_low, ids, filled, slots, after)
+            replies = couple(
+                sums, others, mix_high, mix_low, tables, units, room, after
+            )
             answers.append(exchange(replies))
             after = (replies,)
         totals = []
         for part in range(PARTS):
-            totals.append(apply(turned, answers[part], image, placed, part, cz, after))
+            totals.append(
+                apply(turned, answers[part], image, starts, used, part, cz, per_atom, after)
+            )
             after = (totals[-1],)
-        image = completed(jnp.concatenate(totals, axis=-1))
+        image = completed(jnp.concatenate(totals, axis=-1) if PARTS > 1 else totals[0])
         return image if older is None else 2.0 * image - older
 
-    older, field = None, grid
-    for _ in range(FILTER_DEGREE):
-        older, field = field, advance(field, older)
-    filtered = field[:span_x, :, :span_y].astype(BF16)
+    def packed():
+        cap = TIGHT * each * units // 64
+        span = NARROW * atoms * units // 256
+        older, field = None, grid
+        for _ in range(FILTER_DEGREE):
+            older, field = field, advance(field, older, cap, span)
+        return field[:span_x, :, :span_y].astype(BF16)
+
+    def roomy():
+        cap = (each + 1) * units
+        span = (atoms + 1) * units
+
+        def step(at, fields):
+            older, field = fields
+            image = advance(field, None, cap, span)
+            return field, jnp.where(at == 0, image, 2.0 * image - older)
+
+        fields = (jnp.zeros_like(grid), grid)
+        field = lax.fori_loop(0, FILTER_DEGREE, step, fields)[1]
+        return field[:span_x, :, :span_y].astype(BF16)
+
+    if MODE == "cond":
+        filtered = lax.cond(fits, packed, roomy)
+    else:
+        filtered = packed() if MODE == "fast" else roomy()
     return jnp.transpose(filtered, (0, 2, 1, 3))
 
 

time: 649 us -> 583 us (0.90)
  blocking collectives: 91.1 us -> 135 us
  local copies, waits for them, and re-layouts: 90.5 us -> 50.3 us
  waiting for transfers between devices: 276 us -> 244 us
  starting transfers between devices: 78.6 us -> 49.1 us
  Pallas kernels: 90.1 us -> 73.3 us
  other arithmetic: 12 us -> 19.6 us
    unnamed x131 -> x9, local copies, waits for them, and re-layouts: 81.9 us -> 6.8 us
    all_to_all x3, blocking collectives: 91.1 us -> 135 us  [exchange(): lax.all_to_all(x, both, split_axis=0, concat_axis=0, axis_index_groups=te...]
    all_to_all x10 -> x3, starting transfers between devices: 44.9 us -> 11.2 us  [exchange(): lax.all_to_all(x, both, split_axis=0, concat_axis=0, axis_index_groups=te...]
    ppermute x22 -> x19, waiting for transfers between devices: 173 us -> 140 us  [shifted(): return lax.ppermute(x, axes if len(axes) > 1 else axes[0], pairs)]
    pallas_call x18 -> x9, Pallas kernels: 58.9 us -> 28.6 us  [the longest x3 10.2 us: couple(): pl.pallas_call(body, in_specs=[smem()] * 5 + [vmem] * 4 + unread(after),...]
    another operation x3 -> x129, local copies, waits for them, and re-layouts: 0.08 us -> 28.5 us  [the longest x1 0.08 us: on_device(): flat = atom_names.reshape(entries)]
    pallas_call x3, Pallas kernels: 8.07 us -> 18.1 us  [stiffen(): pl.pallas_call(body, grid=(cells,), in_specs=[pl.BlockSpec((1, nodes, nod...]
    all_to_all x0 -> x1, starting transfers between devices: none -> 7.33 us  [on_device(): notes = lax.all_to_all(notes, both, split_axis=0, concat_axis=0, tiled=True)]
  transfers between devices with their start and end apart: 32 -> 23, of which waited for: 21 -> 18; matrix products, arithmetic and copies ran while one was open for 1% -> 3% of each run, Pallas kernels for 9% -> 5%
where the time goes in v3:
time: 583 us; the launch traced here: 576 us
  waiting for transfers between devices  244 us (42%)
  blocking collectives  135 us (23%)
  Pallas kernels  73.3 us (13%)
  local copies, waits for them, and re-layouts  50.3 us (9%)
  starting transfers between devices  49.1 us (8%)
  other arithmetic  19.6 us (3%)
    ppermute x19, waiting for transfers between devices, shifted(): return lax.ppermute(x, axes if len(axes) > 1 else axes[0], pairs)  140 us
    all_to_all x3, blocking collectives, exchange(): lax.all_to_all(x, both, split_axis=0, concat_axis=0, axis_index_groups=te...  135 us
    all_to_all x3, waiting for transfers between devices, exchange(): lax.all_to_all(x, both, split_axis=0, concat_axis=0, axis_index_groups=te...  104 us
    ppermute x19, starting transfers between devices, shifted(): return lax.ppermute(x, axes if len(axes) > 1 else axes[0], pairs)  30.5 us
    another operation x128, local copies, waits for them, and re-layouts  27.7 us
    pallas_call x3, Pallas kernels, stiffen(): pl.pallas_call(body, grid=(cells,), in_specs=[pl.BlockSpec((1, nodes, nod...  18.1 us
    pallas_call x3, Pallas kernels, project(): pl.pallas_call(body, grid=(cells,), in_specs=[smem(), whole(field.shape),...  13.6 us
  transfers between devices with their start and end apart: 23, of which 18 were waited for; matrix products, arithmetic and copies ran while one was open for 3% of the time, Pallas kernels for 5%

profile of v3, /device:TPU:0, one launch (start us, length us, event | category | flops | bytes accessed | tf_op | source)
XLA Modules:
  0.0 575.5 jit_solution(9391088838698932261)
XLA Ops:
  2.1 7.3 %all-to-all-start.8 = ((s32[32,1,160]{2,1,0:T(1,128)}), s32[32,1,160]{2,1,0:T(1,128)S(1)}, u32[]{:S(2)}, u32[]{:S(2)}) async-start(s32[32,1,160]{2,1,0:T(1,128)} %broadcast_in_dim.201), calls=%async_computation.8 | async-start | bytes 65536 | tf_op jit(solution)/shard_map/all_to_all | solution.py:395
  26.8 11.0 %canonical.1 = (bf16[8,512,512]{2,1,0:T(8,128)(2,1)}, bf16[8,512,512]{2,1,0:T(8,128)(2,1)}, bf16[8,512,512]{2,1,0:T(8,128)(2,1)}) custom-call(s32[8,1,512]{2,1,0:T(1,128)S(1)} %fusion.31.place_ref, bf16[8,512,512]{2,1,0:T(8,128)(2,1)S(1)} %bitcast.168, bf16[8,512,512]{2,1,0:T(8,128)(2,1)S(1)} %bitcast.169), custom_call_target="tpu_custom_call" | custom-call | tf_op jit(solution)/shard_map/canonical/pallas_call | solution.py:67
  47.4 3.7 convert_bitcast_fusion
  51.2 520.4 %conditional.2 = (f32[15,29,8,256]{3,2,1,0:T(8,128)}) conditional(s32[]{:T(128)} %convert_element_type.194, (s32[128]{0:T(128)S(1)}, s32[128]{0:T(128)S(1)}, s32[16,16]{1,0:T(8,128)S(1)}, bf16[8,512,512]{2,1,0:T(8,128)(2,1)}, bf16[8,512,512]{2,1,0:T(8,128)(2,1)}, /*index=5*/s32[256]{0:T(256)S(1)}, s32[16]{0:T(128)S(1)}, s32[64]{0:T(128)S(1)}, ...), branch_computations={%region_11.14_spmd, %region_14.15_spmd} | conditional | flops 39332880 | bytes 545557824
  51.5 7.4 %project.8 = (bf16[8,512,256]{2,1,0:T(8,128)(2,1)S(1)}, bf16[864,8,256]{2,1,0:T(8,128)(2,1)S(1)}) custom-call(s32[128]{0:T(128)S(1)} %multiply_add_fusion.1.starts_ref, f32[15,29,8,256]{3,2,1,0:T(8,128)} %get-tuple-element.331.field_ref, bf16[8,512,512]{2,1,0:T(8,128)(2,1)} %get-tuple-element.332.straight_ref), custom_call_target="tpu_custom_call" | custom-call | tf_op jit(solution)/shard_map/cond/branch_1_fun/project/pallas_call | solution.py:140
  62.1 3.8 all-to-all-start
  68.9 6.0 %stiffen.4.refs_0_.begun_ref = f32[15,29,8,256]{3,2,1,0:T(8,128)S(1)} custom-call(bf16[8,512,512]{2,1,0:T(8,128)(2,1)} %get-tuple-element.334.stiff_ref, bf16[8,512,256]{2,1,0:T(8,128)(2,1)S(1)} %copy-done.22), custom_call_target="tpu_custom_call" | custom-call | tf_op jit(solution)/shard_map/cond/branch_1_fun/stiffen/pallas_call | solution.py:180
  76.7 33.7 %all-to-all-done.incoming_ref = bf16[864,8,256]{2,1,0:T(8,128)(2,1)S(1)} async-done(((bf16[864,8,256]{2,1,0:T(8,128)(2,1)}), bf16[864,8,256]{2,1,0:T(8,128)(2,1)S(1)}, u32[]{:S(2)}, u32[]{:S(2)}) %all-to-all-start) | async-done | bytes 3538976 | tf_op jit(solution)/shard_map/cond/branch_1_fun/all_to_all | solution.py:383
  116.7 34.5 %collective-permute-done.others_ref = bf16[188,8,256]{2,1,0:T(8,128)(2,1)S(1)} collective-permute-done((bf16[188,8,256]{2,1,0:T(8,128)(2,1)S(1)}, bf16[188,8,256]{2,1,0:T(8,128)(2,1)S(1)}, u32[]{:S(2)}, u32[]{:S(2)}) %collective-permute-start) | collective-permute-done | bytes 770080 | tf_op jit(solution)/shard_map/cond/branch_1_fun/ppermute | solution.py:33
  154.7 45.0 %all_to_all.45.answers_ref = bf16[864,8,256]{2,1,0:T(8,128)(2,1)S(1)} all-to-all(bf16[864,8,256]{2,1,0:T(8,128)(2,1)S(1)} %couple.4.refs_0_), channel_id=1, replica_groups={{0,1,2,3,8,9,10,11,16,17,18,19,24,25,26,27},{4,5,6,7,12,13,14,15,20,21,..., dimensions={0} | all-to-all | bytes 7077888 | tf_op jit(solution)/shard_map/cond/branch_1_fun/all_to_all | solution.py:383
  205.2 4.2 collective-permute-start.2
  209.4 5.8 %collective-permute-done.1 = bf16[15,29,256]{2,0,1:T(8,128)(2,1)S(1)} collective-permute-done((bf16[15,29,256]{2,0,1:T(8,128)(2,1)S(1)}, bf16[15,29,256]{2,0,1:T(8,128)(2,1)S(1)}, u32[]{:S(2)}, u32[]{:S(2)}) %collective-permute-start.1) | collective-permute-done | bytes 222752 | tf_op jit(solution)/shard_map/cond/branch_1_fun/ppermute | solution.py:33
  233.6 3.8 all-to-all-start.2
  239.0 6.0 %stiffen.5.refs_0_.begun_ref = f32[15,29,8,256]{3,2,1,0:T(8,128)S(1)} custom-call(bf16[8,512,512]{2,1,0:T(8,128)(2,1)} %get-tuple-element.334.stiff_ref, bf16[8,512,256]{2,1,0:T(8,128)(2,1)S(1)} %copy-done.24), custom_call_target="tpu_custom_call" | custom-call | tf_op jit(solution)/shard_map/cond/branch_1_fun/stiffen/pallas_call | solution.py:180
  246.8 35.1 %all-to-all-done.2.incoming_ref = bf16[864,8,256]{2,1,0:T(8,128)(2,1)S(1)} async-done(((bf16[864,8,256]{2,1,0:T(8,128)(2,1)}), bf16[864,8,256]{2,1,0:T(8,128)(2,1)S(1)}, u32[]{:S(2)}, u32[]{:S(2)}) %all-to-all-start.2) | async-done | bytes 3538976 | tf_op jit(solution)/shard_map/cond/branch_1_fun/all_to_all | solution.py:383
  289.2 33.6 %collective-permute-done.5.others_ref = bf16[188,8,256]{2,1,0:T(8,128)(2,1)S(1)} collective-permute-done((bf16[188,8,256]{2,1,0:T(8,128)(2,1)S(1)}, bf16[188,8,256]{2,1,0:T(8,128)(2,1)S(1)}, u32[]{:S(2)}, u32[]{:S(2)}) %collective-permute-start.5) | collective-permute-done | bytes 770080 | tf_op jit(solution)/shard_map/cond/branch_1_fun/ppermute | solution.py:33
  326.3 45.0 %all_to_all.46.answers_ref = bf16[864,8,256]{2,1,0:T(8,128)(2,1)S(1)} all-to-all(bf16[864,8,256]{2,1,0:T(8,128)(2,1)S(1)} %couple.5.refs_0_), channel_id=1, replica_groups={{0,1,2,3,8,9,10,11,16,17,18,19,24,25,26,27},{4,5,6,7,12,13,14,15,20,21,..., dimensions={0} | all-to-all | bytes 7077888 | tf_op jit(solution)/shard_map/cond/branch_1_fun/all_to_all | solution.py:383
  380.3 6.4 %collective-permute-done.6 = bf16[15,29,256]{2,0,1:T(8,128)(2,1)S(1)} collective-permute-done((bf16[15,29,256]{2,0,1:T(8,128)(2,1)S(1)}, bf16[15,29,256]{2,0,1:T(8,128)(2,1)S(1)}, u32[]{:S(2)}, u32[]{:S(2)}) %collective-permute-start.6) | collective-permute-done | bytes 222752 | tf_op jit(solution)/shard_map/cond/branch_1_fun/ppermute | solution.py:33
  404.5 3.8 all-to-all-start.4
  409.8 6.0 %stiffen.6.refs_0_.begun_ref = f32[15,29,8,256]{3,2,1,0:T(8,128)S(1)} custom-call(bf16[8,512,512]{2,1,0:T(8,128)(2,1)} %get-tuple-element.334.stiff_ref, bf16[8,512,256]{2,1,0:T(8,128)(2,1)S(1)} %copy-done.26), custom_call_target="tpu_custom_call" | custom-call | tf_op jit(solution)/shard_map/cond/branch_1_fun/stiffen/pallas_call | solution.py:180
  417.7 35.1 %all-to-all-done.4.incoming_ref = bf16[864,8,256]{2,1,0:T(8,128)(2,1)S(1)} async-done(((bf16[864,8,256]{2,1,0:T(8,128)(2,1)}), bf16[864,8,256]{2,1,0:T(8,128)(2,1)S(1)}, u32[]{:S(2)}, u32[]{:S(2)}) %all-to-all-start.4) | async-done | bytes 3538976 | tf_op jit(solution)/shard_map/cond/branch_1_fun/all_to_all | solution.py:383
  460.8 33.5 %collective-permute-done.10.others_ref = bf16[188,8,256]{2,1,0:T(8,128)(2,1)S(1)} collective-permute-done((bf16[188,8,256]{2,1,0:T(8,128)(2,1)S(1)}, bf16[188,8,256]{2,1,0:T(8,128)(2,1)S(1)}, u32[]{:S(2)}, u32[]{:S(2)}) %collective-permute-start.10) | collective-permute-done | bytes 770080 | tf_op jit(solution)/shard_map/cond/branch_1_fun/ppermute | solution.py:33
  497.7 45.1 %all_to_all.47.answers_ref = bf16[864,8,256]{2,1,0:T(8,128)(2,1)S(1)} all-to-all(bf16[864,8,256]{2,1,0:T(8,128)(2,1)S(1)} %couple.6.refs_0_), channel_id=1, replica_groups={{0,1,2,3,8,9,10,11,16,17,18,19,24,25,26,27},{4,5,6,7,12,13,14,15,20,21,..., dimensions={0} | all-to-all | bytes 7077888 | tf_op jit(solution)/shard_map/cond/branch_1_fun/all_to_all | solution.py:383
  551.9 6.4 %collective-permute-done.11 = bf16[15,29,256]{2,0,1:T(8,128)(2,1)S(1)} collective-permute-done((bf16[15,29,256]{2,0,1:T(8,128)(2,1)S(1)}, bf16[15,29,256]{2,0,1:T(8,128)(2,1)S(1)}, u32[]{:S(2)}, u32[]{:S(2)}) %collective-permute-start.11) | collective-permute-done | bytes 222752 | tf_op jit(solution)/shard_map/cond/branch_1_fun/ppermute | solution.py:33
  (286 shorter events, 150.0 us)
Async XLA Ops:
  2.1 35.7 %all-to-all-start.8 = ((s32[32,1,160]{2,1,0:T(1,128)}), s32[32,1,160]{2,1,0:T(1,128)S(1)}, u32[]{:S(2)}, u32[]{:S(2)}) async-start(s32[32,1,160]{2,1,0:T(1,128)} %broadcast_in_dim.201), calls=%async_computation.8 | async-start | bytes 65536 | tf_op jit(solution)/shard_map/all_to_all | solution.py:395
  10.6 34.2 %collective-permute-start.20 = (f32[256,128]{1,0:T(8,128)S(1)}, f32[256,128]{1,0:T(8,128)S(1)}, u32[]{:S(2)}, u32[]{:S(2)}) collective-permute-start(f32[256,128]{1,0:T(8,128)S(1)} %reshape.433), channel_id=1, source_target_pairs={{0,4},{1,5},{2,6},{3,7},{4,0},{5,1},{6,2},{7,3},{8,12},{9,13},{10,... | collective-permute-start | bytes 393224 | tf_op jit(solution)/shard_map/ppermute | solution.py:33
  16.8 30.6 %collective-permute-start.21 = (bf16[14,1,29,256]{3,1,2,0:T(2,128)(2,1)}, bf16[14,1,29,256]{3,1,2,0:T(2,128)(2,1)}, u32[]{:S(2)}, u32[]{:S(2)}) collective-permute-start(bf16[14,1,29,256]{3,1,2,0:T(2,128)(2,1)} %slice.145), channel_id=1, source_target_pairs={{0,7},{1,0},{2,1},{3,2},{4,3},{5,4},{6,5},{7,6},{8,15},{9,8},{10,9... | collective-permute-start | bytes 623624 | tf_op jit(solution)/shard_map/ppermute | solution.py:33
  19.8 27.6 %collective-permute-start.22 = (bf16[1,7,29,256]{3,1,2,0:T(8,128)(2,1)}, bf16[1,7,29,256]{3,1,2,0:T(8,128)(2,1)}, u32[]{:S(2)}, u32[]{:S(2)}) collective-permute-start(bf16[1,7,29,256]{3,1,2,0:T(8,128)(2,1)} %slice.146), channel_id=1, source_target_pairs={{0,24},{8,0},{16,8},{24,16},{1,25},{9,1},{17,9},{25,17},{2,26},{10... | collective-permute-start | bytes 311816 | tf_op jit(solution)/shard_map/ppermute | solution.py:33
  21.1 26.4 %collective-permute-start.23 = (bf16[1,1,29,256]{3,1,2,0:T(2,128)(2,1)}, bf16[1,1,29,256]{3,1,2,0:T(2,128)(2,1)S(1)}, u32[]{:S(2)}, u32[]{:S(2)}) collective-permute-start(bf16[1,1,29,256]{3,1,2,0:T(2,128)(2,1)} %slice.147), channel_id=1, source_target_pairs={{0,31},{1,24},{2,25},{3,26},{4,27},{5,28},{6,29},{7,30},{8,7},{9,0... | collective-permute-start | bytes 44552 | tf_op jit(solution)/shard_map/ppermute | solution.py:33
  62.1 48.3 %all-to-all-start = ((bf16[864,8,256]{2,1,0:T(8,128)(2,1)}), bf16[864,8,256]{2,1,0:T(8,128)(2,1)S(1)}, u32[]{:S(2)}, u32[]{:S(2)}) async-start(bf16[864,8,256]{2,1,0:T(8,128)(2,1)} %copy-done.18), calls=%async_computation | async-start | bytes 7077888 | tf_op jit(solution)/shard_map/cond/branch_1_fun/all_to_all | solution.py:383
  115.2 36.1 %collective-permute-start = (bf16[188,8,256]{2,1,0:T(8,128)(2,1)S(1)}, bf16[188,8,256]{2,1,0:T(8,128)(2,1)S(1)}, u32[]{:S(2)}, u32[]{:S(2)}) collective-permute-start(bf16[188,8,256]{2,1,0:T(8,128)(2,1)S(1)} %get-tuple-element.337), channel_id=1, source_target_pairs={{0,4},{1,5},{2,6},{3,7},{4,0},{5,1},{6,2},{7,3},{8,12},{9,13},{10,... | collective-permute-start | bytes 2310152 | tf_op jit(solution)/shard_map/cond/branch_1_fun/ppermute | solution.py:33
  203.9 11.2 %collective-permute-start.1 = (bf16[15,29,256]{2,0,1:T(8,128)(2,1)S(1)}, bf16[15,29,256]{2,0,1:T(8,128)(2,1)S(1)}, u32[]{:S(2)}, u32[]{:S(2)}) collective-permute-start(bf16[15,29,256]{2,0,1:T(8,128)(2,1)S(1)} %bitcast.178), channel_id=1, source_target_pairs={{0,1},{1,2},{2,3},{3,4},{4,5},{5,6},{6,7},{7,0},{8,9},{9,10},{10,1... | collective-permute-start | bytes 668168 | tf_op jit(solution)/shard_map/cond/branch_1_fun/ppermute | solution.py:33
  205.2 13.0 %collective-permute-start.2 = (bf16[15,29,256]{2,0,1:T(8,128)(2,1)S(1)}, bf16[15,29,256]{2,0,1:T(8,128)(2,1)S(1)}, u32[]{:S(2)}, u32[]{:S(2)}) collective-permute-start(bf16[15,29,256]{2,0,1:T(8,128)(2,1)S(1)} %bitcast.179), channel_id=1, source_target_pairs={{0,7},{1,0},{2,1},{3,2},{4,3},{5,4},{6,5},{7,6},{8,15},{9,8},{10,9... | collective-permute-start | bytes 668168 | tf_op jit(solution)/shard_map/cond/branch_1_fun/ppermute | solution.py:33
  219.7 3.1 collective-permute-start.4
  219.9 5.1 collective-permute-start.3
  233.6 48.3 %all-to-all-start.2 = ((bf16[864,8,256]{2,1,0:T(8,128)(2,1)}), bf16[864,8,256]{2,1,0:T(8,128)(2,1)S(1)}, u32[]{:S(2)}, u32[]{:S(2)}) async-start(bf16[864,8,256]{2,1,0:T(8,128)(2,1)} %copy-done.19), calls=%async_computation.2 | async-start | bytes 7077888 | tf_op jit(solution)/shard_map/cond/branch_1_fun/all_to_all | solution.py:383
  286.8 36.1 %collective-permute-start.5 = (bf16[188,8,256]{2,1,0:T(8,128)(2,1)S(1)}, bf16[188,8,256]{2,1,0:T(8,128)(2,1)S(1)}, u32[]{:S(2)}, u32[]{:S(2)}) collective-permute-start(bf16[188,8,256]{2,1,0:T(8,128)(2,1)S(1)} %get-tuple-element.343), channel_id=1, source_target_pairs={{0,4},{1,5},{2,6},{3,7},{4,0},{5,1},{6,2},{7,3},{8,12},{9,13},{10,... | collective-permute-start | bytes 2310152 | tf_op jit(solution)/shard_map/cond/branch_1_fun/ppermute | solution.py:33
  375.5 11.2 %collective-permute-start.6 = (bf16[15,29,256]{2,0,1:T(8,128)(2,1)S(1)}, bf16[15,29,256]{2,0,1:T(8,128)(2,1)S(1)}, u32[]{:S(2)}, u32[]{:S(2)}) collective-permute-start(bf16[15,29,256]{2,0,1:T(8,128)(2,1)S(1)} %bitcast.182), channel_id=1, source_target_pairs={{0,1},{1,2},{2,3},{3,4},{4,5},{5,6},{6,7},{7,0},{8,9},{9,10},{10,1... | collective-permute-start | bytes 668168 | tf_op jit(solution)/shard_map/cond/branch_1_fun/ppermute | solution.py:33
  376.6 12.4 %collective-permute-start.7 = (bf16[15,29,256]{2,0,1:T(8,128)(2,1)S(1)}, bf16[15,29,256]{2,0,1:T(8,128)(2,1)S(1)}, u32[]{:S(2)}, u32[]{:S(2)}) collective-permute-start(bf16[15,29,256]{2,0,1:T(8,128)(2,1)S(1)} %bitcast.180), channel_id=1, source_target_pairs={{0,7},{1,0},{2,1},{3,2},{4,3},{5,4},{6,5},{7,6},{8,15},{9,8},{10,9... | collective-permute-start | bytes 668168 | tf_op jit(solution)/shard_map/cond/branch_1_fun/ppermute | solution.py:33
  390.7 3.1 collective-permute-start.9
  390.7 5.2 collective-permute-start.8
  404.5 48.3 %all-to-all-start.4 = ((bf16[864,8,256]{2,1,0:T(8,128)(2,1)}), bf16[864,8,256]{2,1,0:T(8,128)(2,1)S(1)}, u32[]{:S(2)}, u32[]{:S(2)}) async-start(bf16[864,8,256]{2,1,0:T(8,128)(2,1)} %copy-done.20), calls=%async_computation.4 | async-start | bytes 7077888 | tf_op jit(solution)/shard_map/cond/branch_1_fun/all_to_all | solution.py:383
  457.6 36.6 %collective-permute-start.10 = (bf16[188,8,256]{2,1,0:T(8,128)(2,1)S(1)}, bf16[188,8,256]{2,1,0:T(8,128)(2,1)S(1)}, u32[]{:S(2)}, u32[]{:S(2)}) collective-permute-start(bf16[188,8,256]{2,1,0:T(8,128)(2,1)S(1)} %get-tuple-element.347), channel_id=1, source_target_pairs={{0,4},{1,5},{2,6},{3,7},{4,0},{5,1},{6,2},{7,3},{8,12},{9,13},{10,... | collective-permute-start | bytes 2310152 | tf_op jit(solution)/shard_map/cond/branch_1_fun/ppermute | solution.py:33
  494.3 48.6 %copy-start.34 = (bf16[8,512,512]{2,1,0:T(8,128)(2,1)S(1)}, bf16[8,512,512]{2,1,0:T(8,128)(2,1)}, u32[]{:S(2)}) copy-start(bf16[8,512,512]{2,1,0:T(8,128)(2,1)} %get-tuple-element.325.turned_ref) | copy-start | bytes 12582916 | tf_op jit(solution)/shard_map/conditional
  547.0 11.2 %collective-permute-start.11 = (bf16[15,29,256]{2,0,1:T(8,128)(2,1)S(1)}, bf16[15,29,256]{2,0,1:T(8,128)(2,1)S(1)}, u32[]{:S(2)}, u32[]{:S(2)}) collective-permute-start(bf16[15,29,256]{2,0,1:T(8,128)(2,1)S(1)} %bitcast.183), channel_id=1, source_target_pairs={{0,1},{1,2},{2,3},{3,4},{4,5},{5,6},{6,7},{7,0},{8,9},{9,10},{10,1... | collective-permute-start | bytes 668168 | tf_op jit(solution)/shard_map/cond/branch_1_fun/ppermute | solution.py:33
  548.2 12.4 %collective-permute-start.12 = (bf16[15,29,256]{2,0,1:T(8,128)(2,1)S(1)}, bf16[15,29,256]{2,0,1:T(8,128)(2,1)S(1)}, u32[]{:S(2)}, u32[]{:S(2)}) collective-permute-start(bf16[15,29,256]{2,0,1:T(8,128)(2,1)S(1)} %bitcast.181), channel_id=1, source_target_pairs={{0,7},{1,0},{2,1},{3,2},{4,3},{5,4},{6,5},{7,6},{8,15},{9,8},{10,9... | collective-permute-start | bytes 668168 | tf_op jit(solution)/shard_map/cond/branch_1_fun/ppermute | solution.py:33
  562.3 3.1 collective-permute-start.14
  562.4 5.1 collective-permute-start.13
  (66 other events, 1179.9 us)

commit v4 on v3

--- a/solution.py
+++ b/solution.py
@@ -2,6 +2,7 @@
 
 import jax
 import jax.numpy as jnp
+import numpy as np
 from jax import lax
 from jax.experimental import pallas as pl
 from jax.experimental.pallas import tpu as pltpu
@@ -11,8 +12,9 @@
 FILTER_DEGREE = 3
 PARTS = 1
 UNIT = 8
-TIGHT = 54
-NARROW = 188
+TIGHT = 47
+NARROW = 172
+TURNS = 4
 MODE = "cond"
 GRANT = 20 * 1024 * 1024
 GROUP = 8
@@ -87,12 +89,13 @@
     )(places.reshape(cells, 1, nodes), matrices, shapes)
 
 
-def spread(mixers):
+def spread(mixers, after):
     atoms, per_atom, _ = mixers.shape
     groups = atoms // GROUP
     edge = GROUP * per_atom
 
-    def body(mixers_ref, high_ref, low_ref):
+    def body(mixers_ref, *refs):
+        high_ref, low_ref = refs[len(after) :]
         rows = lax.broadcasted_iota(jnp.int32, (edge, edge), 0) // per_atom
         columns = lax.broadcasted_iota(jnp.int32, (edge, edge), 1) // per_atom
         for g in range(groups):
@@ -106,12 +109,12 @@
     vmem = pl.BlockSpec(memory_space=pltpu.VMEM)
     return pl.pallas_call(
         body,
-        in_specs=[vmem],
+        in_specs=[vmem] + unread(after),
         out_specs=[vmem, vmem],
         out_shape=[jax.ShapeDtypeStruct((groups, edge, edge), BF16)] * 2,
         compiler_params=pltpu.CompilerParams(vmem_limit_bytes=GRANT),
         name="spread",
-    )(mixers)
+    )(mixers, *after)
 
 
 def project(field, straight, starts, room, cz, per_atom):
@@ -401,8 +404,6 @@
     at_inner = (inner[:, :, None] == jnp.arange(home_atoms)).astype(BF16)
     picked = jnp.einsum("seh,hi->sei", at_home, needs.astype(BF16), preferred_element_type=F32)
     sizes = jnp.sum(picked * at_inner.astype(F32), axis=2).astype(jnp.int32)
-    collectors = homes // n_gy * half + homes_y % half
-    held = homes_y // half * home_atoms + inner
 
     def by_half(x):
         return x.reshape((n_gx, 2, half) + x.shape[1:])
@@ -417,12 +418,41 @@
         for h in range(2)
     ]
     common = ((split[0] > 0) & (split[1] > 0)).astype(jnp.int32)
-    at_collector = collectors[:, :, None] == jnp.arange(senders)
-    loads = jnp.sum(jnp.where(at_collector, sizes[:, :, None], 0), axis=1)
-    crossing = jnp.sum(by_half(common * needs), axis=(1, 3))
-    fits = (jnp.max(loads) + units - 1 <= TIGHT * each * units // 64) & (
-        jnp.max(crossing) + units <= NARROW * atoms * units // 256
+
+    order = jnp.arange(entries)[None, :, None]
+    present = homes[:, :, None] == jnp.arange(devices)
+    sized = sizes[:, :, None]
+    loads = jnp.sum(jnp.where(present, sized, 0), axis=1)
+    ends = jnp.max(jnp.where(present, order * (2 * units) + sized, 0), axis=1)
+    crossing = jnp.sum(common * needs, axis=1)
+    table = jnp.concatenate([loads, ends, crossing[None]], axis=0).astype(F32)
+    table = table.reshape(2 * devices + 1, n_gx, 2, half)
+    lower = table[:, :, 0].reshape(-1, 1, senders)
+    turned_to = np.zeros((senders, TURNS * TURNS, senders), np.float32)
+    for j, k, p, r in itertools.product(range(TURNS), range(TURNS), range(n_gx), range(half)):
+        source = (p + j) % n_gx * half + (r + k) % half
+        turned_to[source, j * TURNS + k, p * half + r] = 1.0
+    upper = jnp.einsum(
+        "ah,hcg->acg",
+        table[:, :, 1].reshape(-1, senders),
+        jnp.asarray(turned_to),
+        precision=lax.Precision.HIGHEST,
     )
+    tail = jnp.maximum(lower, upper)[devices : 2 * devices].astype(jnp.int32) % (2 * units)
+    joint = (lower + upper).astype(jnp.int32)
+    cap = TIGHT * each * units // 64
+    span = NARROW * atoms * units // 256
+    fullest = jnp.max(joint[:devices] - tail + units, axis=(0, 2))
+    widest = jnp.max(joint[-1] + units, axis=1)
+    scores = jnp.maximum(fullest * span, widest * cap)
+    best = jnp.argmin(scores).astype(jnp.int32)
+    fits = jnp.min(scores) <= cap * span
+    turn_x, turn_y = best // TURNS, best % TURNS
+    over = homes_y // half
+    held = over * home_atoms + inner
+    places_x = (homes // n_gy - turn_x * over) % n_gx
+    places_y = (homes_y % half - turn_y * over) % half
+    collectors = places_x * half + places_y
 
     def of_me(x):
         return lax.dynamic_index_in_dim(x, me, 0, keepdims=False)
@@ -432,8 +462,10 @@
         return x.reshape((senders,) + x.shape[2:])
 
     def hosted(x):
-        x = lax.dynamic_index_in_dim(by_half(x), my_x, 0, keepdims=False)
-        return lax.dynamic_index_in_dim(x, my_place, 1, keepdims=False).reshape(atoms)
+        first = my_x * n_gy + my_place
+        second = (my_x + turn_x) % n_gx * n_gy + half + (my_place + turn_y) % half
+        rows = [lax.dynamic_index_in_dim(x, at, 0, keepdims=False) for at in (first, second)]
+        return jnp.concatenate(rows)
 
     before = jnp.arange(entries)[:, None] < jnp.arange(entries)[None, :]
     own, used = of_me(collectors), of_me(sizes)
@@ -453,15 +485,20 @@
     upto = jnp.arange(atoms)[:, None] < jnp.arange(atoms)[None, :]
     spots = jnp.sum(jnp.where(upto, moved[:, None], 0), axis=0)
 
-    partner = shifted(coupling.reshape(-1, 128), ("gy",), (half,)).reshape(coupling.shape)
-    mixers = jnp.where(
-        my_half > 0,
-        jnp.concatenate([partner, coupling], axis=0),
-        jnp.concatenate([coupling, partner], axis=0),
-    )
+    flat = coupling.reshape(-1, 128)
+    partner = shifted(flat, ("gy",), (half,))
+    lower_mix = jnp.where(my_half > 0, partner, flat)
+    upper_mix = jnp.where(my_half > 0, flat, partner)
+    choices = [upper_mix] + [shifted(upper_mix, ("gx",), (-j,)) for j in range(1, TURNS)]
+    upper_mix = lax.select_n(turn_x, *choices)
+    choices = [upper_mix]
+    for k in range(1, TURNS):
+        pairs = [(h * half + (r + k) % half, h * half + r) for h in range(2) for r in range(half)]
+        choices.append(lax.ppermute(upper_mix, "gy", pairs))
+    upper_mix = lax.select_n(turn_y, *choices)
+    mixers = jnp.concatenate([lower_mix, upper_mix], axis=0).reshape(atoms, per_atom, per_atom)
     active = (jnp.arange(per_atom)[None, :] < hosted(counts)[:, None]).astype(F32)
     mixers = mixers * active[:, :, None] * active[:, None, :]
-    mix_high, mix_low = spread(mixers)
 
     cell_ids = jnp.arange(cells, dtype=jnp.int32)[:, None]
     node_w = node_map % layers - cell_ids % cz * deg
@@ -483,12 +520,14 @@
     grid = jnp.transpose(widened, (0, 2, 1, 3)).astype(F32)
     extended = grid.shape[:3]
 
-    def advance(field, older, cap, span):
+    def advance(field, older, mixing, cap, span):
         room = senders * cap
         starts = own * cap + offsets
         begins = (places_in + jnp.arange(senders)[:, None] * cap).reshape(slots)
         tables = (ids, begins, filled, spots, shared)
         local, *outgoing = project(field, straight, starts, room, cz, per_atom)
+        if mixing is None:
+            mixing = spread(mixers, (local,))
         image = stiffen(stiff, local, extended, cz)
         after = (image,)
         gathered = []
@@ -499,9 +538,7 @@
         answers = []
         for sums, sent in gathered:
             others = shifted(sent, ("gy",), (half,))
-            replies = couple(
-                sums, others, mix_high, mix_low, tables, units, room, after
-            )
+            replies = couple(sums, others, *mixing, tables, units, room, after)
             answers.append(exchange(replies))
             after = (replies,)
         totals = []
@@ -511,23 +548,22 @@
             )
             after = (totals[-1],)
         image = completed(jnp.concatenate(totals, axis=-1) if PARTS > 1 else totals[0])
-        return image if older is None else 2.0 * image - older
+        return image if older is None else 2.0 * image - older, mixing
 
     def packed():
-        cap = TIGHT * each * units // 64
-        span = NARROW * atoms * units // 256
+        mixing = None
         older, field = None, grid
         for _ in range(FILTER_DEGREE):
-            older, field = field, advance(field, older, cap, span)
+            image, mixing = advance(field, older, mixing, cap, span)
+            older, field = field, image
         return field[:span_x, :, :span_y].astype(BF16)
 
     def roomy():
-        cap = (each + 1) * units
-        span = (atoms + 1) * units
+        mixing = spread(mixers, ())
 
         def step(at, fields):
             older, field = fields
-            image = advance(field, None, cap, span)
+            image, _ = advance(field, None, mixing, (each + 1) * units, (atoms + 1) * units)
             return field, jnp.where(at == 0, image, 2.0 * image - older)
 
         fields = (jnp.zeros_like(grid), grid)

time: 583 us -> 556 us (0.954)
  waiting for transfers between devices: 244 us -> 227 us
  blocking collectives: 135 us -> 120 us
    all_to_all x3, waiting for transfers between devices: 104 us -> 88.5 us  [exchange(): lax.all_to_all(x, both, split_axis=0, concat_axis=0, axis_index_groups=te...]
    all_to_all x3, blocking collectives: 135 us -> 120 us  [exchange(): lax.all_to_all(x, both, split_axis=0, concat_axis=0, axis_index_groups=te...]
    ppermute x19 -> x22, waiting for transfers between devices: 140 us -> 135 us  [shifted(): return lax.ppermute(x, axes if len(axes) > 1 else axes[0], pairs)]
    ppermute x19 -> x22, starting transfers between devices: 30.5 us -> 33.1 us  [shifted(): return lax.ppermute(x, axes if len(axes) > 1 else axes[0], pairs)]
    another operation x128 -> x104, local copies, waits for them, and re-layouts: 27.7 us -> 30.2 us
  transfers between devices with their start and end apart: 23 -> 29, of which waited for: 18 -> 23; matrix products, arithmetic and copies ran while one was open for 3% -> 3% of each run, Pallas kernels for 5% -> 5%
where the time goes in v4:
time: 556 us; the launch traced here: 548 us
  waiting for transfers between devices  227 us (41%)
  blocking collectives  120 us (22%)
  Pallas kernels  69.7 us (13%)
  starting transfers between devices  54.5 us (10%)
  local copies, waits for them, and re-layouts  50.7 us (9%)
  other arithmetic  19.7 us (4%)
    ppermute x22, waiting for transfers between devices, shifted(): return lax.ppermute(x, axes if len(axes) > 1 else axes[0], pairs)  135 us
    all_to_all x3, blocking collectives, exchange(): lax.all_to_all(x, both, split_axis=0, concat_axis=0, axis_index_groups=te...  120 us
    all_to_all x3, waiting for transfers between devices, exchange(): lax.all_to_all(x, both, split_axis=0, concat_axis=0, axis_index_groups=te...  88.5 us
    ppermute x22, starting transfers between devices, shifted(): return lax.ppermute(x, axes if len(axes) > 1 else axes[0], pairs)  33.1 us
    another operation x104, local copies, waits for them, and re-layouts  30.2 us
    pallas_call x3, Pallas kernels, stiffen(): pl.pallas_call(body, grid=(cells,), in_specs=[pl.BlockSpec((1, nodes, nod...  18.1 us
    pallas_call x3, Pallas kernels, project(): pl.pallas_call(body, grid=(cells,), in_specs=[smem(), whole(field.shape),...  13.2 us
    all_to_all x3, starting transfers between devices, exchange(): lax.all_to_all(x, both, split_axis=0, concat_axis=0, axis_index_groups=te...  11.4 us
  transfers between devices with their start and end apart: 29, of which 23 were waited for; matrix products, arithmetic and copies ran while one was open for 3% of the time, Pallas kernels for 5%

profile of v4, /device:TPU:0, one launch (start us, length us, event | category | flops | bytes accessed | tf_op | source)
XLA Modules:
  0.0 548.4 jit_solution(4026207328631618630)
XLA Ops:
  2.1 7.3 %all-to-all-start.8 = ((s32[32,1,160]{2,1,0:T(1,128)}), s32[32,1,160]{2,1,0:T(1,128)S(1)}, u32[]{:S(2)}, u32[]{:S(2)}) async-start(s32[32,1,160]{2,1,0:T(1,128)} %broadcast_in_dim.210), calls=%async_computation.8 | async-start | bytes 65536 | tf_op jit(solution)/shard_map/all_to_all | solution.py:398
  25.1 11.0 %canonical.1 = (bf16[8,512,512]{2,1,0:T(8,128)(2,1)}, bf16[8,512,512]{2,1,0:T(8,128)(2,1)}, bf16[8,512,512]{2,1,0:T(8,128)(2,1)}) custom-call(s32[8,1,512]{2,1,0:T(1,128)S(1)} %fusion.25.place_ref, bf16[8,512,512]{2,1,0:T(8,128)(2,1)S(1)} %bitcast.188, bf16[8,512,512]{2,1,0:T(8,128)(2,1)S(1)} %bitcast.189), custom_call_target="tpu_custom_call" | custom-call | tf_op jit(solution)/shard_map/canonical/pallas_call | solution.py:69
  64.0 480.4 %conditional.2 = (f32[15,29,8,256]{3,2,1,0:T(8,128)}) conditional(s32[]{:T(128)} %convert_element_type.212, (f32[64,32,32]{2,1,0:T(8,128)S(1)}, s32[128]{0:T(128)S(1)}, s32[128]{0:T(128)S(1)}, s32[16,16]{1,0:T(8,128)S(1)}, bf16[8,512,512]{2,1,0:T(8,128)(2,1)}, /*index=5*/bf16[8,512,512]{2,1,0:T(8,128)(2,1)}, s32[256]{0:T(256)S(1)}, ...), branch_computations={%region_13.16_spmd, %region_16.17_spmd} | conditional | flops 39332880 | bytes 535093760
  65.5 7.0 %project.8 = (bf16[8,512,256]{2,1,0:T(8,128)(2,1)S(1)}, bf16[752,8,256]{2,1,0:T(8,128)(2,1)S(1)}) custom-call(s32[128]{0:T(128)S(1)} %multiply_add_fusion.1.starts_ref, f32[15,29,8,256]{3,2,1,0:T(8,128)} %get-tuple-element.328.field_ref, bf16[8,512,512]{2,1,0:T(8,128)(2,1)} %get-tuple-element.329.straight_ref), custom_call_target="tpu_custom_call" | custom-call | tf_op jit(solution)/shard_map/cond/branch_1_fun/project/pallas_call | solution.py:143
  75.5 3.7 all-to-all-start
  81.1 6.0 %stiffen.4.refs_0_.begun_ref = f32[15,29,8,256]{3,2,1,0:T(8,128)S(1)} custom-call(bf16[8,512,512]{2,1,0:T(8,128)(2,1)} %get-tuple-element.331.stiff_ref, bf16[8,512,256]{2,1,0:T(8,128)(2,1)S(1)} %copy-done.23), custom_call_target="tpu_custom_call" | custom-call | tf_op jit(solution)/shard_map/cond/branch_1_fun/stiffen/pallas_call | solution.py:183
  89.0 29.4 %all-to-all-done.incoming_ref = bf16[752,8,256]{2,1,0:T(8,128)(2,1)S(1)} async-done(((bf16[752,8,256]{2,1,0:T(8,128)(2,1)}), bf16[752,8,256]{2,1,0:T(8,128)(2,1)S(1)}, u32[]{:S(2)}, u32[]{:S(2)}) %all-to-all-start) | async-done | bytes 3080224 | tf_op jit(solution)/shard_map/cond/branch_1_fun/all_to_all | solution.py:386
  125.4 30.7 %collective-permute-done.others_ref = bf16[172,8,256]{2,1,0:T(8,128)(2,1)S(1)} collective-permute-done((bf16[172,8,256]{2,1,0:T(8,128)(2,1)S(1)}, bf16[172,8,256]{2,1,0:T(8,128)(2,1)S(1)}, u32[]{:S(2)}, u32[]{:S(2)}) %collective-permute-start) | collective-permute-done | bytes 704544 | tf_op jit(solution)/shard_map/cond/branch_1_fun/ppermute | solution.py:35
  161.2 40.1 %all_to_all.45.answers_ref = bf16[752,8,256]{2,1,0:T(8,128)(2,1)S(1)} all-to-all(bf16[752,8,256]{2,1,0:T(8,128)(2,1)S(1)} %couple.4.refs_0_), channel_id=1, replica_groups={{0,1,2,3,8,9,10,11,16,17,18,19,24,25,26,27},{4,5,6,7,12,13,14,15,20,21,..., dimensions={0} | all-to-all | bytes 6160384 | tf_op jit(solution)/shard_map/cond/branch_1_fun/all_to_all | solution.py:386
  206.9 3.6 collective-permute-start.2
  210.5 6.4 %collective-permute-done.1 = bf16[15,29,256]{2,0,1:T(8,128)(2,1)S(1)} collective-permute-done((bf16[15,29,256]{2,0,1:T(8,128)(2,1)S(1)}, bf16[15,29,256]{2,0,1:T(8,128)(2,1)S(1)}, u32[]{:S(2)}, u32[]{:S(2)}) %collective-permute-start.1) | collective-permute-done | bytes 222752 | tf_op jit(solution)/shard_map/cond/branch_1_fun/ppermute | solution.py:35
  234.6 3.7 all-to-all-start.2
  240.0 6.0 %stiffen.5.refs_0_.begun_ref = f32[15,29,8,256]{3,2,1,0:T(8,128)S(1)} custom-call(bf16[8,512,512]{2,1,0:T(8,128)(2,1)} %get-tuple-element.331.stiff_ref, bf16[8,512,256]{2,1,0:T(8,128)(2,1)S(1)} %copy-done.31), custom_call_target="tpu_custom_call" | custom-call | tf_op jit(solution)/shard_map/cond/branch_1_fun/stiffen/pallas_call | solution.py:183
  247.9 29.6 %all-to-all-done.2.incoming_ref = bf16[752,8,256]{2,1,0:T(8,128)(2,1)S(1)} async-done(((bf16[752,8,256]{2,1,0:T(8,128)(2,1)}), bf16[752,8,256]{2,1,0:T(8,128)(2,1)S(1)}, u32[]{:S(2)}, u32[]{:S(2)}) %all-to-all-start.2) | async-done | bytes 3080224 | tf_op jit(solution)/shard_map/cond/branch_1_fun/all_to_all | solution.py:386
  284.2 31.0 %collective-permute-done.5.others_ref = bf16[172,8,256]{2,1,0:T(8,128)(2,1)S(1)} collective-permute-done((bf16[172,8,256]{2,1,0:T(8,128)(2,1)S(1)}, bf16[172,8,256]{2,1,0:T(8,128)(2,1)S(1)}, u32[]{:S(2)}, u32[]{:S(2)}) %collective-permute-start.5) | collective-permute-done | bytes 704544 | tf_op jit(solution)/shard_map/cond/branch_1_fun/ppermute | solution.py:35
  318.4 40.0 %all_to_all.46.answers_ref = bf16[752,8,256]{2,1,0:T(8,128)(2,1)S(1)} all-to-all(bf16[752,8,256]{2,1,0:T(8,128)(2,1)S(1)} %couple.5.refs_0_), channel_id=1, replica_groups={{0,1,2,3,8,9,10,11,16,17,18,19,24,25,26,27},{4,5,6,7,12,13,14,15,20,21,..., dimensions={0} | all-to-all | bytes 6160384 | tf_op jit(solution)/shard_map/cond/branch_1_fun/all_to_all | solution.py:386
  367.5 6.5 %collective-permute-done.6 = bf16[15,29,256]{2,0,1:T(8,128)(2,1)S(1)} collective-permute-done((bf16[15,29,256]{2,0,1:T(8,128)(2,1)S(1)}, bf16[15,29,256]{2,0,1:T(8,128)(2,1)S(1)}, u32[]{:S(2)}, u32[]{:S(2)}) %collective-permute-start.6) | collective-permute-done | bytes 222752 | tf_op jit(solution)/shard_map/cond/branch_1_fun/ppermute | solution.py:35
  391.5 4.0 all-to-all-start.4
  397.1 6.0 %stiffen.6.refs_0_.begun_ref = f32[15,29,8,256]{3,2,1,0:T(8,128)S(1)} custom-call(bf16[8,512,512]{2,1,0:T(8,128)(2,1)} %get-tuple-element.331.stiff_ref, bf16[8,512,256]{2,1,0:T(8,128)(2,1)S(1)} %copy-done.33), custom_call_target="tpu_custom_call" | custom-call | tf_op jit(solution)/shard_map/cond/branch_1_fun/stiffen/pallas_call | solution.py:183
  405.0 29.5 %all-to-all-done.4.incoming_ref = bf16[752,8,256]{2,1,0:T(8,128)(2,1)S(1)} async-done(((bf16[752,8,256]{2,1,0:T(8,128)(2,1)}), bf16[752,8,256]{2,1,0:T(8,128)(2,1)S(1)}, u32[]{:S(2)}, u32[]{:S(2)}) %all-to-all-start.4) | async-done | bytes 3080224 | tf_op jit(solution)/shard_map/cond/branch_1_fun/all_to_all | solution.py:386
  441.9 30.7 %collective-permute-done.10.others_ref = bf16[172,8,256]{2,1,0:T(8,128)(2,1)S(1)} collective-permute-done((bf16[172,8,256]{2,1,0:T(8,128)(2,1)S(1)}, bf16[172,8,256]{2,1,0:T(8,128)(2,1)S(1)}, u32[]{:S(2)}, u32[]{:S(2)}) %collective-permute-start.10) | collective-permute-done | bytes 704544 | tf_op jit(solution)/shard_map/cond/branch_1_fun/ppermute | solution.py:35
  475.8 39.8 %all_to_all.47.answers_ref = bf16[752,8,256]{2,1,0:T(8,128)(2,1)S(1)} all-to-all(bf16[752,8,256]{2,1,0:T(8,128)(2,1)S(1)} %couple.6.refs_0_), channel_id=1, replica_groups={{0,1,2,3,8,9,10,11,16,17,18,19,24,25,26,27},{4,5,6,7,12,13,14,15,20,21,..., dimensions={0} | all-to-all | bytes 6160384 | tf_op jit(solution)/shard_map/cond/branch_1_fun/all_to_all | solution.py:386
  524.6 6.5 %collective-permute-done.11 = bf16[15,29,256]{2,0,1:T(8,128)(2,1)S(1)} collective-permute-done((bf16[15,29,256]{2,0,1:T(8,128)(2,1)S(1)}, bf16[15,29,256]{2,0,1:T(8,128)(2,1)S(1)}, u32[]{:S(2)}, u32[]{:S(2)}) %collective-permute-start.11) | collective-permute-done | bytes 222752 | tf_op jit(solution)/shard_map/cond/branch_1_fun/ppermute | solution.py:35
  540.6 3.7 fusion.4
  (277 shorter events, 160.8 us)
Async XLA Ops:
  2.1 34.0 %all-to-all-start.8 = ((s32[32,1,160]{2,1,0:T(1,128)}), s32[32,1,160]{2,1,0:T(1,128)S(1)}, u32[]{:S(2)}, u32[]{:S(2)}) async-start(s32[32,1,160]{2,1,0:T(1,128)} %broadcast_in_dim.210), calls=%async_computation.8 | async-start | bytes 65536 | tf_op jit(solution)/shard_map/all_to_all | solution.py:398
  10.6 34.9 %collective-permute-start.20 = (f32[256,128]{1,0:T(8,128)S(1)}, f32[256,128]{1,0:T(8,128)S(1)}, u32[]{:S(2)}, u32[]{:S(2)}) collective-permute-start(f32[256,128]{1,0:T(8,128)S(1)} %reshape.443), channel_id=1, source_target_pairs={{0,4},{1,5},{2,6},{3,7},{4,0},{5,1},{6,2},{7,3},{8,12},{9,13},{10,... | collective-permute-start | bytes 393224 | tf_op jit(solution)/shard_map/ppermute | solution.py:35
  16.0 40.9 %collective-permute-start.27 = (bf16[14,1,29,256]{3,1,2,0:T(2,128)(2,1)S(1)}, bf16[14,1,29,256]{3,1,2,0:T(2,128)(2,1)S(1)}, u32[]{:S(2)}, u32[]{:S(2)}) collective-permute-start(bf16[14,1,29,256]{3,1,2,0:T(2,128)(2,1)S(1)} %slice.171), channel_id=1, source_target_pairs={{0,7},{1,0},{2,1},{3,2},{4,3},{5,4},{6,5},{7,6},{8,15},{9,8},{10,9... | collective-permute-start | bytes 623624 | tf_op jit(solution)/shard_map/ppermute | solution.py:35
  19.1 37.8 %collective-permute-start.28 = (bf16[1,7,29,256]{3,1,2,0:T(8,128)(2,1)}, bf16[1,7,29,256]{3,1,2,0:T(8,128)(2,1)S(1)}, u32[]{:S(2)}, u32[]{:S(2)}) collective-permute-start(bf16[1,7,29,256]{3,1,2,0:T(8,128)(2,1)} %slice.172), channel_id=1, source_target_pairs={{0,24},{8,0},{16,8},{24,16},{1,25},{9,1},{17,9},{25,17},{2,26},{10... | collective-permute-start | bytes 311816 | tf_op jit(solution)/shard_map/ppermute | solution.py:35
  46.5 7.7 %collective-permute-start.22 = (f32[256,128]{1,0:T(8,128)S(1)}, f32[256,128]{1,0:T(8,128)S(1)}, u32[]{:S(2)}, u32[]{:S(2)}) collective-permute-start(f32[256,128]{1,0:T(8,128)S(1)} %get-tuple-element.418), channel_id=1, source_target_pairs={{0,16},{8,24},{16,0},{24,8},{1,17},{9,25},{17,1},{25,9},{2,18},{10... | collective-permute-start | bytes 393224 | tf_op jit(solution)/shard_map/ppermute | solution.py:35
  47.1 7.2 %collective-permute-start.23 = (f32[256,128]{1,0:T(8,128)S(1)}, f32[256,128]{1,0:T(8,128)S(1)}, u32[]{:S(2)}, u32[]{:S(2)}) collective-permute-start(f32[256,128]{1,0:T(8,128)S(1)} %get-tuple-element.418), channel_id=1, source_target_pairs={{0,8},{8,16},{16,24},{24,0},{1,9},{9,17},{17,25},{25,1},{2,10},{10... | collective-permute-start | bytes 393224 | tf_op jit(solution)/shard_map/ppermute | solution.py:35
  50.4 5.2 collective-permute-start.29
  54.3 5.4 collective-permute-start.24
  54.9 5.7 %collective-permute-start.25 = (f32[256,128]{1,0:T(8,128)S(1)}, f32[256,128]{1,0:T(8,128)S(1)}, u32[]{:S(2)}, u32[]{:S(2)}) collective-permute-start(f32[256,128]{1,0:T(8,128)S(1)} %select_select_fusion.1), channel_id=1, source_target_pairs={{2,0},{3,1},{0,2},{1,3},{6,4},{7,5},{4,6},{5,7},{10,8},{11,9},{8,1... | collective-permute-start | bytes 393224 | tf_op jit(solution)/shard_map/ppermute | solution.py:497
  55.6 7.7 %collective-permute-start.26 = (f32[256,128]{1,0:T(8,128)S(1)}, f32[256,128]{1,0:T(8,128)S(1)}, u32[]{:S(2)}, u32[]{:S(2)}) collective-permute-start(f32[256,128]{1,0:T(8,128)S(1)} %select_select_fusion.1), channel_id=1, source_target_pairs={{3,0},{0,1},{1,2},{2,3},{7,4},{4,5},{5,6},{6,7},{11,8},{8,9},{9,10... | collective-permute-start | bytes 393224 | tf_op jit(solution)/shard_map/ppermute | solution.py:497
  75.5 42.8 %all-to-all-start = ((bf16[752,8,256]{2,1,0:T(8,128)(2,1)}), bf16[752,8,256]{2,1,0:T(8,128)(2,1)S(1)}, u32[]{:S(2)}, u32[]{:S(2)}) async-start(bf16[752,8,256]{2,1,0:T(8,128)(2,1)} %copy-done.27), calls=%async_computation | async-start | bytes 6160384 | tf_op jit(solution)/shard_map/cond/branch_1_fun/all_to_all | solution.py:386
  122.6 33.5 %collective-permute-start = (bf16[172,8,256]{2,1,0:T(8,128)(2,1)S(1)}, bf16[172,8,256]{2,1,0:T(8,128)(2,1)S(1)}, u32[]{:S(2)}, u32[]{:S(2)}) collective-permute-start(bf16[172,8,256]{2,1,0:T(8,128)(2,1)S(1)} %get-tuple-element.334), channel_id=1, source_target_pairs={{0,4},{1,5},{2,6},{3,7},{4,0},{5,1},{6,2},{7,3},{8,12},{9,13},{10,... | collective-permute-start | bytes 2113544 | tf_op jit(solution)/shard_map/cond/branch_1_fun/ppermute | solution.py:35
  205.6 11.3 %collective-permute-start.1 = (bf16[15,29,256]{2,0,1:T(8,128)(2,1)S(1)}, bf16[15,29,256]{2,0,1:T(8,128)(2,1)S(1)}, u32[]{:S(2)}, u32[]{:S(2)}) collective-permute-start(bf16[15,29,256]{2,0,1:T(8,128)(2,1)S(1)} %bitcast.198), channel_id=1, source_target_pairs={{0,1},{1,2},{2,3},{3,4},{4,5},{5,6},{6,7},{7,0},{8,9},{9,10},{10,1... | collective-permute-start | bytes 668168 | tf_op jit(solution)/shard_map/cond/branch_1_fun/ppermute | solution.py:35
  206.9 12.5 %collective-permute-start.2 = (bf16[15,29,256]{2,0,1:T(8,128)(2,1)S(1)}, bf16[15,29,256]{2,0,1:T(8,128)(2,1)S(1)}, u32[]{:S(2)}, u32[]{:S(2)}) collective-permute-start(bf16[15,29,256]{2,0,1:T(8,128)(2,1)S(1)} %bitcast.199), channel_id=1, source_target_pairs={{0,7},{1,0},{2,1},{3,2},{4,3},{5,4},{6,5},{7,6},{8,15},{9,8},{10,9... | collective-permute-start | bytes 668168 | tf_op jit(solution)/shard_map/cond/branch_1_fun/ppermute | solution.py:35
  234.6 42.8 %all-to-all-start.2 = ((bf16[752,8,256]{2,1,0:T(8,128)(2,1)}), bf16[752,8,256]{2,1,0:T(8,128)(2,1)S(1)}, u32[]{:S(2)}, u32[]{:S(2)}) async-start(bf16[752,8,256]{2,1,0:T(8,128)(2,1)} %copy-done.28), calls=%async_computation.2 | async-start | bytes 6160384 | tf_op jit(solution)/shard_map/cond/branch_1_fun/all_to_all | solution.py:386
  281.7 33.5 %collective-permute-start.5 = (bf16[172,8,256]{2,1,0:T(8,128)(2,1)S(1)}, bf16[172,8,256]{2,1,0:T(8,128)(2,1)S(1)}, u32[]{:S(2)}, u32[]{:S(2)}) collective-permute-start(bf16[172,8,256]{2,1,0:T(8,128)(2,1)S(1)} %get-tuple-element.341), channel_id=1, source_target_pairs={{0,4},{1,5},{2,6},{3,7},{4,0},{5,1},{6,2},{7,3},{8,12},{9,13},{10,... | collective-permute-start | bytes 2113544 | tf_op jit(solution)/shard_map/cond/branch_1_fun/ppermute | solution.py:35
  362.6 11.3 %collective-permute-start.6 = (bf16[15,29,256]{2,0,1:T(8,128)(2,1)S(1)}, bf16[15,29,256]{2,0,1:T(8,128)(2,1)S(1)}, u32[]{:S(2)}, u32[]{:S(2)}) collective-permute-start(bf16[15,29,256]{2,0,1:T(8,128)(2,1)S(1)} %bitcast.202), channel_id=1, source_target_pairs={{0,1},{1,2},{2,3},{3,4},{4,5},{5,6},{6,7},{7,0},{8,9},{9,10},{10,1... | collective-permute-start | bytes 668168 | tf_op jit(solution)/shard_map/cond/branch_1_fun/ppermute | solution.py:35
  363.9 12.5 %collective-permute-start.7 = (bf16[15,29,256]{2,0,1:T(8,128)(2,1)S(1)}, bf16[15,29,256]{2,0,1:T(8,128)(2,1)S(1)}, u32[]{:S(2)}, u32[]{:S(2)}) collective-permute-start(bf16[15,29,256]{2,0,1:T(8,128)(2,1)S(1)} %bitcast.200), channel_id=1, source_target_pairs={{0,7},{1,0},{2,1},{3,2},{4,3},{5,4},{6,5},{7,6},{8,15},{9,8},{10,9... | collective-permute-start | bytes 668168 | tf_op jit(solution)/shard_map/cond/branch_1_fun/ppermute | solution.py:35
  378.0 5.1 collective-permute-start.8
  391.5 43.0 %all-to-all-start.4 = ((bf16[752,8,256]{2,1,0:T(8,128)(2,1)}), bf16[752,8,256]{2,1,0:T(8,128)(2,1)S(1)}, u32[]{:S(2)}, u32[]{:S(2)}) async-start(bf16[752,8,256]{2,1,0:T(8,128)(2,1)} %copy-done.29), calls=%async_computation.4 | async-start | bytes 6160384 | tf_op jit(solution)/shard_map/cond/branch_1_fun/all_to_all | solution.py:386
  438.8 33.8 %collective-permute-start.10 = (bf16[172,8,256]{2,1,0:T(8,128)(2,1)S(1)}, bf16[172,8,256]{2,1,0:T(8,128)(2,1)S(1)}, u32[]{:S(2)}, u32[]{:S(2)}) collective-permute-start(bf16[172,8,256]{2,1,0:T(8,128)(2,1)S(1)} %get-tuple-element.345), channel_id=1, source_target_pairs={{0,4},{1,5},{2,6},{3,7},{4,0},{5,1},{6,2},{7,3},{8,12},{9,13},{10,... | collective-permute-start | bytes 2113544 | tf_op jit(solution)/shard_map/cond/branch_1_fun/ppermute | solution.py:35
  519.8 11.3 %collective-permute-start.11 = (bf16[15,29,256]{2,0,1:T(8,128)(2,1)S(1)}, bf16[15,29,256]{2,0,1:T(8,128)(2,1)S(1)}, u32[]{:S(2)}, u32[]{:S(2)}) collective-permute-start(bf16[15,29,256]{2,0,1:T(8,128)(2,1)S(1)} %bitcast.203), channel_id=1, source_target_pairs={{0,1},{1,2},{2,3},{3,4},{4,5},{5,6},{6,7},{7,0},{8,9},{9,10},{10,1... | collective-permute-start | bytes 668168 | tf_op jit(solution)/shard_map/cond/branch_1_fun/ppermute | solution.py:35
  521.1 12.4 %collective-permute-start.12 = (bf16[15,29,256]{2,0,1:T(8,128)(2,1)S(1)}, bf16[15,29,256]{2,0,1:T(8,128)(2,1)S(1)}, u32[]{:S(2)}, u32[]{:S(2)}) collective-permute-start(bf16[15,29,256]{2,0,1:T(8,128)(2,1)S(1)} %bitcast.201), channel_id=1, source_target_pairs={{0,7},{1,0},{2,1},{3,2},{4,3},{5,4},{6,5},{7,6},{8,15},{9,8},{10,9... | collective-permute-start | bytes 668168 | tf_op jit(solution)/shard_map/cond/branch_1_fun/ppermute | solution.py:35
  535.3 5.2 collective-permute-start.13
  (60 other events, 928.9 us)

commit v5 on v4

--- a/solution.py
+++ b/solution.py
@@ -98,13 +98,17 @@
         high_ref, low_ref = refs[len(after) :]
         rows = lax.broadcasted_iota(jnp.int32, (edge, edge), 0) // per_atom
         columns = lax.broadcasted_iota(jnp.int32, (edge, edge), 1) // per_atom
-        for g in range(groups):
-            block = mixers_ref[g * GROUP : (g + 1) * GROUP].reshape(edge, per_atom)
+
+        def one(g, carry):
+            block = mixers_ref[pl.ds(g * GROUP, GROUP)].reshape(edge, per_atom)
             block = jnp.concatenate([block] * GROUP, axis=1)
             block = jnp.where(rows == columns, block, 0.0)
             high = block.astype(BF16)
             high_ref[g] = high
             low_ref[g] = (block - high.astype(F32)).astype(BF16)
+            return carry
+
+        lax.fori_loop(0, groups, one, 0)
 
     vmem = pl.BlockSpec(memory_space=pltpu.VMEM)
     return pl.pallas_call(
@@ -341,20 +345,55 @@
     )(starts, used, turned, answers, begun, *after)
 
 
-def completed(total):
+def finish(total, sides, ends, scale, older):
     span_u, span_w, span_v, breadth = total.shape
+
+    def body(scale_ref, total_ref, prev_v_ref, next_v_ref, prev_u_ref, next_u_ref, *refs):
+        out_ref = refs[-1]
+        times = scale_ref[0]
+        at = lax.broadcasted_iota(jnp.int32, (span_w, span_v, breadth), 1)
+
+        def row(u, carry):
+            first = prev_v_ref[u].astype(F32)[:, None]
+            last = next_v_ref[u].astype(F32)[:, None]
+            value = total_ref[u] + jnp.where(at == 0, first, 0.0)
+            value = times * (value + jnp.where(at == span_v - 1, last, 0.0))
+            if older is not None:
+                value = value - refs[0][u]
+            out_ref[u] = value
+            return carry
+
+        lax.fori_loop(0, span_u, row, 0)
+        out_ref[0] = out_ref[0] + times * prev_u_ref[...].astype(F32)
+        out_ref[span_u - 1] = out_ref[span_u - 1] + times * next_u_ref[...].astype(F32)
+
+    vmem = pl.BlockSpec(memory_space=pltpu.VMEM)
+    known = [] if older is None else [older]
+    return pl.pallas_call(
+        body,
+        in_specs=[smem()] + [vmem] * (5 + len(known)),
+        out_specs=vmem,
+        out_shape=jax.ShapeDtypeStruct(total.shape, F32),
+        compiler_params=pltpu.CompilerParams(vmem_limit_bytes=GRANT),
+        name="finish",
+    )(scale, total, *sides, *ends, *known)
+
+
+def completed(total, scale, older):
     low_v = total[:, :, 0].astype(BF16)
     high_v = total[:, :, -1].astype(BF16)
-    from_next = shifted(low_v, ("gy",), (-1,)).astype(F32)[:, :, None]
-    from_prev = shifted(high_v, ("gy",), (1,)).astype(F32)[:, :, None]
-    gap = jnp.zeros((span_u, span_w, span_v - 2, breadth), F32)
-    total = total + jnp.concatenate([from_prev, gap, from_next], axis=2)
-    low_u = total[0].astype(BF16)
-    high_u = total[-1].astype(BF16)
-    from_next = shifted(low_u, ("gx",), (-1,)).astype(F32)[None]
-    from_prev = shifted(high_u, ("gx",), (1,)).astype(F32)[None]
-    gap = jnp.zeros((span_u - 2, span_w, span_v, breadth), F32)
-    return total + jnp.concatenate([from_prev, gap, from_next], axis=0)
+    next_v = shifted(low_v, ("gy",), (-1,))
+    prev_v = shifted(high_v, ("gy",), (1,))
+
+    def edge(u):
+        row = total[u]
+        first = row[:, :1] + prev_v[u][:, None].astype(F32)
+        last = row[:, -1:] + next_v[u][:, None].astype(F32)
+        return jnp.concatenate([first, row[:, 1:-1], last], axis=1).astype(BF16)
+
+    next_u = shifted(edge(0), ("gx",), (-1,))
+    prev_u = shifted(edge(-1), ("gx",), (1,))
+    return finish(total, (prev_v, next_v), (prev_u, next_u), scale, older)
 
 
 def on_device(orbitals, cell_matrices, cell_nodes, projectors, entry_atom, coupling, proj_counts):
@@ -520,7 +559,7 @@
     grid = jnp.transpose(widened, (0, 2, 1, 3)).astype(F32)
     extended = grid.shape[:3]
 
-    def advance(field, older, mixing, cap, span):
+    def advance(field, older, scale, mixing, cap, span):
         room = senders * cap
         starts = own * cap + offsets
         begins = (places_in + jnp.arange(senders)[:, None] * cap).reshape(slots)
@@ -547,14 +586,15 @@
                 apply(turned, answers[part], image, starts, used, part, cz, per_atom, after)
             )
             after = (totals[-1],)
-        image = completed(jnp.concatenate(totals, axis=-1) if PARTS > 1 else totals[0])
-        return image if older is None else 2.0 * image - older, mixing
+        total = jnp.concatenate(totals, axis=-1) if PARTS > 1 else totals[0]
+        return completed(total, scale, older), mixing
 
     def packed():
         mixing = None
         older, field = None, grid
-        for _ in range(FILTER_DEGREE):
-            image, mixing = advance(field, older, mixing, cap, span)
+        for step in range(FILTER_DEGREE):
+            scale = jnp.full((1,), 1.0 if step == 0 else 2.0, F32)
+            image, mixing = advance(field, older, scale, mixing, cap, span)
             older, field = field, image
         return field[:span_x, :, :span_y].astype(BF16)
 
@@ -563,8 +603,11 @@
 
         def step(at, fields):
             older, field = fields
-            image, _ = advance(field, None, mixing, (each + 1) * units, (atoms + 1) * units)
-            return field, jnp.where(at == 0, image, 2.0 * image - older)
+            scale = jnp.where(at == 0, 1.0, 2.0).astype(F32).reshape(1)
+            image, _ = advance(
+                field, older, scale, mixing, (each + 1) * units, (atoms + 1) * units
+            )
+            return field, image
 
         fields = (jnp.zeros_like(grid), grid)
         field = lax.fori_loop(0, FILTER_DEGREE, step, fields)[1]

time: 556 us -> 541 us (0.973); the launches traced: 548 us -> 540 us
  other arithmetic: 19.7 us -> 11.3 us
  Pallas kernels: 69.7 us -> 76 us
    pallas_call x0 -> x3, Pallas kernels: none -> 5.79 us  [finish(): pl.pallas_call(body, in_specs=[smem()] + [vmem] * (5 + len(known)), out_s...]
    another operation x104 -> x70, local copies, waits for them, and re-layouts: 30.2 us -> 28.1 us
  transfers between devices with their start and end apart: 29 -> 29, of which waited for: 23 -> 22; matrix products, arithmetic and copies ran while one was open for 3% -> 3% of each run, Pallas kernels for 5% -> 6%
where the time goes in v5:
time: 541 us; the launch traced here: 540 us
  waiting for transfers between devices  227 us (42%)
  blocking collectives  120 us (22%)
  Pallas kernels  76 us (14%)
  starting transfers between devices  53.7 us (10%)
  local copies, waits for them, and re-layouts  47 us (9%)
  other arithmetic  11.3 us (2%)
    ppermute x22, waiting for transfers between devices, shifted(): return lax.ppermute(x, axes if len(axes) > 1 else axes[0], pairs)  135 us
    all_to_all x3, blocking collectives, exchange(): lax.all_to_all(x, both, split_axis=0, concat_axis=0, axis_index_groups=te...  120 us
    all_to_all x3, waiting for transfers between devices, exchange(): lax.all_to_all(x, both, split_axis=0, concat_axis=0, axis_index_groups=te...  88.7 us
    ppermute x22, starting transfers between devices, shifted(): return lax.ppermute(x, axes if len(axes) > 1 else axes[0], pairs)  32.5 us
    another operation x70, local copies, waits for them, and re-layouts  28.1 us
    pallas_call x3, Pallas kernels, stiffen(): pl.pallas_call(body, grid=(cells,), in_specs=[pl.BlockSpec((1, nodes, nod...  18.1 us
    pallas_call x3, Pallas kernels, project(): pl.pallas_call(body, grid=(cells,), in_specs=[smem(), whole(field.shape),...  13.3 us
    all_to_all x3, starting transfers between devices, exchange(): lax.all_to_all(x, both, split_axis=0, concat_axis=0, axis_index_groups=te...  11.2 us
  transfers between devices with their start and end apart: 29, of which 22 were waited for; matrix products, arithmetic and copies ran while one was open for 3% of the time, Pallas kernels for 6%

profile of v5, /device:TPU:0, one launch (start us, length us, event | category | flops | bytes accessed | tf_op | source)
XLA Modules:
  0.0 539.8 jit_solution(6286273048615742991)
XLA Ops:
  2.1 7.3 %all-to-all-start.8 = ((s32[32,1,160]{2,1,0:T(1,128)}), s32[32,1,160]{2,1,0:T(1,128)S(1)}, u32[]{:S(2)}, u32[]{:S(2)}) async-start(s32[32,1,160]{2,1,0:T(1,128)} %broadcast_in_dim.98), calls=%async_computation.8 | async-start | bytes 65536 | tf_op jit(solution)/shard_map/all_to_all | solution.py:437
  24.5 11.0 %canonical.1 = (bf16[8,512,512]{2,1,0:T(8,128)(2,1)}, bf16[8,512,512]{2,1,0:T(8,128)(2,1)}, bf16[8,512,512]{2,1,0:T(8,128)(2,1)}) custom-call(s32[8,1,512]{2,1,0:T(1,128)S(1)} %fusion.65.place_ref, bf16[8,512,512]{2,1,0:T(8,128)(2,1)S(1)} %bitcast.271, bf16[8,512,512]{2,1,0:T(8,128)(2,1)S(1)} %bitcast.272), custom_call_target="tpu_custom_call" | custom-call | tf_op jit(solution)/shard_map/canonical/pallas_call | solution.py:69
  55.9 3.6 convert_bitcast_fusion
  62.8 473.2 %conditional.2 = (f32[15,29,8,256]{3,2,1,0:T(8,128)}) conditional(s32[]{:T(128)} %convert_element_type.396, (f32[64,32,32]{2,1,0:T(8,128)S(1)}, s32[128]{0:T(128)S(1)}, s32[128]{0:T(128)S(1)}, s32[16,16]{1,0:T(8,128)S(1)}, bf16[8,512,512]{2,1,0:T(8,128)(2,1)}, /*index=5*/bf16[8,512,512]{2,1,0:T(8,128)(2,1)}, s32[256]{0:T(256)S(1)}, ...), branch_computations={%region_13.16_spmd, %region_16.17_spmd} | conditional | flops 2405904 | bytes 468180224
  64.0 7.0 %project.8 = (bf16[8,512,256]{2,1,0:T(8,128)(2,1)S(1)}, bf16[752,8,256]{2,1,0:T(8,128)(2,1)S(1)}) custom-call(s32[128]{0:T(128)S(1)} %multiply_add_fusion.1.starts_ref, f32[15,29,8,256]{3,2,1,0:T(8,128)} %get-tuple-element.325.field_ref.refs_0_, bf16[8,512,512]{2,1,0:T(8,128)(2,1)} %get-tuple-element.326.straight_ref), custom_call_target="tpu_custom_call" | custom-call | tf_op jit(solution)/shard_map/cond/branch_1_fun/project/pallas_call | solution.py:147
  74.0 3.7 all-to-all-start
  79.6 6.0 %stiffen.4.refs_0_.begun_ref = f32[15,29,8,256]{3,2,1,0:T(8,128)S(1)} custom-call(bf16[8,512,512]{2,1,0:T(8,128)(2,1)} %get-tuple-element.328.stiff_ref, bf16[8,512,256]{2,1,0:T(8,128)(2,1)S(1)} %copy-done.24), custom_call_target="tpu_custom_call" | custom-call | tf_op jit(solution)/shard_map/cond/branch_1_fun/stiffen/pallas_call | solution.py:187
  87.4 29.5 %all-to-all-done.incoming_ref = bf16[752,8,256]{2,1,0:T(8,128)(2,1)S(1)} async-done(((bf16[752,8,256]{2,1,0:T(8,128)(2,1)}), bf16[752,8,256]{2,1,0:T(8,128)(2,1)S(1)}, u32[]{:S(2)}, u32[]{:S(2)}) %all-to-all-start) | async-done | bytes 3080224 | tf_op jit(solution)/shard_map/cond/branch_1_fun/all_to_all | solution.py:425
  124.3 30.2 %collective-permute-done.others_ref = bf16[172,8,256]{2,1,0:T(8,128)(2,1)S(1)} collective-permute-done((bf16[172,8,256]{2,1,0:T(8,128)(2,1)S(1)}, bf16[172,8,256]{2,1,0:T(8,128)(2,1)S(1)}, u32[]{:S(2)}, u32[]{:S(2)}) %collective-permute-start) | collective-permute-done | bytes 704544 | tf_op jit(solution)/shard_map/cond/branch_1_fun/ppermute | solution.py:35
  159.8 40.0 %all_to_all.45.answers_ref = bf16[752,8,256]{2,1,0:T(8,128)(2,1)S(1)} all-to-all(bf16[752,8,256]{2,1,0:T(8,128)(2,1)S(1)} %couple.4.refs_0_), channel_id=1, replica_groups={{0,1,2,3,8,9,10,11,16,17,18,19,24,25,26,27},{4,5,6,7,12,13,14,15,20,21,..., dimensions={0} | all-to-all | bytes 6160384 | tf_op jit(solution)/shard_map/cond/branch_1_fun/all_to_all | solution.py:425
  209.1 6.5 %collective-permute-done.1 = bf16[15,29,256]{2,0,1:T(8,128)(2,1)S(1)} collective-permute-done((bf16[15,29,256]{2,0,1:T(8,128)(2,1)S(1)}, bf16[15,29,256]{2,0,1:T(8,128)(2,1)S(1)}, u32[]{:S(2)}, u32[]{:S(2)}) %collective-permute-start.1) | collective-permute-done | bytes 222752 | tf_op jit(solution)/shard_map/cond/branch_1_fun/ppermute | solution.py:35
  230.7 3.7 all-to-all-start.2
  236.0 6.0 %stiffen.5.refs_0_.begun_ref = f32[15,29,8,256]{3,2,1,0:T(8,128)S(1)} custom-call(bf16[8,512,512]{2,1,0:T(8,128)(2,1)} %get-tuple-element.328.stiff_ref, bf16[8,512,256]{2,1,0:T(8,128)(2,1)S(1)} %copy-done.34), custom_call_target="tpu_custom_call" | custom-call | tf_op jit(solution)/shard_map/cond/branch_1_fun/stiffen/pallas_call | solution.py:187
  243.9 29.6 %all-to-all-done.2.incoming_ref = bf16[752,8,256]{2,1,0:T(8,128)(2,1)S(1)} async-done(((bf16[752,8,256]{2,1,0:T(8,128)(2,1)}), bf16[752,8,256]{2,1,0:T(8,128)(2,1)S(1)}, u32[]{:S(2)}, u32[]{:S(2)}) %all-to-all-start.2) | async-done | bytes 3080224 | tf_op jit(solution)/shard_map/cond/branch_1_fun/all_to_all | solution.py:425
  280.0 31.2 %collective-permute-done.5.others_ref = bf16[172,8,256]{2,1,0:T(8,128)(2,1)S(1)} collective-permute-done((bf16[172,8,256]{2,1,0:T(8,128)(2,1)S(1)}, bf16[172,8,256]{2,1,0:T(8,128)(2,1)S(1)}, u32[]{:S(2)}, u32[]{:S(2)}) %collective-permute-start.5) | collective-permute-done | bytes 704544 | tf_op jit(solution)/shard_map/cond/branch_1_fun/ppermute | solution.py:35
  314.4 40.0 %all_to_all.46.answers_ref = bf16[752,8,256]{2,1,0:T(8,128)(2,1)S(1)} all-to-all(bf16[752,8,256]{2,1,0:T(8,128)(2,1)S(1)} %couple.5.refs_0_), channel_id=1, replica_groups={{0,1,2,3,8,9,10,11,16,17,18,19,24,25,26,27},{4,5,6,7,12,13,14,15,20,21,..., dimensions={0} | all-to-all | bytes 6160384 | tf_op jit(solution)/shard_map/cond/branch_1_fun/all_to_all | solution.py:425
  363.7 6.5 %collective-permute-done.6 = bf16[15,29,256]{2,0,1:T(8,128)(2,1)S(1)} collective-permute-done((bf16[15,29,256]{2,0,1:T(8,128)(2,1)S(1)}, bf16[15,29,256]{2,0,1:T(8,128)(2,1)S(1)}, u32[]{:S(2)}, u32[]{:S(2)}) %collective-permute-start.6) | collective-permute-done | bytes 222752 | tf_op jit(solution)/shard_map/cond/branch_1_fun/ppermute | solution.py:35
  385.5 3.7 all-to-all-start.4
  390.9 6.0 %stiffen.6.refs_0_.begun_ref = f32[15,29,8,256]{3,2,1,0:T(8,128)S(1)} custom-call(bf16[8,512,512]{2,1,0:T(8,128)(2,1)} %get-tuple-element.328.stiff_ref, bf16[8,512,256]{2,1,0:T(8,128)(2,1)S(1)} %copy-done.32), custom_call_target="tpu_custom_call" | custom-call | tf_op jit(solution)/shard_map/cond/branch_1_fun/stiffen/pallas_call | solution.py:187
  398.7 29.6 %all-to-all-done.4.incoming_ref = bf16[752,8,256]{2,1,0:T(8,128)(2,1)S(1)} async-done(((bf16[752,8,256]{2,1,0:T(8,128)(2,1)}), bf16[752,8,256]{2,1,0:T(8,128)(2,1)S(1)}, u32[]{:S(2)}, u32[]{:S(2)}) %all-to-all-start.4) | async-done | bytes 3080224 | tf_op jit(solution)/shard_map/cond/branch_1_fun/all_to_all | solution.py:425
  435.4 30.7 %collective-permute-done.10.others_ref = bf16[172,8,256]{2,1,0:T(8,128)(2,1)S(1)} collective-permute-done((bf16[172,8,256]{2,1,0:T(8,128)(2,1)S(1)}, bf16[172,8,256]{2,1,0:T(8,128)(2,1)S(1)}, u32[]{:S(2)}, u32[]{:S(2)}) %collective-permute-start.10) | collective-permute-done | bytes 704544 | tf_op jit(solution)/shard_map/cond/branch_1_fun/ppermute | solution.py:35
  469.2 40.0 %all_to_all.47.answers_ref = bf16[752,8,256]{2,1,0:T(8,128)(2,1)S(1)} all-to-all(bf16[752,8,256]{2,1,0:T(8,128)(2,1)S(1)} %couple.6.refs_0_), channel_id=1, replica_groups={{0,1,2,3,8,9,10,11,16,17,18,19,24,25,26,27},{4,5,6,7,12,13,14,15,20,21,..., dimensions={0} | all-to-all | bytes 6160384 | tf_op jit(solution)/shard_map/cond/branch_1_fun/all_to_all | solution.py:425
  514.9 3.5 collective-permute-start.12
  518.6 6.5 %collective-permute-done.11 = bf16[15,29,256]{2,0,1:T(8,128)(2,1)S(1)} collective-permute-done((bf16[15,29,256]{2,0,1:T(8,128)(2,1)S(1)}, bf16[15,29,256]{2,0,1:T(8,128)(2,1)S(1)}, u32[]{:S(2)}, u32[]{:S(2)}) %collective-permute-start.11) | collective-permute-done | bytes 222752 | tf_op jit(solution)/shard_map/cond/branch_1_fun/ppermute | solution.py:35
  (235 shorter events, 153.9 us)
Async XLA Ops:
  2.1 33.5 %all-to-all-start.8 = ((s32[32,1,160]{2,1,0:T(1,128)}), s32[32,1,160]{2,1,0:T(1,128)S(1)}, u32[]{:S(2)}, u32[]{:S(2)}) async-start(s32[32,1,160]{2,1,0:T(1,128)} %broadcast_in_dim.98), calls=%async_computation.8 | async-start | bytes 65536 | tf_op jit(solution)/shard_map/all_to_all | solution.py:437
  10.6 33.9 %collective-permute-start.20 = (f32[256,128]{1,0:T(8,128)S(1)}, f32[256,128]{1,0:T(8,128)S(1)}, u32[]{:S(2)}, u32[]{:S(2)}) collective-permute-start(f32[256,128]{1,0:T(8,128)S(1)} %reshape.670), channel_id=1, source_target_pairs={{0,4},{1,5},{2,6},{3,7},{4,0},{5,1},{6,2},{7,3},{8,12},{9,13},{10,... | collective-permute-start | bytes 393224 | tf_op jit(solution)/shard_map/ppermute | solution.py:35
  16.0 39.9 %collective-permute-start.27 = (bf16[14,1,29,256]{3,1,2,0:T(2,128)(2,1)S(1)}, bf16[14,1,29,256]{3,1,2,0:T(2,128)(2,1)S(1)}, u32[]{:S(2)}, u32[]{:S(2)}) collective-permute-start(bf16[14,1,29,256]{3,1,2,0:T(2,128)(2,1)S(1)} %slice.371), channel_id=1, source_target_pairs={{0,7},{1,0},{2,1},{3,2},{4,3},{5,4},{6,5},{7,6},{8,15},{9,8},{10,9... | collective-permute-start | bytes 623624 | tf_op jit(solution)/shard_map/ppermute | solution.py:35
  19.1 36.9 %collective-permute-start.28 = (bf16[1,7,29,256]{3,1,2,0:T(8,128)(2,1)}, bf16[1,7,29,256]{3,1,2,0:T(8,128)(2,1)}, u32[]{:S(2)}, u32[]{:S(2)}) collective-permute-start(bf16[1,7,29,256]{3,1,2,0:T(8,128)(2,1)} %slice.372), channel_id=1, source_target_pairs={{0,24},{8,0},{16,8},{24,16},{1,25},{9,1},{17,9},{25,17},{2,26},{10... | collective-permute-start | bytes 311816 | tf_op jit(solution)/shard_map/ppermute | solution.py:35
  45.5 7.7 %collective-permute-start.22 = (f32[256,128]{1,0:T(8,128)S(1)}, f32[256,128]{1,0:T(8,128)S(1)}, u32[]{:S(2)}, u32[]{:S(2)}) collective-permute-start(f32[256,128]{1,0:T(8,128)S(1)} %get-tuple-element.431), channel_id=1, source_target_pairs={{0,16},{8,24},{16,0},{24,8},{1,17},{9,25},{17,1},{25,9},{2,18},{10... | collective-permute-start | bytes 393224 | tf_op jit(solution)/shard_map/ppermute | solution.py:35
  46.1 7.2 %collective-permute-start.23 = (f32[256,128]{1,0:T(8,128)S(1)}, f32[256,128]{1,0:T(8,128)S(1)}, u32[]{:S(2)}, u32[]{:S(2)}) collective-permute-start(f32[256,128]{1,0:T(8,128)S(1)} %get-tuple-element.431), channel_id=1, source_target_pairs={{0,8},{8,16},{16,24},{24,0},{1,9},{9,17},{17,25},{25,1},{2,10},{10... | collective-permute-start | bytes 393224 | tf_op jit(solution)/shard_map/ppermute | solution.py:35
  49.4 5.2 collective-permute-start.29
  53.3 6.2 %collective-permute-start.24 = (f32[256,128]{1,0:T(8,128)S(1)}, f32[256,128]{1,0:T(8,128)S(1)}, u32[]{:S(2)}, u32[]{:S(2)}) collective-permute-start(f32[256,128]{1,0:T(8,128)S(1)} %select_select_fusion.1), channel_id=1, source_target_pairs={{1,0},{2,1},{3,2},{0,3},{5,4},{6,5},{7,6},{4,7},{9,8},{10,9},{11,1... | collective-permute-start | bytes 393224 | tf_op jit(solution)/shard_map/ppermute | solution.py:536
  54.0 5.7 %collective-permute-start.25 = (f32[256,128]{1,0:T(8,128)S(1)}, f32[256,128]{1,0:T(8,128)S(1)}, u32[]{:S(2)}, u32[]{:S(2)}) collective-permute-start(f32[256,128]{1,0:T(8,128)S(1)} %select_select_fusion.1), channel_id=1, source_target_pairs={{2,0},{3,1},{0,2},{1,3},{6,4},{7,5},{4,6},{5,7},{10,8},{11,9},{8,1... | collective-permute-start | bytes 393224 | tf_op jit(solution)/shard_map/ppermute | solution.py:536
  54.6 7.5 %collective-permute-start.26 = (f32[256,128]{1,0:T(8,128)S(1)}, f32[256,128]{1,0:T(8,128)S(1)}, u32[]{:S(2)}, u32[]{:S(2)}) collective-permute-start(f32[256,128]{1,0:T(8,128)S(1)} %select_select_fusion.1), channel_id=1, source_target_pairs={{3,0},{0,1},{1,2},{2,3},{7,4},{4,5},{5,6},{6,7},{11,8},{8,9},{9,10... | collective-permute-start | bytes 393224 | tf_op jit(solution)/shard_map/ppermute | solution.py:536
  74.0 42.8 %all-to-all-start = ((bf16[752,8,256]{2,1,0:T(8,128)(2,1)}), bf16[752,8,256]{2,1,0:T(8,128)(2,1)S(1)}, u32[]{:S(2)}, u32[]{:S(2)}) async-start(bf16[752,8,256]{2,1,0:T(8,128)(2,1)} %copy-done.28), calls=%async_computation | async-start | bytes 6160384 | tf_op jit(solution)/shard_map/cond/branch_1_fun/all_to_all | solution.py:425
  121.1 33.5 %collective-permute-start = (bf16[172,8,256]{2,1,0:T(8,128)(2,1)S(1)}, bf16[172,8,256]{2,1,0:T(8,128)(2,1)S(1)}, u32[]{:S(2)}, u32[]{:S(2)}) collective-permute-start(bf16[172,8,256]{2,1,0:T(8,128)(2,1)S(1)} %get-tuple-element.331), channel_id=1, source_target_pairs={{0,4},{1,5},{2,6},{3,7},{4,0},{5,1},{6,2},{7,3},{8,12},{9,13},{10,... | collective-permute-start | bytes 2113544 | tf_op jit(solution)/shard_map/cond/branch_1_fun/ppermute | solution.py:35
  204.2 11.3 %collective-permute-start.1 = (bf16[15,29,256]{2,0,1:T(8,128)(2,1)S(1)}, bf16[15,29,256]{2,0,1:T(8,128)(2,1)S(1)}, u32[]{:S(2)}, u32[]{:S(2)}) collective-permute-start(bf16[15,29,256]{2,0,1:T(8,128)(2,1)S(1)} %get-tuple-element.417), channel_id=1, source_target_pairs={{0,1},{1,2},{2,3},{3,4},{4,5},{5,6},{6,7},{7,0},{8,9},{9,10},{10,1... | collective-permute-start | bytes 668168 | tf_op jit(solution)/shard_map/cond/branch_1_fun/ppermute | solution.py:35
  205.5 12.4 %collective-permute-start.2 = (bf16[15,29,256]{2,0,1:T(8,128)(2,1)S(1)}, bf16[15,29,256]{2,0,1:T(8,128)(2,1)S(1)}, u32[]{:S(2)}, u32[]{:S(2)}) collective-permute-start(bf16[15,29,256]{2,0,1:T(8,128)(2,1)S(1)} %get-tuple-element.416), channel_id=1, source_target_pairs={{0,7},{1,0},{2,1},{3,2},{4,3},{5,4},{6,5},{7,6},{8,15},{9,8},{10,9... | collective-permute-start | bytes 668168 | tf_op jit(solution)/shard_map/cond/branch_1_fun/ppermute | solution.py:35
  218.3 5.0 collective-permute-start.3
  230.7 42.8 %all-to-all-start.2 = ((bf16[752,8,256]{2,1,0:T(8,128)(2,1)}), bf16[752,8,256]{2,1,0:T(8,128)(2,1)S(1)}, u32[]{:S(2)}, u32[]{:S(2)}) async-start(bf16[752,8,256]{2,1,0:T(8,128)(2,1)} %copy-done.30), calls=%async_computation.2 | async-start | bytes 6160384 | tf_op jit(solution)/shard_map/cond/branch_1_fun/all_to_all | solution.py:425
  277.7 33.5 %collective-permute-start.5 = (bf16[172,8,256]{2,1,0:T(8,128)(2,1)S(1)}, bf16[172,8,256]{2,1,0:T(8,128)(2,1)S(1)}, u32[]{:S(2)}, u32[]{:S(2)}) collective-permute-start(bf16[172,8,256]{2,1,0:T(8,128)(2,1)S(1)} %get-tuple-element.338), channel_id=1, source_target_pairs={{0,4},{1,5},{2,6},{3,7},{4,0},{5,1},{6,2},{7,3},{8,12},{9,13},{10,... | collective-permute-start | bytes 2113544 | tf_op jit(solution)/shard_map/cond/branch_1_fun/ppermute | solution.py:35
  358.9 11.3 %collective-permute-start.6 = (bf16[15,29,256]{2,0,1:T(8,128)(2,1)S(1)}, bf16[15,29,256]{2,0,1:T(8,128)(2,1)S(1)}, u32[]{:S(2)}, u32[]{:S(2)}) collective-permute-start(bf16[15,29,256]{2,0,1:T(8,128)(2,1)S(1)} %get-tuple-element.415), channel_id=1, source_target_pairs={{0,1},{1,2},{2,3},{3,4},{4,5},{5,6},{6,7},{7,0},{8,9},{9,10},{10,1... | collective-permute-start | bytes 668168 | tf_op jit(solution)/shard_map/cond/branch_1_fun/ppermute | solution.py:35
  360.1 12.4 %collective-permute-start.7 = (bf16[15,29,256]{2,0,1:T(8,128)(2,1)S(1)}, bf16[15,29,256]{2,0,1:T(8,128)(2,1)S(1)}, u32[]{:S(2)}, u32[]{:S(2)}) collective-permute-start(bf16[15,29,256]{2,0,1:T(8,128)(2,1)S(1)} %get-tuple-element.414), channel_id=1, source_target_pairs={{0,7},{1,0},{2,1},{3,2},{4,3},{5,4},{6,5},{7,6},{8,15},{9,8},{10,9... | collective-permute-start | bytes 668168 | tf_op jit(solution)/shard_map/cond/branch_1_fun/ppermute | solution.py:35
  373.0 5.0 collective-permute-start.8
  385.5 42.8 %all-to-all-start.4 = ((bf16[752,8,256]{2,1,0:T(8,128)(2,1)}), bf16[752,8,256]{2,1,0:T(8,128)(2,1)S(1)}, u32[]{:S(2)}, u32[]{:S(2)}) async-start(bf16[752,8,256]{2,1,0:T(8,128)(2,1)} %copy-done.29), calls=%async_computation.4 | async-start | bytes 6160384 | tf_op jit(solution)/shard_map/cond/branch_1_fun/all_to_all | solution.py:425
  432.6 33.5 %collective-permute-start.10 = (bf16[172,8,256]{2,1,0:T(8,128)(2,1)S(1)}, bf16[172,8,256]{2,1,0:T(8,128)(2,1)S(1)}, u32[]{:S(2)}, u32[]{:S(2)}) collective-permute-start(bf16[172,8,256]{2,1,0:T(8,128)(2,1)S(1)} %get-tuple-element.342), channel_id=1, source_target_pairs={{0,4},{1,5},{2,6},{3,7},{4,0},{5,1},{6,2},{7,3},{8,12},{9,13},{10,... | collective-permute-start | bytes 2113544 | tf_op jit(solution)/shard_map/cond/branch_1_fun/ppermute | solution.py:35
  513.7 11.3 %collective-permute-start.11 = (bf16[15,29,256]{2,0,1:T(8,128)(2,1)S(1)}, bf16[15,29,256]{2,0,1:T(8,128)(2,1)S(1)}, u32[]{:S(2)}, u32[]{:S(2)}) collective-permute-start(bf16[15,29,256]{2,0,1:T(8,128)(2,1)S(1)} %get-tuple-element.413), channel_id=1, source_target_pairs={{0,1},{1,2},{2,3},{3,4},{4,5},{5,6},{6,7},{7,0},{8,9},{9,10},{10,1... | collective-permute-start | bytes 668168 | tf_op jit(solution)/shard_map/cond/branch_1_fun/ppermute | solution.py:35
  514.9 12.4 %collective-permute-start.12 = (bf16[15,29,256]{2,0,1:T(8,128)(2,1)S(1)}, bf16[15,29,256]{2,0,1:T(8,128)(2,1)S(1)}, u32[]{:S(2)}, u32[]{:S(2)}) collective-permute-start(bf16[15,29,256]{2,0,1:T(8,128)(2,1)S(1)} %get-tuple-element.412), channel_id=1, source_target_pairs={{0,7},{1,0},{2,1},{3,2},{4,3},{5,4},{6,5},{7,6},{8,15},{9,8},{10,9... | collective-permute-start | bytes 668168 | tf_op jit(solution)/shard_map/cond/branch_1_fun/ppermute | solution.py:35
  (44 other events, 542.1 us)

commit v6 on v5

--- a/solution.py
+++ b/solution.py
@@ -47,46 +47,41 @@
     return [pl.BlockSpec(memory_space=pl.ANY)] * len(after)
 
 
-def canonical(places, matrices, shapes):
-    cells, nodes = places.shape
-    rows = shapes.shape[1]
-
-    def body(place_ref, matrix_ref, shape_ref, stiff_ref, turned_ref, straight_ref):
-        spots = lax.broadcasted_iota(jnp.int32, (nodes, nodes), 0)
-        pick = (spots == place_ref[0]).astype(BF16)
-        last = (((1,), (1,)), ((), ()))
+def pick_matrix(place_ref, nodes):
+    spots = lax.broadcasted_iota(jnp.int32, (nodes, nodes), 0)
+    return (spots == place_ref[0]).astype(BF16)
+
+
+LAST = (((1,), (1,)), ((), ()))
+
+
+def canonical(places, matrices, shapes, after):
+    cells, rows, nodes = shapes.shape
+
+    def body(place_ref, matrix_ref, shape_ref, *refs):
+        stiff_ref, turned_ref = refs[len(after) :]
+        pick = pick_matrix(place_ref, nodes)
         half = jnp.dot(pick, matrix_ref[0], preferred_element_type=F32).astype(BF16)
-        stiff_ref[0] = lax.dot_general(
-            half, pick, last, preferred_element_type=F32
-        ).astype(BF16)
-        turned_ref[0] = lax.dot_general(
-            pick, shape_ref[0], last, preferred_element_type=F32
-        ).astype(BF16)
-        straight_ref[0] = lax.dot_general(
-            shape_ref[0], pick, last, preferred_element_type=F32
-        ).astype(BF16)
+        full = lax.dot_general(half, pick, LAST, preferred_element_type=F32)
+        stiff_ref[0] = full.astype(BF16)
+        flipped = lax.dot_general(pick, shape_ref[0], LAST, preferred_element_type=F32)
+        turned_ref[0] = flipped.astype(BF16)
+
+    def block(shape):
+        return pl.BlockSpec((1,) + shape, lambda c: (c, 0, 0))
 
     return pl.pallas_call(
         body,
         grid=(cells,),
-        in_specs=[
-            pl.BlockSpec((1, 1, nodes), lambda c: (c, 0, 0)),
-            pl.BlockSpec((1, nodes, nodes), lambda c: (c, 0, 0)),
-            pl.BlockSpec((1, rows, nodes), lambda c: (c, 0, 0)),
-        ],
-        out_specs=[
-            pl.BlockSpec((1, nodes, nodes), lambda c: (c, 0, 0)),
-            pl.BlockSpec((1, nodes, rows), lambda c: (c, 0, 0)),
-            pl.BlockSpec((1, rows, nodes), lambda c: (c, 0, 0)),
-        ],
+        in_specs=[block((1, nodes)), block((nodes, nodes)), block((rows, nodes))] + unread(after),
+        out_specs=[block((nodes, nodes)), block((nodes, rows))],
         out_shape=[
             jax.ShapeDtypeStruct((cells, nodes, nodes), BF16),
             jax.ShapeDtypeStruct((cells, nodes, rows), BF16),
-            jax.ShapeDtypeStruct((cells, rows, nodes), BF16),
         ],
         compiler_params=pltpu.CompilerParams(vmem_limit_bytes=GRANT),
         name="canonical",
-    )(places.reshape(cells, 1, nodes), matrices, shapes)
+    )(places, matrices, shapes, *after)
 
 
 def spread(mixers, after):
@@ -121,7 +116,7 @@
     )(mixers, *after)
 
 
-def project(field, straight, starts, room, cz, per_atom):
+def project(field, straight, starts, room, cz, per_atom, places=None):
     cells, rows, nodes = straight.shape
     side = field.shape[2]
     deg = side - 1
@@ -129,40 +124,49 @@
     per_cell = rows // per_atom
     width = breadth // PARTS
     units = per_atom // UNIT
-
-    def body(starts_ref, field_ref, straight_ref, local_ref, *out_refs):
+    raw = places is not None
+
+    def body(starts_ref, field_ref, straight_ref, *refs):
+        if raw:
+            place_ref, grid_ref, *refs = refs
+        local_ref, *out_refs = refs
         c = pl.program_id(0)
         u = c // cz * deg
         w = c % cz * deg
         block = field_ref[pl.ds(u, side), pl.ds(w, side)]
         local = block.reshape(nodes, breadth).astype(BF16)
         local_ref[0] = local
-        values = jnp.dot(straight_ref[0], local, preferred_element_type=F32)
+        rows_of = straight_ref[0]
+        if raw:
+            pick = pick_matrix(place_ref, nodes)
+            rows_of = lax.dot_general(rows_of, pick, LAST, preferred_element_type=F32)
+            rows_of = rows_of.astype(BF16)
+            grid_ref[0] = rows_of
+        values = jnp.dot(rows_of, local, preferred_element_type=F32)
         for k in range(per_cell):
             start = starts_ref[c * per_cell + k]
             for s, out_ref in enumerate(out_refs):
                 piece = values[k * per_atom : (k + 1) * per_atom, s * width : (s + 1) * width]
                 out_ref[pl.ds(start, units)] = piece.reshape(units, UNIT, width).astype(BF16)
 
+    def block(shape):
+        return pl.BlockSpec((1,) + shape, lambda c: (c, 0, 0))
+
+    turning = [jax.ShapeDtypeStruct(straight.shape, BF16)] if raw else []
     return pl.pallas_call(
         body,
         grid=(cells,),
-        in_specs=[
-            smem(),
-            whole(field.shape),
-            pl.BlockSpec((1, rows, nodes), lambda c: (c, 0, 0)),
-        ],
-        out_specs=[
-            pl.BlockSpec((1, nodes, breadth), lambda c: (c, 0, 0)),
-        ]
+        in_specs=[smem(), whole(field.shape), block((rows, nodes))]
+        + ([block((1, nodes))] if raw else []),
+        out_specs=([block((rows, nodes))] if raw else [])
+        + [block((nodes, breadth))]
         + [whole((room, UNIT, width))] * PARTS,
-        out_shape=[
-            jax.ShapeDtypeStruct((cells, nodes, breadth), BF16),
-        ]
+        out_shape=turning
+        + [jax.ShapeDtypeStruct((cells, nodes, breadth), BF16)]
         + [jax.ShapeDtypeStruct((room, UNIT, width), BF16)] * PARTS,
         compiler_params=pltpu.CompilerParams(vmem_limit_bytes=GRANT),
         name="project",
-    )(starts, field, straight)
+    )(starts, field, straight, *([places] if raw else []))
 
 
 def stiffen(stiff, local, extended, cz):
@@ -544,7 +548,7 @@
     node_v = node_map // layers % (span_y + 1)
     node_u = node_map // (layers * (span_y + 1)) - cell_ids // cz * deg
     places = (node_u * side + node_w) * side + node_v
-    stiff, turned, straight = canonical(places, matrices, shapes)
+    places = places.reshape(cells, 1, nodes)
 
     row_next = shifted(orbitals[:1], ("gx",), (-1,))
     column_next = shifted(orbitals[:, :1], ("gy",), (-1,))
@@ -559,21 +563,27 @@
     grid = jnp.transpose(widened, (0, 2, 1, 3)).astype(F32)
     extended = grid.shape[:3]
 
-    def advance(field, older, scale, mixing, cap, span):
+    def advance(field, older, scale, known, cap, span):
         room = senders * cap
         starts = own * cap + offsets
         begins = (places_in + jnp.arange(senders)[:, None] * cap).reshape(slots)
         tables = (ids, begins, filled, spots, shared)
-        local, *outgoing = project(field, straight, starts, room, cz, per_atom)
-        if mixing is None:
-            mixing = spread(mixers, (local,))
+        if known is None:
+            straight, local, *outgoing = project(field, shapes, starts, room, cz, per_atom, places)
+        else:
+            straight, stiff, turned, *mixing = known
+            local, *outgoing = project(field, straight, starts, room, cz, per_atom)
+        if known is None:
+            stiff, turned = canonical(places, matrices, shapes, (local,))
+            mixing = spread(mixers, (turned,))
         image = stiffen(stiff, local, extended, cz)
-        after = (image,)
+        after = ()
         gathered = []
         for packet in outgoing:
             incoming = exchange(packet)
             gathered.append(merge(incoming, tables, atoms, units, span, after))
             after = (gathered[-1][0],)
+        after = after + (image,)
         answers = []
         for sums, sent in gathered:
             others = shifted(sent, ("gy",), (half,))
@@ -587,25 +597,23 @@
             )
             after = (totals[-1],)
         total = jnp.concatenate(totals, axis=-1) if PARTS > 1 else totals[0]
-        return completed(total, scale, older), mixing
+        return completed(total, scale, older), (straight, stiff, turned, *mixing)
 
     def packed():
-        mixing = None
+        known = None
         older, field = None, grid
         for step in range(FILTER_DEGREE):
             scale = jnp.full((1,), 1.0 if step == 0 else 2.0, F32)
-            image, mixing = advance(field, older, scale, mixing, cap, span)
+            image, known = advance(field, older, scale, known, cap, span)
             older, field = field, image
         return field[:span_x, :, :span_y].astype(BF16)
 
     def roomy():
-        mixing = spread(mixers, ())
-
         def step(at, fields):
             older, field = fields
             scale = jnp.where(at == 0, 1.0, 2.0).astype(F32).reshape(1)
             image, _ = advance(
-                field, older, scale, mixing, (each + 1) * units, (atoms + 1) * units
+                field, older, scale, None, (each + 1) * units, (atoms + 1) * units
             )
             return field, image
 

time: 541 us -> 515 us (0.952)
  blocking collectives: 120 us -> 201 us
  waiting for transfers between devices: 227 us -> 172 us
  local copies, waits for them, and re-layouts: 47 us -> 19.4 us
  starting transfers between devices: 53.7 us -> 38.2 us
  Pallas kernels: 76 us -> 67.4 us
    all_to_all x3 -> x5, blocking collectives: 120 us -> 201 us  [exchange(): lax.all_to_all(x, both, split_axis=0, concat_axis=0, axis_index_groups=te...]
    all_to_all x3 -> x1, waiting for transfers between devices: 88.7 us -> 38.9 us  [exchange(): lax.all_to_all(x, both, split_axis=0, concat_axis=0, axis_index_groups=te...]
    another operation x70 -> x16, local copies, waits for them, and re-layouts: 28.1 us -> 4.89 us
    pallas_call x3, Pallas kernels: 18.1 us -> 8.09 us  [stiffen(): pl.pallas_call(body, grid=(cells,), in_specs=[pl.BlockSpec((1, nodes, nod...]
    ppermute x22, starting transfers between devices: 32.5 us -> 23.6 us  [shifted(): return lax.ppermute(x, axes if len(axes) > 1 else axes[0], pairs)]
    all_to_all x3 -> x1, starting transfers between devices: 11.2 us -> 3.74 us  [exchange(): lax.all_to_all(x, both, split_axis=0, concat_axis=0, axis_index_groups=te...]
  transfers between devices with their start and end apart: 29 -> 27, of which waited for: 22 -> 17; matrix products, arithmetic and copies ran while one was open for 3% -> 3% of each run, Pallas kernels for 6% -> 4%
where the time goes in v6:
time: 515 us; the launch traced here: 514 us
  blocking collectives  201 us (39%)
  waiting for transfers between devices  172 us (33%)
  Pallas kernels  67.4 us (13%)
  starting transfers between devices  38.2 us (7%)
  local copies, waits for them, and re-layouts  19.4 us (4%)
  other arithmetic  10.4 us (2%)
    all_to_all x5, blocking collectives, exchange(): lax.all_to_all(x, both, split_axis=0, concat_axis=0, axis_index_groups=te...  201 us
    ppermute x22, waiting for transfers between devices, shifted(): return lax.ppermute(x, axes if len(axes) > 1 else axes[0], pairs)  133 us
    all_to_all x1, waiting for transfers between devices, exchange(): lax.all_to_all(x, both, split_axis=0, concat_axis=0, axis_index_groups=te...  38.9 us
    ppermute x22, starting transfers between devices, shifted(): return lax.ppermute(x, axes if len(axes) > 1 else axes[0], pairs)  23.6 us
    pallas_call x3, Pallas kernels, project(): pl.pallas_call(body, grid=(cells,), in_specs=[smem(), whole(field.shape),...  15.8 us
  transfers between devices with their start and end apart: 27, of which 17 were waited for; matrix products, arithmetic and copies ran while one was open for 3% of the time, Pallas kernels for 4%

profile of v6, /device:TPU:0, one launch (start us, length us, event | category | flops | bytes accessed | tf_op | source)
XLA Modules:
  0.0 513.9 jit_solution(8193503813603112950)
XLA Ops:
  2.1 7.3 %all-to-all-start.8 = ((s32[32,1,160]{2,1,0:T(1,128)}), s32[32,1,160]{2,1,0:T(1,128)S(1)}, u32[]{:S(2)}, u32[]{:S(2)}) async-start(s32[32,1,160]{2,1,0:T(1,128)} %broadcast_in_dim.98), calls=%async_computation.8 | async-start | bytes 65536 | tf_op jit(solution)/shard_map/all_to_all | solution.py:441
  40.3 8.8 %collective-permute-done.27 = bf16[14,1,29,256]{3,1,2,0:T(2,128)(2,1)S(1)} collective-permute-done((bf16[14,1,29,256]{3,1,2,0:T(2,128)(2,1)S(1)}, bf16[14,1,29,256]{3,1,2,0:T(2,128)(2,1)S(1)}, u32[]{:S(2)}, u32[]{:S(2)}) %collective-permute-start.27) | collective-permute-done | bytes 207904 | tf_op jit(solution)/shard_map/ppermute | solution.py:35
  52.5 457.6 %conditional.2 = (f32[15,29,8,256]{3,2,1,0:T(8,128)}) conditional(s32[]{:T(128)} %convert_element_type.396, (s32[128]{0:T(128)S(1)}, s32[128]{0:T(128)S(1)}, bf16[8,512,512]{2,1,0:T(8,128)(2,1)}, s32[8,1,512]{2,1,0:T(1,128)S(1)}, bf16[8,512,512]{2,1,0:T(8,128)(2,1)}, /*index=5*/s32[16,16]{1,0:T(8,128)S(1)}, s32[256]{0:T(256)S(1)}, ...), branch_computations={%region_13.16_spmd, %region_16.17_spmd} | conditional | flops 2405904 | bytes 163142048
  52.7 9.6 %project.8 = (bf16[8,512,512]{2,1,0:T(8,128)(2,1)S(1)}, bf16[8,512,256]{2,1,0:T(8,128)(2,1)S(1)}, bf16[752,8,256]{2,1,0:T(8,128)(2,1)S(1)}) custom-call(s32[128]{0:T(128)S(1)} %multiply_add_fusion.1.starts_ref, f32[15,29,8,256]{3,2,1,0:T(8,128)} %get-tuple-element.311.field_ref.refs_0_, bf16[8,512,512]{2,1,0:T(8,128)(2,1)} %get-tuple-element.310.straight_ref.shape_ref, ...), custom_call_target="tpu_custom_call" | custom-call | tf_op jit(solution)/shard_map/cond/branch_1_fun/project/pallas_call | solution.py:156
  67.2 3.7 all-to-all-start
  71.1 38.9 %all-to-all-done.incoming_ref = bf16[752,8,256]{2,1,0:T(8,128)(2,1)S(1)} async-done(((bf16[752,8,256]{2,1,0:T(8,128)(2,1)}), bf16[752,8,256]{2,1,0:T(8,128)(2,1)S(1)}, u32[]{:S(2)}, u32[]{:S(2)}) %all-to-all-start) | async-done | bytes 3080224 | tf_op jit(solution)/shard_map/cond/branch_1_fun/all_to_all | solution.py:429
  114.0 9.9 %canonical.6 = (bf16[8,512,512]{2,1,0:T(8,128)(2,1)S(1)}, bf16[8,512,512]{2,1,0:T(8,128)(2,1)S(1)}) custom-call(s32[8,1,512]{2,1,0:T(1,128)S(1)} %get-tuple-element.308.refs_0_.place_ref, bf16[8,512,512]{2,1,0:T(8,128)(2,1)} %get-tuple-element.309.matrix_ref, bf16[8,512,512]{2,1,0:T(8,128)(2,1)} %get-tuple-element.310.straight_ref.shape_ref, ...), custom_call_target="tpu_custom_call" | custom-call | tf_op jit(solution)/shard_map/cond/branch_1_fun/canonical/pallas_call | solution.py:73
  128.1 17.6 %collective-permute-done.others_ref = bf16[172,8,256]{2,1,0:T(8,128)(2,1)S(1)} collective-permute-done((bf16[172,8,256]{2,1,0:T(8,128)(2,1)S(1)}, bf16[172,8,256]{2,1,0:T(8,128)(2,1)S(1)}, u32[]{:S(2)}, u32[]{:S(2)}) %collective-permute-start) | collective-permute-done | bytes 704544 | tf_op jit(solution)/shard_map/cond/branch_1_fun/ppermute | solution.py:35
  145.7 3.2 couple.4.refs_0_
  148.9 39.7 %all_to_all.45.answers_ref = bf16[752,8,256]{2,1,0:T(8,128)(2,1)S(1)} all-to-all(bf16[752,8,256]{2,1,0:T(8,128)(2,1)S(1)} %couple.4.refs_0_), channel_id=1, replica_groups={{0,1,2,3,8,9,10,11,16,17,18,19,24,25,26,27},{4,5,6,7,12,13,14,15,20,21,..., dimensions={0} | all-to-all | bytes 6160384 | tf_op jit(solution)/shard_map/cond/branch_1_fun/all_to_all | solution.py:429
  188.6 3.4 apply.4.total_ref
  195.8 10.5 %collective-permute-done.2 = bf16[15,29,256]{2,0,1:T(8,128)(2,1)S(1)} collective-permute-done((bf16[15,29,256]{2,0,1:T(8,128)(2,1)S(1)}, bf16[15,29,256]{2,0,1:T(8,128)(2,1)S(1)}, u32[]{:S(2)}, u32[]{:S(2)}) %collective-permute-start.2) | collective-permute-done | bytes 222752 | tf_op jit(solution)/shard_map/cond/branch_1_fun/ppermute | solution.py:35
  215.7 41.2 %all_to_all.46.incoming_ref = bf16[752,8,256]{2,1,0:T(8,128)(2,1)S(1)} all-to-all(bf16[752,8,256]{2,1,0:T(8,128)(2,1)S(1)} %get-tuple-element.327), channel_id=1, replica_groups={{0,1,2,3,8,9,10,11,16,17,18,19,24,25,26,27},{4,5,6,7,12,13,14,15,20,21,..., dimensions={0} | all-to-all | bytes 6160384 | tf_op jit(solution)/shard_map/cond/branch_1_fun/all_to_all | solution.py:429
  263.9 29.5 %collective-permute-done.5.others_ref = bf16[172,8,256]{2,1,0:T(8,128)(2,1)S(1)} collective-permute-done((bf16[172,8,256]{2,1,0:T(8,128)(2,1)S(1)}, bf16[172,8,256]{2,1,0:T(8,128)(2,1)S(1)}, u32[]{:S(2)}, u32[]{:S(2)}) %collective-permute-start.5) | collective-permute-done | bytes 704544 | tf_op jit(solution)/shard_map/cond/branch_1_fun/ppermute | solution.py:35
  293.4 3.2 couple.5.refs_0_
  296.6 39.5 %all_to_all.47.answers_ref = bf16[752,8,256]{2,1,0:T(8,128)(2,1)S(1)} all-to-all(bf16[752,8,256]{2,1,0:T(8,128)(2,1)S(1)} %couple.5.refs_0_), channel_id=1, replica_groups={{0,1,2,3,8,9,10,11,16,17,18,19,24,25,26,27},{4,5,6,7,12,13,14,15,20,21,..., dimensions={0} | all-to-all | bytes 6160384 | tf_op jit(solution)/shard_map/cond/branch_1_fun/all_to_all | solution.py:429
  336.1 3.4 apply.5.total_ref
  343.0 10.9 %collective-permute-done.7 = bf16[15,29,256]{2,0,1:T(8,128)(2,1)S(1)} collective-permute-done((bf16[15,29,256]{2,0,1:T(8,128)(2,1)S(1)}, bf16[15,29,256]{2,0,1:T(8,128)(2,1)S(1)}, u32[]{:S(2)}, u32[]{:S(2)}) %collective-permute-start.7) | collective-permute-done | bytes 222752 | tf_op jit(solution)/shard_map/cond/branch_1_fun/ppermute | solution.py:35
  363.5 41.0 %all_to_all.48.incoming_ref = bf16[752,8,256]{2,1,0:T(8,128)(2,1)S(1)} all-to-all(bf16[752,8,256]{2,1,0:T(8,128)(2,1)S(1)} %get-tuple-element.331), channel_id=1, replica_groups={{0,1,2,3,8,9,10,11,16,17,18,19,24,25,26,27},{4,5,6,7,12,13,14,15,20,21,..., dimensions={0} | all-to-all | bytes 6160384 | tf_op jit(solution)/shard_map/cond/branch_1_fun/all_to_all | solution.py:429
  411.3 29.6 %collective-permute-done.10.others_ref = bf16[172,8,256]{2,1,0:T(8,128)(2,1)S(1)} collective-permute-done((bf16[172,8,256]{2,1,0:T(8,128)(2,1)S(1)}, bf16[172,8,256]{2,1,0:T(8,128)(2,1)S(1)}, u32[]{:S(2)}, u32[]{:S(2)}) %collective-permute-start.10) | collective-permute-done | bytes 704544 | tf_op jit(solution)/shard_map/cond/branch_1_fun/ppermute | solution.py:35
  441.0 3.2 couple.6.refs_0_
  444.2 39.5 %all_to_all.49.answers_ref = bf16[752,8,256]{2,1,0:T(8,128)(2,1)S(1)} all-to-all(bf16[752,8,256]{2,1,0:T(8,128)(2,1)S(1)} %couple.6.refs_0_), channel_id=1, replica_groups={{0,1,2,3,8,9,10,11,16,17,18,19,24,25,26,27},{4,5,6,7,12,13,14,15,20,21,..., dimensions={0} | all-to-all | bytes 6160384 | tf_op jit(solution)/shard_map/cond/branch_1_fun/all_to_all | solution.py:429
  483.7 3.4 apply.6.total_ref
  490.4 11.0 %collective-permute-done.12 = bf16[15,29,256]{2,0,1:T(8,128)(2,1)S(1)} collective-permute-done((bf16[15,29,256]{2,0,1:T(8,128)(2,1)S(1)}, bf16[15,29,256]{2,0,1:T(8,128)(2,1)S(1)}, u32[]{:S(2)}, u32[]{:S(2)}) %collective-permute-start.12) | collective-permute-done | bytes 222752 | tf_op jit(solution)/shard_map/cond/branch_1_fun/ppermute | solution.py:35
  (179 shorter events, 101.9 us)
Async XLA Ops:
  2.1 18.7 %all-to-all-start.8 = ((s32[32,1,160]{2,1,0:T(1,128)}), s32[32,1,160]{2,1,0:T(1,128)S(1)}, u32[]{:S(2)}, u32[]{:S(2)}) async-start(s32[32,1,160]{2,1,0:T(1,128)} %broadcast_in_dim.98), calls=%async_computation.8 | async-start | bytes 65536 | tf_op jit(solution)/shard_map/all_to_all | solution.py:441
  10.7 19.3 %collective-permute-start.20 = (f32[256,128]{1,0:T(8,128)S(1)}, f32[256,128]{1,0:T(8,128)S(1)}, u32[]{:S(2)}, u32[]{:S(2)}) collective-permute-start(f32[256,128]{1,0:T(8,128)S(1)} %reshape.673), channel_id=1, source_target_pairs={{0,4},{1,5},{2,6},{3,7},{4,0},{5,1},{6,2},{7,3},{8,12},{9,13},{10,... | collective-permute-start | bytes 393224 | tf_op jit(solution)/shard_map/ppermute | solution.py:35
  15.9 22.2 %collective-permute-start.29 = (bf16[1,1,29,256]{3,1,2,0:T(2,128)(2,1)S(1)}, bf16[1,1,29,256]{3,1,2,0:T(2,128)(2,1)S(1)}, u32[]{:S(2)}, u32[]{:S(2)}) collective-permute-start(bf16[1,1,29,256]{3,1,2,0:T(2,128)(2,1)S(1)} %slice.373), channel_id=1, source_target_pairs={{0,31},{1,24},{2,25},{3,26},{4,27},{5,28},{6,29},{7,30},{8,7},{9,0... | collective-permute-start | bytes 44552 | tf_op jit(solution)/shard_map/ppermute | solution.py:35
  19.3 21.1 %collective-permute-start.28 = (bf16[1,7,29,256]{3,1,2,0:T(8,128)(2,1)}, bf16[1,7,29,256]{3,1,2,0:T(8,128)(2,1)S(1)}, u32[]{:S(2)}, u32[]{:S(2)}) collective-permute-start(bf16[1,7,29,256]{3,1,2,0:T(8,128)(2,1)} %slice.372), channel_id=1, source_target_pairs={{0,24},{8,0},{16,8},{24,16},{1,25},{9,1},{17,9},{25,17},{2,26},{10... | collective-permute-start | bytes 311816 | tf_op jit(solution)/shard_map/ppermute | solution.py:35
  30.0 5.2 %collective-permute-start.23 = (f32[256,128]{1,0:T(8,128)S(1)}, f32[256,128]{1,0:T(8,128)S(1)}, u32[]{:S(2)}, u32[]{:S(2)}) collective-permute-start(f32[256,128]{1,0:T(8,128)S(1)} %get-tuple-element.415), channel_id=1, source_target_pairs={{0,8},{8,16},{16,24},{24,0},{1,9},{9,17},{17,25},{25,1},{2,10},{10... | collective-permute-start | bytes 393224 | tf_op jit(solution)/shard_map/ppermute | solution.py:35
  30.1 6.4 %collective-permute-start.22 = (f32[256,128]{1,0:T(8,128)S(1)}, f32[256,128]{1,0:T(8,128)S(1)}, u32[]{:S(2)}, u32[]{:S(2)}) collective-permute-start(f32[256,128]{1,0:T(8,128)S(1)} %get-tuple-element.415), channel_id=1, source_target_pairs={{0,16},{8,24},{16,0},{24,8},{1,17},{9,25},{17,1},{25,9},{2,18},{10... | collective-permute-start | bytes 393224 | tf_op jit(solution)/shard_map/ppermute | solution.py:35
  30.7 6.0 %collective-permute-start.21 = (f32[256,128]{1,0:T(8,128)S(1)}, f32[256,128]{1,0:T(8,128)S(1)}, u32[]{:S(2)}, u32[]{:S(2)}) collective-permute-start(f32[256,128]{1,0:T(8,128)S(1)} %get-tuple-element.415), channel_id=1, source_target_pairs={{0,24},{8,0},{16,8},{24,16},{1,25},{9,1},{17,9},{25,17},{2,26},{10... | collective-permute-start | bytes 393224 | tf_op jit(solution)/shard_map/ppermute | solution.py:35
  35.2 13.9 %collective-permute-start.27 = (bf16[14,1,29,256]{3,1,2,0:T(2,128)(2,1)S(1)}, bf16[14,1,29,256]{3,1,2,0:T(2,128)(2,1)S(1)}, u32[]{:S(2)}, u32[]{:S(2)}) collective-permute-start(bf16[14,1,29,256]{3,1,2,0:T(2,128)(2,1)S(1)} %slice.371), channel_id=1, source_target_pairs={{0,7},{1,0},{2,1},{3,2},{4,3},{5,4},{6,5},{7,6},{8,15},{9,8},{10,9... | collective-permute-start | bytes 623624 | tf_op jit(solution)/shard_map/ppermute | solution.py:35
  36.8 15.0 %collective-permute-start.26 = (f32[256,128]{1,0:T(8,128)S(1)}, f32[256,128]{1,0:T(8,128)S(1)}, u32[]{:S(2)}, u32[]{:S(2)}) collective-permute-start(f32[256,128]{1,0:T(8,128)S(1)} %select_select_fusion.1), channel_id=1, source_target_pairs={{3,0},{0,1},{1,2},{2,3},{7,4},{4,5},{5,6},{6,7},{11,8},{8,9},{9,10... | collective-permute-start | bytes 393224 | tf_op jit(solution)/shard_map/ppermute | solution.py:540
  37.3 14.5 %collective-permute-start.25 = (f32[256,128]{1,0:T(8,128)S(1)}, f32[256,128]{1,0:T(8,128)S(1)}, u32[]{:S(2)}, u32[]{:S(2)}) collective-permute-start(f32[256,128]{1,0:T(8,128)S(1)} %select_select_fusion.1), channel_id=1, source_target_pairs={{2,0},{3,1},{0,2},{1,3},{6,4},{7,5},{4,6},{5,7},{10,8},{11,9},{8,1... | collective-permute-start | bytes 393224 | tf_op jit(solution)/shard_map/ppermute | solution.py:540
  38.0 13.8 %collective-permute-start.24 = (f32[256,128]{1,0:T(8,128)S(1)}, f32[256,128]{1,0:T(8,128)S(1)}, u32[]{:S(2)}, u32[]{:S(2)}) collective-permute-start(f32[256,128]{1,0:T(8,128)S(1)} %select_select_fusion.1), channel_id=1, source_target_pairs={{1,0},{2,1},{3,2},{0,3},{5,4},{6,5},{7,6},{4,7},{9,8},{10,9},{11,1... | collective-permute-start | bytes 393224 | tf_op jit(solution)/shard_map/ppermute | solution.py:540
  67.2 42.8 %all-to-all-start = ((bf16[752,8,256]{2,1,0:T(8,128)(2,1)}), bf16[752,8,256]{2,1,0:T(8,128)(2,1)S(1)}, u32[]{:S(2)}, u32[]{:S(2)}) async-start(bf16[752,8,256]{2,1,0:T(8,128)(2,1)} %copy-done.7), calls=%async_computation | async-start | bytes 6160384 | tf_op jit(solution)/shard_map/cond/branch_1_fun/all_to_all | solution.py:429
  112.2 33.5 %collective-permute-start = (bf16[172,8,256]{2,1,0:T(8,128)(2,1)S(1)}, bf16[172,8,256]{2,1,0:T(8,128)(2,1)S(1)}, u32[]{:S(2)}, u32[]{:S(2)}) collective-permute-start(bf16[172,8,256]{2,1,0:T(8,128)(2,1)S(1)} %get-tuple-element.321), channel_id=1, source_target_pairs={{0,4},{1,5},{2,6},{3,7},{4,0},{5,1},{6,2},{7,3},{8,12},{9,13},{10,... | collective-permute-start | bytes 2113544 | tf_op jit(solution)/shard_map/cond/branch_1_fun/ppermute | solution.py:35
  193.1 13.2 %collective-permute-start.2 = (bf16[15,29,256]{2,0,1:T(8,128)(2,1)S(1)}, bf16[15,29,256]{2,0,1:T(8,128)(2,1)S(1)}, u32[]{:S(2)}, u32[]{:S(2)}) collective-permute-start(bf16[15,29,256]{2,0,1:T(8,128)(2,1)S(1)} %get-tuple-element.400), channel_id=1, source_target_pairs={{0,7},{1,0},{2,1},{3,2},{4,3},{5,4},{6,5},{7,6},{8,15},{9,8},{10,9... | collective-permute-start | bytes 668168 | tf_op jit(solution)/shard_map/cond/branch_1_fun/ppermute | solution.py:35
  195.7 10.6 %collective-permute-start.1 = (bf16[15,29,256]{2,0,1:T(8,128)(2,1)S(1)}, bf16[15,29,256]{2,0,1:T(8,128)(2,1)S(1)}, u32[]{:S(2)}, u32[]{:S(2)}) collective-permute-start(bf16[15,29,256]{2,0,1:T(8,128)(2,1)S(1)} %get-tuple-element.401), channel_id=1, source_target_pairs={{0,1},{1,2},{2,3},{3,4},{4,5},{5,6},{6,7},{7,0},{8,9},{9,10},{10,1... | collective-permute-start | bytes 668168 | tf_op jit(solution)/shard_map/cond/branch_1_fun/ppermute | solution.py:35
  206.8 4.7 collective-permute-start.3
  259.1 34.3 %collective-permute-start.5 = (bf16[172,8,256]{2,1,0:T(8,128)(2,1)S(1)}, bf16[172,8,256]{2,1,0:T(8,128)(2,1)S(1)}, u32[]{:S(2)}, u32[]{:S(2)}) collective-permute-start(bf16[172,8,256]{2,1,0:T(8,128)(2,1)S(1)} %get-tuple-element.329), channel_id=1, source_target_pairs={{0,4},{1,5},{2,6},{3,7},{4,0},{5,1},{6,2},{7,3},{8,12},{9,13},{10,... | collective-permute-start | bytes 2113544 | tf_op jit(solution)/shard_map/cond/branch_1_fun/ppermute | solution.py:35
  340.6 13.2 %collective-permute-start.7 = (bf16[15,29,256]{2,0,1:T(8,128)(2,1)S(1)}, bf16[15,29,256]{2,0,1:T(8,128)(2,1)S(1)}, u32[]{:S(2)}, u32[]{:S(2)}) collective-permute-start(bf16[15,29,256]{2,0,1:T(8,128)(2,1)S(1)} %get-tuple-element.398), channel_id=1, source_target_pairs={{0,7},{1,0},{2,1},{3,2},{4,3},{5,4},{6,5},{7,6},{8,15},{9,8},{10,9... | collective-permute-start | bytes 668168 | tf_op jit(solution)/shard_map/cond/branch_1_fun/ppermute | solution.py:35
  342.9 11.0 %collective-permute-start.6 = (bf16[15,29,256]{2,0,1:T(8,128)(2,1)S(1)}, bf16[15,29,256]{2,0,1:T(8,128)(2,1)S(1)}, u32[]{:S(2)}, u32[]{:S(2)}) collective-permute-start(bf16[15,29,256]{2,0,1:T(8,128)(2,1)S(1)} %get-tuple-element.399), channel_id=1, source_target_pairs={{0,1},{1,2},{2,3},{3,4},{4,5},{5,6},{6,7},{7,0},{8,9},{9,10},{10,1... | collective-permute-start | bytes 668168 | tf_op jit(solution)/shard_map/cond/branch_1_fun/ppermute | solution.py:35
  354.3 4.6 collective-permute-start.8
  406.7 34.3 %collective-permute-start.10 = (bf16[172,8,256]{2,1,0:T(8,128)(2,1)S(1)}, bf16[172,8,256]{2,1,0:T(8,128)(2,1)S(1)}, u32[]{:S(2)}, u32[]{:S(2)}) collective-permute-start(bf16[172,8,256]{2,1,0:T(8,128)(2,1)S(1)} %get-tuple-element.333), channel_id=1, source_target_pairs={{0,4},{1,5},{2,6},{3,7},{4,0},{5,1},{6,2},{7,3},{8,12},{9,13},{10,... | collective-permute-start | bytes 2113544 | tf_op jit(solution)/shard_map/cond/branch_1_fun/ppermute | solution.py:35
  488.2 13.2 %collective-permute-start.12 = (bf16[15,29,256]{2,0,1:T(8,128)(2,1)S(1)}, bf16[15,29,256]{2,0,1:T(8,128)(2,1)S(1)}, u32[]{:S(2)}, u32[]{:S(2)}) collective-permute-start(bf16[15,29,256]{2,0,1:T(8,128)(2,1)S(1)} %get-tuple-element.396), channel_id=1, source_target_pairs={{0,7},{1,0},{2,1},{3,2},{4,3},{5,4},{6,5},{7,6},{8,15},{9,8},{10,9... | collective-permute-start | bytes 668168 | tf_op jit(solution)/shard_map/cond/branch_1_fun/ppermute | solution.py:35
  490.3 11.1 %collective-permute-start.11 = (bf16[15,29,256]{2,0,1:T(8,128)(2,1)S(1)}, bf16[15,29,256]{2,0,1:T(8,128)(2,1)S(1)}, u32[]{:S(2)}, u32[]{:S(2)}) collective-permute-start(bf16[15,29,256]{2,0,1:T(8,128)(2,1)S(1)} %get-tuple-element.397), channel_id=1, source_target_pairs={{0,1},{1,2},{2,3},{3,4},{4,5},{5,6},{6,7},{7,0},{8,9},{9,10},{10,1... | collective-permute-start | bytes 668168 | tf_op jit(solution)/shard_map/cond/branch_1_fun/ppermute | solution.py:35
  501.8 5.1 collective-permute-start.13
  (15 other events, 94.8 us)

commit v7 on v6

--- a/solution.py
+++ b/solution.py
@@ -12,7 +12,7 @@
 FILTER_DEGREE = 3
 PARTS = 1
 UNIT = 8
-TIGHT = 47
+TIGHT = 46
 NARROW = 172
 TURNS = 4
 MODE = "cond"
@@ -550,9 +550,9 @@
     places = (node_u * side + node_w) * side + node_v
     places = places.reshape(cells, 1, nodes)
 
-    row_next = shifted(orbitals[:1], ("gx",), (-1,))
-    column_next = shifted(orbitals[:, :1], ("gy",), (-1,))
-    corner_next = shifted(orbitals[:1, :1], both, (-1, -1))
+    row_next = shifted(orbitals[0], ("gx",), (-1,))[None]
+    column_next = shifted(orbitals[:, 0], ("gy",), (-1,))[:, None]
+    corner_next = shifted(orbitals[0, 0], both, (-1, -1))[None, None]
     widened = jnp.concatenate(
         [
             jnp.concatenate([orbitals, column_next], axis=1),

time: 515 us -> 509 us (0.988)
  waiting for transfers between devices: 172 us -> 166 us
    ppermute x22, waiting for transfers between devices: 133 us -> 124 us  [shifted(): return lax.ppermute(x, axes if len(axes) > 1 else axes[0], pairs)]
    ppermute x22, starting transfers between devices: 23.6 us -> 29.2 us  [shifted(): return lax.ppermute(x, axes if len(axes) > 1 else axes[0], pairs)]
  transfers between devices with their start and end apart: 27 -> 27, of which waited for: 17 -> 18; matrix products, arithmetic and copies ran while one was open for 3% -> 4% of each run, Pallas kernels for 4% -> 4%
where the time goes in v7:
time: 509 us; the launch traced here: 508 us
  blocking collectives  198 us (39%)
  waiting for transfers between devices  166 us (33%)
  Pallas kernels  67.3 us (13%)
  starting transfers between devices  39.2 us (8%)
  local copies, waits for them, and re-layouts  21.2 us (4%)
  other arithmetic  10.3 us (2%)
    all_to_all x5, blocking collectives, exchange(): lax.all_to_all(x, both, split_axis=0, concat_axis=0, axis_index_groups=te...  198 us
    ppermute x22, waiting for transfers between devices, shifted(): return lax.ppermute(x, axes if len(axes) > 1 else axes[0], pairs)  124 us
    all_to_all x1, waiting for transfers between devices, exchange(): lax.all_to_all(x, both, split_axis=0, concat_axis=0, axis_index_groups=te...  38.1 us
    ppermute x22, starting transfers between devices, shifted(): return lax.ppermute(x, axes if len(axes) > 1 else axes[0], pairs)  29.2 us
    pallas_call x3, Pallas kernels, project(): pl.pallas_call(body, grid=(cells,), in_specs=[smem(), whole(field.shape),...  15.8 us
  transfers between devices with their start and end apart: 27, of which 18 were waited for; matrix products, arithmetic and copies ran while one was open for 4% of the time, Pallas kernels for 4%

profile of v7, /device:TPU:0, one launch (start us, length us, event | category | flops | bytes accessed | tf_op | source)
XLA Modules:
  0.0 508.1 jit_solution(4879314331075480438)
XLA Ops:
  0.7 6.4 %collective-permute-start.29 = (bf16[29,256]{1,0:T(8,128)(2,1)S(1)}, bf16[29,256]{1,0:T(8,128)(2,1)S(1)}, u32[]{:S(2)}, u32[]{:S(2)}) collective-permute-start(bf16[29,256]{1,0:T(8,128)(2,1)S(1)} %slice_bitcast_fusion.34), channel_id=1, source_target_pairs={{0,31},{1,24},{2,25},{3,26},{4,27},{5,28},{6,29},{7,30},{8,7},{9,0... | collective-permute-start | bytes 44552 | tf_op jit(solution)/shard_map/ppermute | solution.py:35
  46.7 3.2 collective-permute-done.24
  50.6 453.8 %conditional.2 = (f32[15,29,8,256]{3,2,1,0:T(8,128)}) conditional(s32[]{:T(128)} %convert_element_type.396, (s32[128]{0:T(128)S(1)}, s32[128]{0:T(128)S(1)}, bf16[8,512,512]{2,1,0:T(8,128)(2,1)}, s32[8,1,512]{2,1,0:T(1,128)S(1)}, bf16[8,512,512]{2,1,0:T(8,128)(2,1)}, /*index=5*/s32[16,16]{1,0:T(8,128)S(1)}, s32[256]{0:T(256)S(1)}, ...), branch_computations={%region_13.16_spmd, %region_16.17_spmd} | conditional | flops 2405904 | bytes 162027936
  50.8 9.6 %project.8 = (bf16[8,512,512]{2,1,0:T(8,128)(2,1)S(1)}, bf16[8,512,256]{2,1,0:T(8,128)(2,1)S(1)}, bf16[736,8,256]{2,1,0:T(8,128)(2,1)S(1)}) custom-call(s32[128]{0:T(128)S(1)} %multiply_add_fusion.1.starts_ref, f32[15,29,8,256]{3,2,1,0:T(8,128)} %get-tuple-element.311.field_ref.refs_0_, bf16[8,512,512]{2,1,0:T(8,128)(2,1)} %get-tuple-element.310.straight_ref.shape_ref, ...), custom_call_target="tpu_custom_call" | custom-call | tf_op jit(solution)/shard_map/cond/branch_1_fun/project/pallas_call | solution.py:156
  65.3 3.7 all-to-all-start
  69.2 38.1 %all-to-all-done.incoming_ref = bf16[736,8,256]{2,1,0:T(8,128)(2,1)S(1)} async-done(((bf16[736,8,256]{2,1,0:T(8,128)(2,1)}), bf16[736,8,256]{2,1,0:T(8,128)(2,1)S(1)}, u32[]{:S(2)}, u32[]{:S(2)}) %all-to-all-start) | async-done | bytes 3014688 | tf_op jit(solution)/shard_map/cond/branch_1_fun/all_to_all | solution.py:429
  111.4 9.9 %canonical.6 = (bf16[8,512,512]{2,1,0:T(8,128)(2,1)S(1)}, bf16[8,512,512]{2,1,0:T(8,128)(2,1)S(1)}) custom-call(s32[8,1,512]{2,1,0:T(1,128)S(1)} %get-tuple-element.308.refs_0_.place_ref, bf16[8,512,512]{2,1,0:T(8,128)(2,1)} %get-tuple-element.309.matrix_ref, bf16[8,512,512]{2,1,0:T(8,128)(2,1)} %get-tuple-element.310.straight_ref.shape_ref, ...), custom_call_target="tpu_custom_call" | custom-call | tf_op jit(solution)/shard_map/cond/branch_1_fun/canonical/pallas_call | solution.py:73
  125.5 17.5 %collective-permute-done.others_ref = bf16[172,8,256]{2,1,0:T(8,128)(2,1)S(1)} collective-permute-done((bf16[172,8,256]{2,1,0:T(8,128)(2,1)S(1)}, bf16[172,8,256]{2,1,0:T(8,128)(2,1)S(1)}, u32[]{:S(2)}, u32[]{:S(2)}) %collective-permute-start) | collective-permute-done | bytes 704544 | tf_op jit(solution)/shard_map/cond/branch_1_fun/ppermute | solution.py:35
  143.1 3.2 couple.4.refs_0_
  146.3 39.2 %all_to_all.45.answers_ref = bf16[736,8,256]{2,1,0:T(8,128)(2,1)S(1)} all-to-all(bf16[736,8,256]{2,1,0:T(8,128)(2,1)S(1)} %couple.4.refs_0_), channel_id=1, replica_groups={{0,1,2,3,8,9,10,11,16,17,18,19,24,25,26,27},{4,5,6,7,12,13,14,15,20,21,..., dimensions={0} | all-to-all | bytes 6029312 | tf_op jit(solution)/shard_map/cond/branch_1_fun/all_to_all | solution.py:429
  185.5 3.4 apply.4.total_ref
  192.6 10.4 %collective-permute-done.2 = bf16[15,29,256]{2,0,1:T(8,128)(2,1)S(1)} collective-permute-done((bf16[15,29,256]{2,0,1:T(8,128)(2,1)S(1)}, bf16[15,29,256]{2,0,1:T(8,128)(2,1)S(1)}, u32[]{:S(2)}, u32[]{:S(2)}) %collective-permute-start.2) | collective-permute-done | bytes 222752 | tf_op jit(solution)/shard_map/cond/branch_1_fun/ppermute | solution.py:35
  212.5 40.6 %all_to_all.46.incoming_ref = bf16[736,8,256]{2,1,0:T(8,128)(2,1)S(1)} all-to-all(bf16[736,8,256]{2,1,0:T(8,128)(2,1)S(1)} %get-tuple-element.327), channel_id=1, replica_groups={{0,1,2,3,8,9,10,11,16,17,18,19,24,25,26,27},{4,5,6,7,12,13,14,15,20,21,..., dimensions={0} | all-to-all | bytes 6029312 | tf_op jit(solution)/shard_map/cond/branch_1_fun/all_to_all | solution.py:429
  260.2 29.3 %collective-permute-done.5.others_ref = bf16[172,8,256]{2,1,0:T(8,128)(2,1)S(1)} collective-permute-done((bf16[172,8,256]{2,1,0:T(8,128)(2,1)S(1)}, bf16[172,8,256]{2,1,0:T(8,128)(2,1)S(1)}, u32[]{:S(2)}, u32[]{:S(2)}) %collective-permute-start.5) | collective-permute-done | bytes 704544 | tf_op jit(solution)/shard_map/cond/branch_1_fun/ppermute | solution.py:35
  289.5 3.2 couple.5.refs_0_
  292.8 39.0 %all_to_all.47.answers_ref = bf16[736,8,256]{2,1,0:T(8,128)(2,1)S(1)} all-to-all(bf16[736,8,256]{2,1,0:T(8,128)(2,1)S(1)} %couple.5.refs_0_), channel_id=1, replica_groups={{0,1,2,3,8,9,10,11,16,17,18,19,24,25,26,27},{4,5,6,7,12,13,14,15,20,21,..., dimensions={0} | all-to-all | bytes 6029312 | tf_op jit(solution)/shard_map/cond/branch_1_fun/all_to_all | solution.py:429
  331.8 3.4 apply.5.total_ref
  338.6 10.9 %collective-permute-done.7 = bf16[15,29,256]{2,0,1:T(8,128)(2,1)S(1)} collective-permute-done((bf16[15,29,256]{2,0,1:T(8,128)(2,1)S(1)}, bf16[15,29,256]{2,0,1:T(8,128)(2,1)S(1)}, u32[]{:S(2)}, u32[]{:S(2)}) %collective-permute-start.7) | collective-permute-done | bytes 222752 | tf_op jit(solution)/shard_map/cond/branch_1_fun/ppermute | solution.py:35
  359.0 40.4 %all_to_all.48.incoming_ref = bf16[736,8,256]{2,1,0:T(8,128)(2,1)S(1)} all-to-all(bf16[736,8,256]{2,1,0:T(8,128)(2,1)S(1)} %get-tuple-element.331), channel_id=1, replica_groups={{0,1,2,3,8,9,10,11,16,17,18,19,24,25,26,27},{4,5,6,7,12,13,14,15,20,21,..., dimensions={0} | all-to-all | bytes 6029312 | tf_op jit(solution)/shard_map/cond/branch_1_fun/all_to_all | solution.py:429
  406.3 29.6 %collective-permute-done.10.others_ref = bf16[172,8,256]{2,1,0:T(8,128)(2,1)S(1)} collective-permute-done((bf16[172,8,256]{2,1,0:T(8,128)(2,1)S(1)}, bf16[172,8,256]{2,1,0:T(8,128)(2,1)S(1)}, u32[]{:S(2)}, u32[]{:S(2)}) %collective-permute-start.10) | collective-permute-done | bytes 704544 | tf_op jit(solution)/shard_map/cond/branch_1_fun/ppermute | solution.py:35
  435.9 3.2 couple.6.refs_0_
  439.1 39.0 %all_to_all.49.answers_ref = bf16[736,8,256]{2,1,0:T(8,128)(2,1)S(1)} all-to-all(bf16[736,8,256]{2,1,0:T(8,128)(2,1)S(1)} %couple.6.refs_0_), channel_id=1, replica_groups={{0,1,2,3,8,9,10,11,16,17,18,19,24,25,26,27},{4,5,6,7,12,13,14,15,20,21,..., dimensions={0} | all-to-all | bytes 6029312 | tf_op jit(solution)/shard_map/cond/branch_1_fun/all_to_all | solution.py:429
  478.1 3.4 apply.6.total_ref
  484.8 11.0 %collective-permute-done.12 = bf16[15,29,256]{2,0,1:T(8,128)(2,1)S(1)} collective-permute-done((bf16[15,29,256]{2,0,1:T(8,128)(2,1)S(1)}, bf16[15,29,256]{2,0,1:T(8,128)(2,1)S(1)}, u32[]{:S(2)}, u32[]{:S(2)}) %collective-permute-start.12) | collective-permute-done | bytes 222752 | tf_op jit(solution)/shard_map/cond/branch_1_fun/ppermute | solution.py:35
  (177 shorter events, 106.1 us)
Async XLA Ops:
  0.7 22.5 %collective-permute-start.29 = (bf16[29,256]{1,0:T(8,128)(2,1)S(1)}, bf16[29,256]{1,0:T(8,128)(2,1)S(1)}, u32[]{:S(2)}, u32[]{:S(2)}) collective-permute-start(bf16[29,256]{1,0:T(8,128)(2,1)S(1)} %slice_bitcast_fusion.34), channel_id=1, source_target_pairs={{0,31},{1,24},{2,25},{3,26},{4,27},{5,28},{6,29},{7,30},{8,7},{9,0... | collective-permute-start | bytes 44552 | tf_op jit(solution)/shard_map/ppermute | solution.py:35
  9.2 14.1 %all-to-all-start.8 = ((s32[32,1,160]{2,1,0:T(1,128)}), s32[32,1,160]{2,1,0:T(1,128)S(1)}, u32[]{:S(2)}, u32[]{:S(2)}) async-start(s32[32,1,160]{2,1,0:T(1,128)} %broadcast_in_dim.107), calls=%async_computation.8 | async-start | bytes 65536 | tf_op jit(solution)/shard_map/all_to_all | solution.py:441
  13.1 19.6 %collective-permute-start.20 = (f32[256,128]{1,0:T(8,128)S(1)}, f32[256,128]{1,0:T(8,128)S(1)}, u32[]{:S(2)}, u32[]{:S(2)}) collective-permute-start(f32[256,128]{1,0:T(8,128)S(1)} %reshape.673), channel_id=1, source_target_pairs={{0,4},{1,5},{2,6},{3,7},{4,0},{5,1},{6,2},{7,3},{8,12},{9,13},{10,... | collective-permute-start | bytes 393224 | tf_op jit(solution)/shard_map/ppermute | solution.py:35
  16.8 19.3 %collective-permute-start.27 = (bf16[14,29,256]{2,1,0:T(8,128)(2,1)S(1)}, bf16[14,29,256]{2,1,0:T(8,128)(2,1)S(1)}, u32[]{:S(2)}, u32[]{:S(2)}) collective-permute-start(bf16[14,29,256]{2,1,0:T(8,128)(2,1)S(1)} %slice_bitcast_fusion.32), channel_id=1, source_target_pairs={{0,7},{1,0},{2,1},{3,2},{4,3},{5,4},{6,5},{7,6},{8,15},{9,8},{10,9... | collective-permute-start | bytes 623624 | tf_op jit(solution)/shard_map/ppermute | solution.py:35
  22.2 21.2 %collective-permute-start.28 = (bf16[7,29,256]{2,0,1:T(8,128)(2,1)}, bf16[7,29,256]{2,0,1:T(8,128)(2,1)S(1)}, u32[]{:S(2)}, u32[]{:S(2)}) collective-permute-start(bf16[7,29,256]{2,0,1:T(8,128)(2,1)} %slice_bitcast_fusion.33), channel_id=1, source_target_pairs={{0,24},{8,0},{16,8},{24,16},{1,25},{9,1},{17,9},{25,17},{2,26},{10... | collective-permute-start | bytes 311816 | tf_op jit(solution)/shard_map/ppermute | solution.py:35
  32.7 5.2 %collective-permute-start.23 = (f32[256,128]{1,0:T(8,128)S(1)}, f32[256,128]{1,0:T(8,128)S(1)}, u32[]{:S(2)}, u32[]{:S(2)}) collective-permute-start(f32[256,128]{1,0:T(8,128)S(1)} %get-tuple-element.415), channel_id=1, source_target_pairs={{0,8},{8,16},{16,24},{24,0},{1,9},{9,17},{17,25},{25,1},{2,10},{10... | collective-permute-start | bytes 393224 | tf_op jit(solution)/shard_map/ppermute | solution.py:35
  32.8 6.4 %collective-permute-start.22 = (f32[256,128]{1,0:T(8,128)S(1)}, f32[256,128]{1,0:T(8,128)S(1)}, u32[]{:S(2)}, u32[]{:S(2)}) collective-permute-start(f32[256,128]{1,0:T(8,128)S(1)} %get-tuple-element.415), channel_id=1, source_target_pairs={{0,16},{8,24},{16,0},{24,8},{1,17},{9,25},{17,1},{25,9},{2,18},{10... | collective-permute-start | bytes 393224 | tf_op jit(solution)/shard_map/ppermute | solution.py:35
  34.1 5.6 %collective-permute-start.21 = (f32[256,128]{1,0:T(8,128)S(1)}, f32[256,128]{1,0:T(8,128)S(1)}, u32[]{:S(2)}, u32[]{:S(2)}) collective-permute-start(f32[256,128]{1,0:T(8,128)S(1)} %get-tuple-element.415), channel_id=1, source_target_pairs={{0,24},{8,0},{16,8},{24,16},{1,25},{9,1},{17,9},{25,17},{2,26},{10... | collective-permute-start | bytes 393224 | tf_op jit(solution)/shard_map/ppermute | solution.py:35
  39.8 6.9 %collective-permute-start.26 = (f32[256,128]{1,0:T(8,128)S(1)}, f32[256,128]{1,0:T(8,128)S(1)}, u32[]{:S(2)}, u32[]{:S(2)}) collective-permute-start(f32[256,128]{1,0:T(8,128)S(1)} %select_select_fusion.1), channel_id=1, source_target_pairs={{3,0},{0,1},{1,2},{2,3},{7,4},{4,5},{5,6},{6,7},{11,8},{8,9},{9,10... | collective-permute-start | bytes 393224 | tf_op jit(solution)/shard_map/ppermute | solution.py:540
  39.8 6.9 %collective-permute-start.25 = (f32[256,128]{1,0:T(8,128)S(1)}, f32[256,128]{1,0:T(8,128)S(1)}, u32[]{:S(2)}, u32[]{:S(2)}) collective-permute-start(f32[256,128]{1,0:T(8,128)S(1)} %select_select_fusion.1), channel_id=1, source_target_pairs={{2,0},{3,1},{0,2},{1,3},{6,4},{7,5},{4,6},{5,7},{10,8},{11,9},{8,1... | collective-permute-start | bytes 393224 | tf_op jit(solution)/shard_map/ppermute | solution.py:540
  41.1 8.8 %collective-permute-start.24 = (f32[256,128]{1,0:T(8,128)S(1)}, f32[256,128]{1,0:T(8,128)S(1)}, u32[]{:S(2)}, u32[]{:S(2)}) collective-permute-start(f32[256,128]{1,0:T(8,128)S(1)} %select_select_fusion.1), channel_id=1, source_target_pairs={{1,0},{2,1},{3,2},{0,3},{5,4},{6,5},{7,6},{4,7},{9,8},{10,9},{11,1... | collective-permute-start | bytes 393224 | tf_op jit(solution)/shard_map/ppermute | solution.py:540
  65.3 42.0 %all-to-all-start = ((bf16[736,8,256]{2,1,0:T(8,128)(2,1)}), bf16[736,8,256]{2,1,0:T(8,128)(2,1)S(1)}, u32[]{:S(2)}, u32[]{:S(2)}) async-start(bf16[736,8,256]{2,1,0:T(8,128)(2,1)} %copy-done.7), calls=%async_computation | async-start | bytes 6029312 | tf_op jit(solution)/shard_map/cond/branch_1_fun/all_to_all | solution.py:429
  109.6 33.5 %collective-permute-start = (bf16[172,8,256]{2,1,0:T(8,128)(2,1)S(1)}, bf16[172,8,256]{2,1,0:T(8,128)(2,1)S(1)}, u32[]{:S(2)}, u32[]{:S(2)}) collective-permute-start(bf16[172,8,256]{2,1,0:T(8,128)(2,1)S(1)} %get-tuple-element.321), channel_id=1, source_target_pairs={{0,4},{1,5},{2,6},{3,7},{4,0},{5,1},{6,2},{7,3},{8,12},{9,13},{10,... | collective-permute-start | bytes 2113544 | tf_op jit(solution)/shard_map/cond/branch_1_fun/ppermute | solution.py:35
  190.0 13.1 %collective-permute-start.2 = (bf16[15,29,256]{2,0,1:T(8,128)(2,1)S(1)}, bf16[15,29,256]{2,0,1:T(8,128)(2,1)S(1)}, u32[]{:S(2)}, u32[]{:S(2)}) collective-permute-start(bf16[15,29,256]{2,0,1:T(8,128)(2,1)S(1)} %get-tuple-element.400), channel_id=1, source_target_pairs={{0,7},{1,0},{2,1},{3,2},{4,3},{5,4},{6,5},{7,6},{8,15},{9,8},{10,9... | collective-permute-start | bytes 668168 | tf_op jit(solution)/shard_map/cond/branch_1_fun/ppermute | solution.py:35
  192.5 10.5 %collective-permute-start.1 = (bf16[15,29,256]{2,0,1:T(8,128)(2,1)S(1)}, bf16[15,29,256]{2,0,1:T(8,128)(2,1)S(1)}, u32[]{:S(2)}, u32[]{:S(2)}) collective-permute-start(bf16[15,29,256]{2,0,1:T(8,128)(2,1)S(1)} %get-tuple-element.401), channel_id=1, source_target_pairs={{0,1},{1,2},{2,3},{3,4},{4,5},{5,6},{6,7},{7,0},{8,9},{9,10},{10,1... | collective-permute-start | bytes 668168 | tf_op jit(solution)/shard_map/cond/branch_1_fun/ppermute | solution.py:35
  203.5 4.6 collective-permute-start.3
  255.3 34.2 %collective-permute-start.5 = (bf16[172,8,256]{2,1,0:T(8,128)(2,1)S(1)}, bf16[172,8,256]{2,1,0:T(8,128)(2,1)S(1)}, u32[]{:S(2)}, u32[]{:S(2)}) collective-permute-start(bf16[172,8,256]{2,1,0:T(8,128)(2,1)S(1)} %get-tuple-element.329), channel_id=1, source_target_pairs={{0,4},{1,5},{2,6},{3,7},{4,0},{5,1},{6,2},{7,3},{8,12},{9,13},{10,... | collective-permute-start | bytes 2113544 | tf_op jit(solution)/shard_map/cond/branch_1_fun/ppermute | solution.py:35
  336.3 13.2 %collective-permute-start.7 = (bf16[15,29,256]{2,0,1:T(8,128)(2,1)S(1)}, bf16[15,29,256]{2,0,1:T(8,128)(2,1)S(1)}, u32[]{:S(2)}, u32[]{:S(2)}) collective-permute-start(bf16[15,29,256]{2,0,1:T(8,128)(2,1)S(1)} %get-tuple-element.398), channel_id=1, source_target_pairs={{0,7},{1,0},{2,1},{3,2},{4,3},{5,4},{6,5},{7,6},{8,15},{9,8},{10,9... | collective-permute-start | bytes 668168 | tf_op jit(solution)/shard_map/cond/branch_1_fun/ppermute | solution.py:35
  338.5 11.0 %collective-permute-start.6 = (bf16[15,29,256]{2,0,1:T(8,128)(2,1)S(1)}, bf16[15,29,256]{2,0,1:T(8,128)(2,1)S(1)}, u32[]{:S(2)}, u32[]{:S(2)}) collective-permute-start(bf16[15,29,256]{2,0,1:T(8,128)(2,1)S(1)} %get-tuple-element.399), channel_id=1, source_target_pairs={{0,1},{1,2},{2,3},{3,4},{4,5},{5,6},{6,7},{7,0},{8,9},{9,10},{10,1... | collective-permute-start | bytes 668168 | tf_op jit(solution)/shard_map/cond/branch_1_fun/ppermute | solution.py:35
  349.9 4.6 collective-permute-start.8
  401.7 34.2 %collective-permute-start.10 = (bf16[172,8,256]{2,1,0:T(8,128)(2,1)S(1)}, bf16[172,8,256]{2,1,0:T(8,128)(2,1)S(1)}, u32[]{:S(2)}, u32[]{:S(2)}) collective-permute-start(bf16[172,8,256]{2,1,0:T(8,128)(2,1)S(1)} %get-tuple-element.333), channel_id=1, source_target_pairs={{0,4},{1,5},{2,6},{3,7},{4,0},{5,1},{6,2},{7,3},{8,12},{9,13},{10,... | collective-permute-start | bytes 2113544 | tf_op jit(solution)/shard_map/cond/branch_1_fun/ppermute | solution.py:35
  482.6 13.2 %collective-permute-start.12 = (bf16[15,29,256]{2,0,1:T(8,128)(2,1)S(1)}, bf16[15,29,256]{2,0,1:T(8,128)(2,1)S(1)}, u32[]{:S(2)}, u32[]{:S(2)}) collective-permute-start(bf16[15,29,256]{2,0,1:T(8,128)(2,1)S(1)} %get-tuple-element.396), channel_id=1, source_target_pairs={{0,7},{1,0},{2,1},{3,2},{4,3},{5,4},{6,5},{7,6},{8,15},{9,8},{10,9... | collective-permute-start | bytes 668168 | tf_op jit(solution)/shard_map/cond/branch_1_fun/ppermute | solution.py:35
  484.6 11.2 %collective-permute-start.11 = (bf16[15,29,256]{2,0,1:T(8,128)(2,1)S(1)}, bf16[15,29,256]{2,0,1:T(8,128)(2,1)S(1)}, u32[]{:S(2)}, u32[]{:S(2)}) collective-permute-start(bf16[15,29,256]{2,0,1:T(8,128)(2,1)S(1)} %get-tuple-element.397), channel_id=1, source_target_pairs={{0,1},{1,2},{2,3},{3,4},{4,5},{5,6},{6,7},{7,0},{8,9},{9,10},{10,1... | collective-permute-start | bytes 668168 | tf_op jit(solution)/shard_map/cond/branch_1_fun/ppermute | solution.py:35
  496.2 5.1 collective-permute-start.13
  (13 other events, 95.4 us)

commit v8 on v7

--- a/solution.py
+++ b/solution.py
@@ -273,7 +273,7 @@
             kept_ref[pl.ds(g * GROUP * units, GROUP * units)] = mixed
             return carry
 
-        lax.fori_loop(0, groups, mix, 0, unroll=2)
+        lax.fori_loop(0, groups, mix, 0, unroll=4)
 
         def sender(g, carry):
             def copy(j, carry):
@@ -383,11 +383,9 @@
     )(scale, total, *sides, *ends, *known)
 
 
-def completed(total, scale, older):
-    low_v = total[:, :, 0].astype(BF16)
-    high_v = total[:, :, -1].astype(BF16)
-    next_v = shifted(low_v, ("gy",), (-1,))
-    prev_v = shifted(high_v, ("gy",), (1,))
+def completed(total, scale, older, final):
+    prev_v = shifted(total[:, :, -1].astype(BF16), ("gy",), (1,))
+    next_v = prev_v if final else shifted(total[:, :, 0].astype(BF16), ("gy",), (-1,))
 
     def edge(u):
         row = total[u]
@@ -395,8 +393,8 @@
         last = row[:, -1:] + next_v[u][:, None].astype(F32)
         return jnp.concatenate([first, row[:, 1:-1], last], axis=1).astype(BF16)
 
-    next_u = shifted(edge(0), ("gx",), (-1,))
     prev_u = shifted(edge(-1), ("gx",), (1,))
+    next_u = prev_u if final else shifted(edge(0), ("gx",), (-1,))
     return finish(total, (prev_v, next_v), (prev_u, next_u), scale, older)
 
 
@@ -563,7 +561,7 @@
     grid = jnp.transpose(widened, (0, 2, 1, 3)).astype(F32)
     extended = grid.shape[:3]
 
-    def advance(field, older, scale, known, cap, span):
+    def advance(field, older, scale, known, cap, span, final=False):
         room = senders * cap
         starts = own * cap + offsets
         begins = (places_in + jnp.arange(senders)[:, None] * cap).reshape(slots)
@@ -597,14 +595,15 @@
             )
             after = (totals[-1],)
         total = jnp.concatenate(totals, axis=-1) if PARTS > 1 else totals[0]
-        return completed(total, scale, older), (straight, stiff, turned, *mixing)
+        return completed(total, scale, older, final), (straight, stiff, turned, *mixing)
 
     def packed():
         known = None
         older, field = None, grid
         for step in range(FILTER_DEGREE):
             scale = jnp.full((1,), 1.0 if step == 0 else 2.0, F32)
-            image, known = advance(field, older, scale, known, cap, span)
+            final = step == FILTER_DEGREE - 1
+            image, known = advance(field, older, scale, known, cap, span, final)
             older, field = field, image
         return field[:span_x, :, :span_y].astype(BF16)
 

time: 509 us -> 504 us (level)
    ppermute x22 -> x20, waiting for transfers between devices: 124 us -> 123 us  [shifted(): return lax.ppermute(x, axes if len(axes) > 1 else axes[0], pairs)]
    ppermute x22 -> x20, starting transfers between devices: 29.2 us -> 27.7 us  [shifted(): return lax.ppermute(x, axes if len(axes) > 1 else axes[0], pairs)]
  transfers between devices with their start and end apart: 27 -> 25, of which waited for: 18 -> 17; matrix products, arithmetic and copies ran while one was open for 4% -> 4% of each run, Pallas kernels for 4% -> 4%
where the time goes in v8:
time: 504 us; the launch traced here: 503 us
  blocking collectives  198 us (39%)
  waiting for transfers between devices  165 us (33%)
  Pallas kernels  66.2 us (13%)
  starting transfers between devices  37.7 us (7%)
  local copies, waits for them, and re-layouts  20.5 us (4%)
  other arithmetic  10.2 us (2%)
    all_to_all x5, blocking collectives, exchange(): lax.all_to_all(x, both, split_axis=0, concat_axis=0, axis_index_groups=te...  198 us
    ppermute x20, waiting for transfers between devices, shifted(): return lax.ppermute(x, axes if len(axes) > 1 else axes[0], pairs)  123 us
    all_to_all x1, waiting for transfers between devices, exchange(): lax.all_to_all(x, both, split_axis=0, concat_axis=0, axis_index_groups=te...  38.1 us
    ppermute x20, starting transfers between devices, shifted(): return lax.ppermute(x, axes if len(axes) > 1 else axes[0], pairs)  27.7 us
    pallas_call x3, Pallas kernels, project(): pl.pallas_call(body, grid=(cells,), in_specs=[smem(), whole(field.shape),...  15.8 us
    pallas_call x3, Pallas kernels, apply(): pl.pallas_call(body, grid=(cells,), in_specs=[smem(), smem(), pl.BlockSpe...  10.1 us
  transfers between devices with their start and end apart: 25, of which 17 were waited for; matrix products, arithmetic and copies ran while one was open for 4% of the time, Pallas kernels for 4%

profile of v8, /device:TPU:0, one launch (start us, length us, event | category | flops | bytes accessed | tf_op | source)
XLA Modules:
  0.0 502.9 jit_solution(10375068583619289529)
XLA Ops:
  0.7 6.4 %collective-permute-start.27 = (bf16[29,256]{1,0:T(8,128)(2,1)S(1)}, bf16[29,256]{1,0:T(8,128)(2,1)S(1)}, u32[]{:S(2)}, u32[]{:S(2)}) collective-permute-start(bf16[29,256]{1,0:T(8,128)(2,1)S(1)} %slice_bitcast_fusion.28), channel_id=1, source_target_pairs={{0,31},{1,24},{2,25},{3,26},{4,27},{5,28},{6,29},{7,30},{8,7},{9,0... | collective-permute-start | bytes 44552 | tf_op jit(solution)/shard_map/ppermute | solution.py:35
  46.7 3.2 collective-permute-done.22
  50.6 448.6 %conditional.2 = (f32[15,29,8,256]{3,2,1,0:T(8,128)}) conditional(s32[]{:T(128)} %convert_element_type.350, (s32[128]{0:T(128)S(1)}, s32[128]{0:T(128)S(1)}, bf16[8,512,512]{2,1,0:T(8,128)(2,1)}, s32[8,1,512]{2,1,0:T(1,128)S(1)}, bf16[8,512,512]{2,1,0:T(8,128)(2,1)}, /*index=5*/s32[16,16]{1,0:T(8,128)S(1)}, s32[256]{0:T(256)S(1)}, ...), branch_computations={%region_13.16_spmd, %region_16.17_spmd} | conditional | flops 1997584 | bytes 153846624
  50.8 9.6 %project.8 = (bf16[8,512,512]{2,1,0:T(8,128)(2,1)S(1)}, bf16[8,512,256]{2,1,0:T(8,128)(2,1)S(1)}, bf16[736,8,256]{2,1,0:T(8,128)(2,1)S(1)}) custom-call(s32[128]{0:T(128)S(1)} %multiply_add_fusion.1.starts_ref, f32[15,29,8,256]{3,2,1,0:T(8,128)} %get-tuple-element.311.field_ref.refs_0_, bf16[8,512,512]{2,1,0:T(8,128)(2,1)} %get-tuple-element.310.straight_ref.shape_ref, ...), custom_call_target="tpu_custom_call" | custom-call | tf_op jit(solution)/shard_map/cond/branch_1_fun/project/pallas_call | solution.py:156
  65.4 3.7 all-to-all-start
  69.3 38.1 %all-to-all-done.incoming_ref = bf16[736,8,256]{2,1,0:T(8,128)(2,1)S(1)} async-done(((bf16[736,8,256]{2,1,0:T(8,128)(2,1)}), bf16[736,8,256]{2,1,0:T(8,128)(2,1)S(1)}, u32[]{:S(2)}, u32[]{:S(2)}) %all-to-all-start) | async-done | bytes 3014688 | tf_op jit(solution)/shard_map/cond/branch_1_fun/all_to_all | solution.py:427
  111.5 9.9 %canonical.6 = (bf16[8,512,512]{2,1,0:T(8,128)(2,1)S(1)}, bf16[8,512,512]{2,1,0:T(8,128)(2,1)S(1)}) custom-call(s32[8,1,512]{2,1,0:T(1,128)S(1)} %get-tuple-element.308.refs_0_.place_ref, bf16[8,512,512]{2,1,0:T(8,128)(2,1)} %get-tuple-element.309.matrix_ref, bf16[8,512,512]{2,1,0:T(8,128)(2,1)} %get-tuple-element.310.straight_ref.shape_ref, ...), custom_call_target="tpu_custom_call" | custom-call | tf_op jit(solution)/shard_map/cond/branch_1_fun/canonical/pallas_call | solution.py:73
  125.6 17.5 %collective-permute-done.others_ref = bf16[172,8,256]{2,1,0:T(8,128)(2,1)S(1)} collective-permute-done((bf16[172,8,256]{2,1,0:T(8,128)(2,1)S(1)}, bf16[172,8,256]{2,1,0:T(8,128)(2,1)S(1)}, u32[]{:S(2)}, u32[]{:S(2)}) %collective-permute-start) | collective-permute-done | bytes 704544 | tf_op jit(solution)/shard_map/cond/branch_1_fun/ppermute | solution.py:35
  146.0 39.2 %all_to_all.45.answers_ref = bf16[736,8,256]{2,1,0:T(8,128)(2,1)S(1)} all-to-all(bf16[736,8,256]{2,1,0:T(8,128)(2,1)S(1)} %couple.4.refs_0_), channel_id=1, replica_groups={{0,1,2,3,8,9,10,11,16,17,18,19,24,25,26,27},{4,5,6,7,12,13,14,15,20,21,..., dimensions={0} | all-to-all | bytes 6029312 | tf_op jit(solution)/shard_map/cond/branch_1_fun/all_to_all | solution.py:427
  185.2 3.4 apply.4.total_ref
  192.3 10.4 %collective-permute-done.2 = bf16[15,29,256]{2,0,1:T(8,128)(2,1)S(1)} collective-permute-done((bf16[15,29,256]{2,0,1:T(8,128)(2,1)S(1)}, bf16[15,29,256]{2,0,1:T(8,128)(2,1)S(1)}, u32[]{:S(2)}, u32[]{:S(2)}) %collective-permute-start.2) | collective-permute-done | bytes 222752 | tf_op jit(solution)/shard_map/cond/branch_1_fun/ppermute | solution.py:35
  209.1 3.1 project.9
  212.2 40.6 %all_to_all.46.incoming_ref = bf16[736,8,256]{2,1,0:T(8,128)(2,1)S(1)} all-to-all(bf16[736,8,256]{2,1,0:T(8,128)(2,1)S(1)} %get-tuple-element.327), channel_id=1, replica_groups={{0,1,2,3,8,9,10,11,16,17,18,19,24,25,26,27},{4,5,6,7,12,13,14,15,20,21,..., dimensions={0} | all-to-all | bytes 6029312 | tf_op jit(solution)/shard_map/cond/branch_1_fun/all_to_all | solution.py:427
  259.9 29.3 %collective-permute-done.5.others_ref = bf16[172,8,256]{2,1,0:T(8,128)(2,1)S(1)} collective-permute-done((bf16[172,8,256]{2,1,0:T(8,128)(2,1)S(1)}, bf16[172,8,256]{2,1,0:T(8,128)(2,1)S(1)}, u32[]{:S(2)}, u32[]{:S(2)}) %collective-permute-start.5) | collective-permute-done | bytes 704544 | tf_op jit(solution)/shard_map/cond/branch_1_fun/ppermute | solution.py:35
  292.1 39.0 %all_to_all.47.answers_ref = bf16[736,8,256]{2,1,0:T(8,128)(2,1)S(1)} all-to-all(bf16[736,8,256]{2,1,0:T(8,128)(2,1)S(1)} %couple.5.refs_0_), channel_id=1, replica_groups={{0,1,2,3,8,9,10,11,16,17,18,19,24,25,26,27},{4,5,6,7,12,13,14,15,20,21,..., dimensions={0} | all-to-all | bytes 6029312 | tf_op jit(solution)/shard_map/cond/branch_1_fun/all_to_all | solution.py:427
  331.1 3.4 apply.5.total_ref
  337.9 10.9 %collective-permute-done.7 = bf16[15,29,256]{2,0,1:T(8,128)(2,1)S(1)} collective-permute-done((bf16[15,29,256]{2,0,1:T(8,128)(2,1)S(1)}, bf16[15,29,256]{2,0,1:T(8,128)(2,1)S(1)}, u32[]{:S(2)}, u32[]{:S(2)}) %collective-permute-start.7) | collective-permute-done | bytes 222752 | tf_op jit(solution)/shard_map/cond/branch_1_fun/ppermute | solution.py:35
  355.2 3.1 project.10
  358.3 40.4 %all_to_all.48.incoming_ref = bf16[736,8,256]{2,1,0:T(8,128)(2,1)S(1)} all-to-all(bf16[736,8,256]{2,1,0:T(8,128)(2,1)S(1)} %get-tuple-element.331), channel_id=1, replica_groups={{0,1,2,3,8,9,10,11,16,17,18,19,24,25,26,27},{4,5,6,7,12,13,14,15,20,21,..., dimensions={0} | all-to-all | bytes 6029312 | tf_op jit(solution)/shard_map/cond/branch_1_fun/all_to_all | solution.py:427
  405.6 29.5 %collective-permute-done.10.others_ref = bf16[172,8,256]{2,1,0:T(8,128)(2,1)S(1)} collective-permute-done((bf16[172,8,256]{2,1,0:T(8,128)(2,1)S(1)}, bf16[172,8,256]{2,1,0:T(8,128)(2,1)S(1)}, u32[]{:S(2)}, u32[]{:S(2)}) %collective-permute-start.10) | collective-permute-done | bytes 704544 | tf_op jit(solution)/shard_map/cond/branch_1_fun/ppermute | solution.py:35
  438.0 39.0 %all_to_all.49.answers_ref = bf16[736,8,256]{2,1,0:T(8,128)(2,1)S(1)} all-to-all(bf16[736,8,256]{2,1,0:T(8,128)(2,1)S(1)} %couple.6.refs_0_), channel_id=1, replica_groups={{0,1,2,3,8,9,10,11,16,17,18,19,24,25,26,27},{4,5,6,7,12,13,14,15,20,21,..., dimensions={0} | all-to-all | bytes 6029312 | tf_op jit(solution)/shard_map/cond/branch_1_fun/all_to_all | solution.py:427
  477.1 3.4 apply.6.total_ref
  482.0 9.6 %collective-permute-done.11 = bf16[15,29,256]{2,0,1:T(8,128)(2,1)S(1)} collective-permute-done((bf16[15,29,256]{2,0,1:T(8,128)(2,1)S(1)}, bf16[15,29,256]{2,0,1:T(8,128)(2,1)S(1)}, u32[]{:S(2)}, u32[]{:S(2)}) %collective-permute-start.11) | collective-permute-done | bytes 222752 | tf_op jit(solution)/shard_map/cond/branch_1_fun/ppermute | solution.py:35
  492.0 4.2 collective-permute-done.12.prev_u_ref.next_u_ref
  (170 shorter events, 101.7 us)
Async XLA Ops:
  0.7 22.5 %collective-permute-start.27 = (bf16[29,256]{1,0:T(8,128)(2,1)S(1)}, bf16[29,256]{1,0:T(8,128)(2,1)S(1)}, u32[]{:S(2)}, u32[]{:S(2)}) collective-permute-start(bf16[29,256]{1,0:T(8,128)(2,1)S(1)} %slice_bitcast_fusion.28), channel_id=1, source_target_pairs={{0,31},{1,24},{2,25},{3,26},{4,27},{5,28},{6,29},{7,30},{8,7},{9,0... | collective-permute-start | bytes 44552 | tf_op jit(solution)/shard_map/ppermute | solution.py:35
  9.2 14.1 %all-to-all-start.8 = ((s32[32,1,160]{2,1,0:T(1,128)}), s32[32,1,160]{2,1,0:T(1,128)S(1)}, u32[]{:S(2)}, u32[]{:S(2)}) async-start(s32[32,1,160]{2,1,0:T(1,128)} %broadcast_in_dim.107), calls=%async_computation.8 | async-start | bytes 65536 | tf_op jit(solution)/shard_map/all_to_all | solution.py:439
  13.1 19.6 %collective-permute-start.18 = (f32[256,128]{1,0:T(8,128)S(1)}, f32[256,128]{1,0:T(8,128)S(1)}, u32[]{:S(2)}, u32[]{:S(2)}) collective-permute-start(f32[256,128]{1,0:T(8,128)S(1)} %reshape.630), channel_id=1, source_target_pairs={{0,4},{1,5},{2,6},{3,7},{4,0},{5,1},{6,2},{7,3},{8,12},{9,13},{10,... | collective-permute-start | bytes 393224 | tf_op jit(solution)/shard_map/ppermute | solution.py:35
  16.8 19.3 %collective-permute-start.25 = (bf16[14,29,256]{2,1,0:T(8,128)(2,1)S(1)}, bf16[14,29,256]{2,1,0:T(8,128)(2,1)S(1)}, u32[]{:S(2)}, u32[]{:S(2)}) collective-permute-start(bf16[14,29,256]{2,1,0:T(8,128)(2,1)S(1)} %slice_bitcast_fusion.26), channel_id=1, source_target_pairs={{0,7},{1,0},{2,1},{3,2},{4,3},{5,4},{6,5},{7,6},{8,15},{9,8},{10,9... | collective-permute-start | bytes 623624 | tf_op jit(solution)/shard_map/ppermute | solution.py:35
  22.2 21.2 %collective-permute-start.26 = (bf16[7,29,256]{2,0,1:T(8,128)(2,1)}, bf16[7,29,256]{2,0,1:T(8,128)(2,1)S(1)}, u32[]{:S(2)}, u32[]{:S(2)}) collective-permute-start(bf16[7,29,256]{2,0,1:T(8,128)(2,1)} %slice_bitcast_fusion.27), channel_id=1, source_target_pairs={{0,24},{8,0},{16,8},{24,16},{1,25},{9,1},{17,9},{25,17},{2,26},{10... | collective-permute-start | bytes 311816 | tf_op jit(solution)/shard_map/ppermute | solution.py:35
  32.8 5.2 %collective-permute-start.21 = (f32[256,128]{1,0:T(8,128)S(1)}, f32[256,128]{1,0:T(8,128)S(1)}, u32[]{:S(2)}, u32[]{:S(2)}) collective-permute-start(f32[256,128]{1,0:T(8,128)S(1)} %get-tuple-element.409), channel_id=1, source_target_pairs={{0,8},{8,16},{16,24},{24,0},{1,9},{9,17},{17,25},{25,1},{2,10},{10... | collective-permute-start | bytes 393224 | tf_op jit(solution)/shard_map/ppermute | solution.py:35
  32.8 6.4 %collective-permute-start.20 = (f32[256,128]{1,0:T(8,128)S(1)}, f32[256,128]{1,0:T(8,128)S(1)}, u32[]{:S(2)}, u32[]{:S(2)}) collective-permute-start(f32[256,128]{1,0:T(8,128)S(1)} %get-tuple-element.409), channel_id=1, source_target_pairs={{0,16},{8,24},{16,0},{24,8},{1,17},{9,25},{17,1},{25,9},{2,18},{10... | collective-permute-start | bytes 393224 | tf_op jit(solution)/shard_map/ppermute | solution.py:35
  34.2 5.6 %collective-permute-start.19 = (f32[256,128]{1,0:T(8,128)S(1)}, f32[256,128]{1,0:T(8,128)S(1)}, u32[]{:S(2)}, u32[]{:S(2)}) collective-permute-start(f32[256,128]{1,0:T(8,128)S(1)} %get-tuple-element.409), channel_id=1, source_target_pairs={{0,24},{8,0},{16,8},{24,16},{1,25},{9,1},{17,9},{25,17},{2,26},{10... | collective-permute-start | bytes 393224 | tf_op jit(solution)/shard_map/ppermute | solution.py:35
  39.8 6.9 %collective-permute-start.24 = (f32[256,128]{1,0:T(8,128)S(1)}, f32[256,128]{1,0:T(8,128)S(1)}, u32[]{:S(2)}, u32[]{:S(2)}) collective-permute-start(f32[256,128]{1,0:T(8,128)S(1)} %select_select_fusion.1), channel_id=1, source_target_pairs={{3,0},{0,1},{1,2},{2,3},{7,4},{4,5},{5,6},{6,7},{11,8},{8,9},{9,10... | collective-permute-start | bytes 393224 | tf_op jit(solution)/shard_map/ppermute | solution.py:538
  39.9 6.9 %collective-permute-start.23 = (f32[256,128]{1,0:T(8,128)S(1)}, f32[256,128]{1,0:T(8,128)S(1)}, u32[]{:S(2)}, u32[]{:S(2)}) collective-permute-start(f32[256,128]{1,0:T(8,128)S(1)} %select_select_fusion.1), channel_id=1, source_target_pairs={{2,0},{3,1},{0,2},{1,3},{6,4},{7,5},{4,6},{5,7},{10,8},{11,9},{8,1... | collective-permute-start | bytes 393224 | tf_op jit(solution)/shard_map/ppermute | solution.py:538
  41.1 8.8 %collective-permute-start.22 = (f32[256,128]{1,0:T(8,128)S(1)}, f32[256,128]{1,0:T(8,128)S(1)}, u32[]{:S(2)}, u32[]{:S(2)}) collective-permute-start(f32[256,128]{1,0:T(8,128)S(1)} %select_select_fusion.1), channel_id=1, source_target_pairs={{1,0},{2,1},{3,2},{0,3},{5,4},{6,5},{7,6},{4,7},{9,8},{10,9},{11,1... | collective-permute-start | bytes 393224 | tf_op jit(solution)/shard_map/ppermute | solution.py:538
  65.4 42.0 %all-to-all-start = ((bf16[736,8,256]{2,1,0:T(8,128)(2,1)}), bf16[736,8,256]{2,1,0:T(8,128)(2,1)S(1)}, u32[]{:S(2)}, u32[]{:S(2)}) async-start(bf16[736,8,256]{2,1,0:T(8,128)(2,1)} %copy-done.7), calls=%async_computation | async-start | bytes 6029312 | tf_op jit(solution)/shard_map/cond/branch_1_fun/all_to_all | solution.py:427
  109.7 33.5 %collective-permute-start = (bf16[172,8,256]{2,1,0:T(8,128)(2,1)S(1)}, bf16[172,8,256]{2,1,0:T(8,128)(2,1)S(1)}, u32[]{:S(2)}, u32[]{:S(2)}) collective-permute-start(bf16[172,8,256]{2,1,0:T(8,128)(2,1)S(1)} %get-tuple-element.321), channel_id=1, source_target_pairs={{0,4},{1,5},{2,6},{3,7},{4,0},{5,1},{6,2},{7,3},{8,12},{9,13},{10,... | collective-permute-start | bytes 2113544 | tf_op jit(solution)/shard_map/cond/branch_1_fun/ppermute | solution.py:35
  189.7 13.1 %collective-permute-start.2 = (bf16[15,29,256]{2,0,1:T(8,128)(2,1)S(1)}, bf16[15,29,256]{2,0,1:T(8,128)(2,1)S(1)}, u32[]{:S(2)}, u32[]{:S(2)}) collective-permute-start(bf16[15,29,256]{2,0,1:T(8,128)(2,1)S(1)} %get-tuple-element.396), channel_id=1, source_target_pairs={{0,7},{1,0},{2,1},{3,2},{4,3},{5,4},{6,5},{7,6},{8,15},{9,8},{10,9... | collective-permute-start | bytes 668168 | tf_op jit(solution)/shard_map/cond/branch_1_fun/ppermute | solution.py:35
  192.2 10.5 %collective-permute-start.1 = (bf16[15,29,256]{2,0,1:T(8,128)(2,1)S(1)}, bf16[15,29,256]{2,0,1:T(8,128)(2,1)S(1)}, u32[]{:S(2)}, u32[]{:S(2)}) collective-permute-start(bf16[15,29,256]{2,0,1:T(8,128)(2,1)S(1)} %get-tuple-element.397), channel_id=1, source_target_pairs={{0,1},{1,2},{2,3},{3,4},{4,5},{5,6},{6,7},{7,0},{8,9},{9,10},{10,1... | collective-permute-start | bytes 668168 | tf_op jit(solution)/shard_map/cond/branch_1_fun/ppermute | solution.py:35
  203.2 4.6 collective-permute-start.3
  255.0 34.2 %collective-permute-start.5 = (bf16[172,8,256]{2,1,0:T(8,128)(2,1)S(1)}, bf16[172,8,256]{2,1,0:T(8,128)(2,1)S(1)}, u32[]{:S(2)}, u32[]{:S(2)}) collective-permute-start(bf16[172,8,256]{2,1,0:T(8,128)(2,1)S(1)} %get-tuple-element.329), channel_id=1, source_target_pairs={{0,4},{1,5},{2,6},{3,7},{4,0},{5,1},{6,2},{7,3},{8,12},{9,13},{10,... | collective-permute-start | bytes 2113544 | tf_op jit(solution)/shard_map/cond/branch_1_fun/ppermute | solution.py:35
  335.6 13.2 %collective-permute-start.7 = (bf16[15,29,256]{2,0,1:T(8,128)(2,1)S(1)}, bf16[15,29,256]{2,0,1:T(8,128)(2,1)S(1)}, u32[]{:S(2)}, u32[]{:S(2)}) collective-permute-start(bf16[15,29,256]{2,0,1:T(8,128)(2,1)S(1)} %get-tuple-element.394), channel_id=1, source_target_pairs={{0,7},{1,0},{2,1},{3,2},{4,3},{5,4},{6,5},{7,6},{8,15},{9,8},{10,9... | collective-permute-start | bytes 668168 | tf_op jit(solution)/shard_map/cond/branch_1_fun/ppermute | solution.py:35
  337.8 11.0 %collective-permute-start.6 = (bf16[15,29,256]{2,0,1:T(8,128)(2,1)S(1)}, bf16[15,29,256]{2,0,1:T(8,128)(2,1)S(1)}, u32[]{:S(2)}, u32[]{:S(2)}) collective-permute-start(bf16[15,29,256]{2,0,1:T(8,128)(2,1)S(1)} %get-tuple-element.395), channel_id=1, source_target_pairs={{0,1},{1,2},{2,3},{3,4},{4,5},{5,6},{6,7},{7,0},{8,9},{9,10},{10,1... | collective-permute-start | bytes 668168 | tf_op jit(solution)/shard_map/cond/branch_1_fun/ppermute | solution.py:35
  349.0 3.5 collective-permute-start.9
  349.2 4.6 collective-permute-start.8
  401.0 34.2 %collective-permute-start.10 = (bf16[172,8,256]{2,1,0:T(8,128)(2,1)S(1)}, bf16[172,8,256]{2,1,0:T(8,128)(2,1)S(1)}, u32[]{:S(2)}, u32[]{:S(2)}) collective-permute-start(bf16[172,8,256]{2,1,0:T(8,128)(2,1)S(1)} %get-tuple-element.333), channel_id=1, source_target_pairs={{0,4},{1,5},{2,6},{3,7},{4,0},{5,1},{6,2},{7,3},{8,12},{9,13},{10,... | collective-permute-start | bytes 2113544 | tf_op jit(solution)/shard_map/cond/branch_1_fun/ppermute | solution.py:35
  480.9 10.8 %collective-permute-start.11 = (bf16[15,29,256]{2,0,1:T(8,128)(2,1)S(1)}, bf16[15,29,256]{2,0,1:T(8,128)(2,1)S(1)}, u32[]{:S(2)}, u32[]{:S(2)}) collective-permute-start(bf16[15,29,256]{2,0,1:T(8,128)(2,1)S(1)} %bitcast.262), channel_id=1, source_target_pairs={{0,1},{1,2},{2,3},{3,4},{4,5},{5,6},{6,7},{7,0},{8,9},{9,10},{10,1... | collective-permute-start | bytes 668168 | tf_op jit(solution)/shard_map/cond/branch_1_fun/ppermute | solution.py:35
  491.8 4.3 collective-permute-start.12
  (11 other events, 89.0 us)
